TPU v7x, 32 devices: a whole 2x2x4 slice. The times are simulated.
32 devices in a mesh: dp: 8 (over z, core), mp: 4 (over y, x).
Axes of the slice: x: 2, y: 2, z: 4, core: 2. Of those that a mesh axis runs over, the one named last changes fastest.
Arguments:
- x_in: bfloat16 [8, 1024, 2048], P('dp'), may hold values from -6 to 6
- lengths: int32 [8], P('dp'), may hold values from 512 to 1024, as said below
- gain_attn: bfloat16 [2048], P('dp'), may hold values from 0.5 to 1.5
- query_weight: bfloat16 [2048, 2048], P('dp', 'mp'), may hold values from -0.125 to 0.125
- key_projection_matrix: bfloat16 [2048, 4, 256], P('dp', None, 'mp'), may hold values from -0.125 to 0.125
- value_projection_matrix: bfloat16 [2048, 4, 256], P('dp', None, 'mp'), may hold values from -0.125 to 0.125
- out_weight: bfloat16 [2048, 2048], P('mp', 'dp'), may hold values from -0.75 to 0.75
- gain_ffn: bfloat16 [2048], P('dp'), may hold values from 0.5 to 1.5
- gate_weight: bfloat16 [2048, 8192], P('dp', 'mp'), may hold values from -0.125 to 0.125
- up_weight: bfloat16 [2048, 8192], P('dp', 'mp'), may hold values from -0.125 to 0.125
- down_weight: bfloat16 [8192, 2048], P('mp', 'dp'), may hold values from -0.0625 to 0.0625
- cotangent: bfloat16 [8, 1024, 2048], P('dp'), may hold values from -6 to 6
Outputs:
- layer_out: bfloat16 [8, 1024, 2048], P('dp')
- grad_input: float32 [8, 1024, 2048], P('dp')
- gain_attn_grad: float32 [2048], P('dp')
- query_grad: float32 [2048, 2048], P('dp', 'mp')
- key_projection_grad: float32 [2048, 4, 256], P('dp', None, 'mp')
- value_projection_grad: float32 [2048, 4, 256], P('dp', None, 'mp')
- out_grad: float32 [2048, 2048], P('mp', 'dp')
- gain_ffn_grad: float32 [2048], P('dp')
- gate_grad: float32 [2048, 8192], P('dp', 'mp')
- up_grad: float32 [2048, 8192], P('dp', 'mp')
- down_grad: float32 [8192, 2048], P('mp', 'dp')
Inputs may be any that keep to these rules, and one draw needn't show every extreme that they name: A sequence's valid slots are its first lengths positions; in every draw some sequence fills all 1024 slots.
All inputs are finite; a program needn't handle non-finite values.
Results may differ from a plain program's by a relative error of at most 0.014.
Values may be sent and summed in bfloat16 or wider, within the bound.
No kernel may reach another device: no remote copies, remote signals or barrier semaphores. Data moves between devices by JAX's collectives and lax.ppermute only.
A program may use at most 256 MiB of HBM per device.

v0:
```python
import jax
import jax.numpy as jnp
from jax import lax
from jax.sharding import PartitionSpec as P

QUERY_HEADS = 8
KEY_VALUE_HEADS = 4
HEAD_SIZE = 256


eps_norm = 1e-06
rope_base = 1000042.0
neg_large = -1e30
exact = lax.Precision.HIGHEST


def rope_tables(slot_length, size):
    half_size = size // 2
    inv_freq = rope_base ** (-(jnp.arange(half_size, dtype=jnp.float32) * 2.0 / size))
    angles = jnp.arange(slot_length, dtype=jnp.float32)[:, None] * inv_freq[None, :]
    return (jnp.cos(angles), jnp.sin(angles))


def apply_rotation(values, cosine_lookup, sine_lookup):
    half_size = values.shape[-1] // 2
    first_half = values[..., :half_size]
    second_half = values[..., half_size:]
    cos_b = cosine_lookup[:, None, :]
    sin_b = sine_lookup[:, None, :]
    return jnp.concatenate(
        [first_half * cos_b - second_half * sin_b, second_half * cos_b + first_half * sin_b],
        axis=-1,
    )


def apply_rotation_back(grads, cosine_lookup, sine_lookup):
    half_size = grads.shape[-1] // 2
    first_half = grads[..., :half_size]
    second_half = grads[..., half_size:]
    cos_b = cosine_lookup[:, None, :]
    sin_b = sine_lookup[:, None, :]
    return jnp.concatenate(
        [first_half * cos_b + second_half * sin_b, second_half * cos_b - first_half * sin_b],
        axis=-1,
    )


def norm_forward(tok_rows):
    factor = lax.rsqrt(jnp.mean(tok_rows * tok_rows, axis=-1, keepdims=True) + eps_norm)
    return (tok_rows * factor, factor)


def norm_backward(normed, factor, grad_h, gain):
    grad_n = grad_h * gain
    gain_grad = jnp.sum(grad_h * normed, axis=0)
    grad_rows = factor * (grad_n - normed * jnp.mean(grad_n * normed, axis=-1, keepdims=True))
    return (grad_rows, gain_grad)


def matrix_multiply(left, right):
    return jnp.dot(left, right, preferred_element_type=jnp.float32)


def product_rows(left, right):
    return lax.dot_general(
        left, right, (((0,), (0,)), ((), ())), preferred_element_type=jnp.float32
    )


def dot_cols(left, right):
    return lax.dot_general(
        left, right, (((1,), (1,)), ((), ())), preferred_element_type=jnp.float32
    )


def scores_block(q_block, keys_reduced, first_row, seq_len, factor):
    raw_scores = jnp.einsum(
        "qhd,khd->hqk", q_block, keys_reduced, preferred_element_type=jnp.float32
    )
    q_pos = first_row + jnp.arange(q_block.shape[0])
    k_pos = jnp.arange(keys_reduced.shape[0])
    allowed = (k_pos[None, :] <= q_pos[:, None]) & (k_pos[None, :] < seq_len)
    return jnp.where(allowed[None], raw_scores * factor, neg_large)


def attend(queries, keys_reduced, values_reduced, seq_len, factor):
    slot_length = queries.shape[0]
    block_rows = min(512, slot_length)
    parts = []
    totals = []
    for first_row in range(0, slot_length, block_rows):
        q_block = queries[first_row : first_row + block_rows]
        scores = scores_block(q_block, keys_reduced, first_row, seq_len, factor)
        row_max = jnp.max(scores, axis=-1, keepdims=True)
        exp_scores = jnp.exp(scores - row_max)
        row_total = jnp.sum(exp_scores, axis=-1, keepdims=True)
        attn_probs = (exp_scores / row_total).astype(jnp.bfloat16)
        parts.append(
            jnp.einsum(
                "hqk,khd->qhd", attn_probs, values_reduced, preferred_element_type=jnp.float32
            ).astype(jnp.bfloat16)
        )
        totals.append((row_max + jnp.log(row_total))[..., 0])
    return (jnp.concatenate(parts, axis=0), jnp.concatenate(totals, axis=1))


def attend_back(queries, keys_reduced, values_reduced, grad_ctx, log_total, seq_len, factor):
    slot_length = queries.shape[0]
    block_rows = min(512, slot_length)
    dq_parts = []
    d_keys = jnp.zeros(keys_reduced.shape, jnp.float32)
    d_values = jnp.zeros(values_reduced.shape, jnp.float32)
    for first_row in range(0, slot_length, block_rows):
        q_block = queries[first_row : first_row + block_rows]
        g_block = grad_ctx[first_row : first_row + block_rows]
        scores = scores_block(q_block, keys_reduced, first_row, seq_len, factor)
        attn_probs = jnp.exp(scores - log_total[:, first_row : first_row + block_rows, None])
        grad_p = jnp.einsum(
            "qhd,khd->hqk", g_block, values_reduced, preferred_element_type=jnp.float32
        )
        inner_sum = jnp.sum(attn_probs * grad_p, axis=-1, keepdims=True)
        grad_s = (attn_probs * (grad_p - inner_sum) * factor).astype(jnp.bfloat16)
        dq_parts.append(
            jnp.einsum("hqk,khd->qhd", grad_s, keys_reduced, preferred_element_type=jnp.float32)
        )
        d_keys = d_keys + jnp.einsum(
            "hqk,qhd->khd", grad_s, q_block, preferred_element_type=jnp.float32
        )
        d_values = d_values + jnp.einsum(
            "hqk,qhd->khd",
            attn_probs.astype(jnp.bfloat16),
            g_block,
            preferred_element_type=jnp.float32,
        )
    return (jnp.concatenate(dq_parts, axis=0), d_keys, d_values)


def local(
    x_in,
    lengths,
    gain_attn,
    query_weight,
    key_projection_matrix,
    value_projection_matrix,
    out_weight,
    gain_ffn,
    gate_weight,
    up_weight,
    down_weight,
    cotangent,
):
    sequences_per_device, slot_length, model_feature_width = x_in.shape
    overall_rows = sequences_per_device * slot_length
    heads_here = query_weight.shape[1] // HEAD_SIZE
    query_group_width = QUERY_HEADS // KEY_VALUE_HEADS
    head_portion = key_projection_matrix.shape[2]
    factor = HEAD_SIZE ** (-0.5)
    first_head = lax.axis_index("mp") * heads_here
    key_value_listing = [(first_head + head_j) // query_group_width for head_j in range(heads_here)]
    cosine_lookup, sine_lookup = rope_tables(slot_length, HEAD_SIZE)
    g_attn, wq_all, key_weight_gathered, value_weight_gathered, wo_all = (
        lax.all_gather(gain_attn, "dp", axis=0, tiled=True),
        lax.all_gather(query_weight, "dp", axis=0, tiled=True),
        lax.all_gather(key_projection_matrix, "dp", axis=0, tiled=True),
        lax.all_gather(value_projection_matrix, "dp", axis=0, tiled=True),
        lax.all_gather(out_weight, "dp", axis=1, tiled=True),
    )
    g_ffn, wg_all, wu_all, wd_all = (
        lax.all_gather(gain_ffn, "dp", axis=0, tiled=True),
        lax.all_gather(gate_weight, "dp", axis=0, tiled=True),
        lax.all_gather(up_weight, "dp", axis=0, tiled=True),
        lax.all_gather(down_weight, "dp", axis=1, tiled=True),
    )
    tok_rows = x_in.reshape(overall_rows, model_feature_width).astype(jnp.float32)
    normed_in, factor_in = norm_forward(tok_rows)
    hidden_attention = (normed_in * g_attn.astype(jnp.float32)).astype(jnp.bfloat16)
    q_lin = matrix_multiply(hidden_attention, wq_all)
    key_linear = matrix_multiply(
        hidden_attention,
        key_weight_gathered.reshape(model_feature_width, KEY_VALUE_HEADS * head_portion),
    ).reshape(overall_rows, KEY_VALUE_HEADS, head_portion)
    value_linear = matrix_multiply(
        hidden_attention,
        value_weight_gathered.reshape(model_feature_width, KEY_VALUE_HEADS * head_portion),
    ).reshape(overall_rows, KEY_VALUE_HEADS, head_portion)
    queries = apply_rotation(
        q_lin.reshape(sequences_per_device, slot_length, heads_here, HEAD_SIZE),
        cosine_lookup,
        sine_lookup,
    ).astype(jnp.bfloat16)
    keys_complete, values_complete = (
        lax.all_gather(key_linear, "mp", axis=2, tiled=True),
        lax.all_gather(value_linear, "mp", axis=2, tiled=True),
    )
    keys_gathered_every = apply_rotation(
        keys_complete.reshape(sequences_per_device, slot_length, KEY_VALUE_HEADS, HEAD_SIZE),
        cosine_lookup,
        sine_lookup,
    ).astype(jnp.bfloat16)
    values_gathered_every = values_complete.reshape(
        sequences_per_device, slot_length, KEY_VALUE_HEADS, HEAD_SIZE
    ).astype(jnp.bfloat16)
    keys_reduced = jnp.concatenate(
        [
            lax.dynamic_index_in_dim(keys_gathered_every, kv_idx, 2, keepdims=True)
            for kv_idx in key_value_listing
        ],
        axis=2,
    )
    values_reduced = jnp.concatenate(
        [
            lax.dynamic_index_in_dim(values_gathered_every, kv_idx, 2, keepdims=True)
            for kv_idx in key_value_listing
        ],
        axis=2,
    )
    seq_i = 0
    ctx_seq, total_seq = attend(
        queries[seq_i], keys_reduced[seq_i], values_reduced[seq_i], lengths[seq_i], factor
    )
    contexts = [ctx_seq]
    log_totals = [total_seq]
    context = jnp.stack(contexts).reshape(overall_rows, heads_here * HEAD_SIZE)
    attn_rows = lax.psum(matrix_multiply(context, wo_all), "mp")
    mid_rows = tok_rows + attn_rows
    normed_mid, factor_mid = norm_forward(mid_rows)
    h_ffn = (normed_mid * g_ffn.astype(jnp.float32)).astype(jnp.bfloat16)
    gate_proj = matrix_multiply(h_ffn, wg_all)
    up_proj = matrix_multiply(h_ffn, wu_all)
    gate_sig = jax.nn.sigmoid(gate_proj)
    hidden = (gate_proj * gate_sig * up_proj).astype(jnp.bfloat16)
    ffn_rows = lax.psum(matrix_multiply(hidden, wd_all).astype(jnp.bfloat16), "mp").astype(
        jnp.float32
    )
    layer_out = (
        (mid_rows + ffn_rows)
        .astype(jnp.bfloat16)
        .reshape(sequences_per_device, slot_length, model_feature_width)
    )
    g_ffn, wg_all, wu_all, wd_all = (
        lax.all_gather(gain_ffn, "dp", axis=0, tiled=True),
        lax.all_gather(gate_weight, "dp", axis=0, tiled=True),
        lax.all_gather(up_weight, "dp", axis=0, tiled=True),
        lax.all_gather(down_weight, "dp", axis=1, tiled=True),
    )
    valid_mask = (jnp.arange(slot_length)[None, :] < lengths[:, None]).astype(jnp.float32)
    grad_o = (cotangent.astype(jnp.float32) * valid_mask[:, :, None]).reshape(
        overall_rows, model_feature_width
    )
    grad_low = grad_o.astype(jnp.bfloat16)
    d_hidden = dot_cols(grad_low, wd_all)
    down_grad = product_rows(hidden, grad_low)
    d_gate = (d_hidden * up_proj * gate_sig * (1.0 + gate_proj * (1.0 - gate_sig))).astype(
        jnp.bfloat16
    )
    d_up = (d_hidden * gate_proj * gate_sig).astype(jnp.bfloat16)
    gate_grad = product_rows(h_ffn, d_gate)
    up_grad = product_rows(h_ffn, d_up)
    d_h2 = lax.psum(dot_cols(d_gate, wg_all) + dot_cols(d_up, wu_all), "mp")
    d_mid, gain_ffn_grad = norm_backward(normed_mid, factor_mid, d_h2, g_ffn.astype(jnp.float32))
    ffn_out = (
        lax.psum_scatter(gain_ffn_grad, "dp", scatter_dimension=0, tiled=True),
        lax.psum_scatter(gate_grad, "dp", scatter_dimension=0, tiled=True),
        lax.psum_scatter(up_grad, "dp", scatter_dimension=0, tiled=True),
        lax.psum_scatter(down_grad, "dp", scatter_dimension=1, tiled=True),
    )
    g_attn, wq_all, key_weight_gathered, value_weight_gathered, wo_all = (
        lax.all_gather(gain_attn, "dp", axis=0, tiled=True),
        lax.all_gather(query_weight, "dp", axis=0, tiled=True),
        lax.all_gather(key_projection_matrix, "dp", axis=0, tiled=True),
        lax.all_gather(value_projection_matrix, "dp", axis=0, tiled=True),
        lax.all_gather(out_weight, "dp", axis=1, tiled=True),
    )
    grad_mid = grad_o + d_mid
    grad_mid_low = grad_mid.astype(jnp.bfloat16)
    out_grad = product_rows(context, grad_mid_low)
    d_context = (
        dot_cols(grad_mid_low, wo_all)
        .astype(jnp.bfloat16)
        .reshape(sequences_per_device, slot_length, heads_here, HEAD_SIZE)
    )
    seq_i = 0
    dq_seq, dk_seq, dv_seq = attend_back(
        queries[seq_i],
        keys_reduced[seq_i],
        values_reduced[seq_i],
        d_context[seq_i],
        log_totals[seq_i],
        lengths[seq_i],
        factor,
    )
    dq_list = [dq_seq]
    dk_list = [dk_seq]
    dv_list = [dv_seq]
    indicator_vector = (
        jnp.stack(key_value_listing)[:, None] == jnp.arange(KEY_VALUE_HEADS)[None, :]
    ).astype(jnp.float32)
    key_grad_every = jnp.einsum(
        "sljd,jh->slhd", jnp.stack(dk_list), indicator_vector, precision=exact
    )
    value_grad_every = jnp.einsum(
        "sljd,jh->slhd", jnp.stack(dv_list), indicator_vector, precision=exact
    )
    key_linear_grad = apply_rotation_back(key_grad_every, cosine_lookup, sine_lookup).reshape(
        overall_rows, KEY_VALUE_HEADS, HEAD_SIZE
    )
    value_linear_grad = value_grad_every.reshape(overall_rows, KEY_VALUE_HEADS, HEAD_SIZE)
    key_grad_portion, value_grad_portion = (
        lax.psum_scatter(
            key_linear_grad.astype(jnp.bfloat16), "mp", scatter_dimension=2, tiled=True
        ).astype(jnp.float32),
        lax.psum_scatter(
            value_linear_grad.astype(jnp.bfloat16), "mp", scatter_dimension=2, tiled=True
        ).astype(jnp.float32),
    )
    gradient_keys = key_grad_portion.reshape(overall_rows, KEY_VALUE_HEADS * head_portion).astype(
        jnp.bfloat16
    )
    gradient_values = value_grad_portion.reshape(
        overall_rows, KEY_VALUE_HEADS * head_portion
    ).astype(jnp.bfloat16)
    grad_q = (
        apply_rotation_back(jnp.stack(dq_list), cosine_lookup, sine_lookup)
        .reshape(overall_rows, heads_here * HEAD_SIZE)
        .astype(jnp.bfloat16)
    )
    query_grad = product_rows(hidden_attention, grad_q)
    key_projection_grad = product_rows(hidden_attention, gradient_keys).reshape(
        model_feature_width, KEY_VALUE_HEADS, head_portion
    )
    value_projection_grad = product_rows(hidden_attention, gradient_values).reshape(
        model_feature_width, KEY_VALUE_HEADS, head_portion
    )
    key_weight_flattened = key_weight_gathered.reshape(
        model_feature_width, KEY_VALUE_HEADS * head_portion
    )
    value_weight_flattened = value_weight_gathered.reshape(
        model_feature_width, KEY_VALUE_HEADS * head_portion
    )
    d_h1 = lax.psum(
        dot_cols(grad_q, wq_all)
        + dot_cols(gradient_keys, key_weight_flattened)
        + dot_cols(gradient_values, value_weight_flattened),
        "mp",
    )
    d_in, gain_attn_grad = norm_backward(normed_in, factor_in, d_h1, g_attn.astype(jnp.float32))
    grad_input = (grad_mid + d_in).reshape(sequences_per_device, slot_length, model_feature_width)
    attn_out = (
        lax.psum_scatter(gain_attn_grad, "dp", scatter_dimension=0, tiled=True),
        lax.psum_scatter(query_grad, "dp", scatter_dimension=0, tiled=True),
        lax.psum_scatter(key_projection_grad, "dp", scatter_dimension=0, tiled=True),
        lax.psum_scatter(value_projection_grad, "dp", scatter_dimension=0, tiled=True),
        lax.psum_scatter(out_grad, "dp", scatter_dimension=1, tiled=True),
    )
    return (
        layer_out,
        grad_input,
        attn_out[0],
        attn_out[1],
        attn_out[2],
        attn_out[3],
        attn_out[4],
        ffn_out[0],
        ffn_out[1],
        ffn_out[2],
        ffn_out[3],
    )


def solution(mesh):
    return jax.shard_map(
        local,
        mesh=mesh,
        in_specs=(
            P("dp", None, None),
            P("dp"),
            P("dp"),
            P("dp", "mp"),
            P("dp", None, "mp"),
            P("dp", None, "mp"),
            P("mp", "dp"),
            P("dp"),
            P("dp", "mp"),
            P("dp", "mp"),
            P("mp", "dp"),
            P("dp", None, None),
        ),
        out_specs=(
            P("dp", None, None),
            P("dp", None, None),
            P("dp"),
            P("dp", "mp"),
            P("dp", None, "mp"),
            P("dp", None, "mp"),
            P("mp", "dp"),
            P("dp"),
            P("dp", "mp"),
            P("dp", "mp"),
            P("mp", "dp"),
        ),
        check_vma=False,
    )
```

profile of v0, /device:TPU:0, one launch (start us, length us, event | category | flops | bytes accessed | tf_op | source)
XLA Modules:
  0.0 1990.7 jit_solution(2483262229292576084)
XLA Ops:
  10.1 13.4 all-gather
  41.0 19.5 all-gather.18.cloned.1.call-done
  70.1 19.7 all-gather.16.cloned.1.call-done
  98.1 28.9 %all-gather.14.cloned.1.call-done = bf16[1024,4,256]{0,2,1:T(8,128)(2,1)} async-done(((bf16[1024,4,64]{0,2,1:T(8,128)(2,1)}), bf16[1024,4,256]{0,2,1:T(8,128)(2,1)}) %all-gather.14.cloned.1.call-update) | async-done | bytes 2097168 | tf_op jit(solution)/shard_map/all_gather | solution.py:193
  128.3 53.7 %all-gather.20.cloned.1.call-done = f32[1024,4,256]{0,2,1:T(8,128)} async-done(((f32[1024,4,64]{0,2,1:T(8,128)}), f32[1024,4,256]{0,2,1:T(8,128)}) %all-gather.20.cloned.1.call-update) | async-done | bytes 4194320 | tf_op jit(solution)/shard_map/all_gather | solution.py:192
  193.2 21.1 %all-gather.22.cloned.1.call-done = bf16[512,2048]{1,0:T(8,128)(2,1)} async-done(((bf16[512,256]{1,0:T(8,128)(2,1)}), bf16[512,2048]{1,0:T(8,128)(2,1)}) %all-gather.22.cloned.1.call-update) | async-done | bytes 2097168 | tf_op jit(solution)/shard_map/all_gather | solution.py:166
  223.8 12.1 all-gather.1
  236.0 157.0 %all-reduce.10.cloned.1.call-done = f32[1024,2048]{1,0:T(8,128)} async-done(((f32[1024,2048]{1,0:T(8,128)}), f32[1024,2048]{1,0:T(8,128)}) %all-reduce.10.cloned.1.call-update) | async-done | bytes 8388624 | tf_op jit(solution)/shard_map/psum | solution.py:224
  405.0 72.5 %all-gather.26.cloned.1.call-done = bf16[2048,2048]{1,0:T(8,128)(2,1)} async-done(((bf16[256,2048]{1,0:T(8,128)(2,1)}), bf16[2048,2048]{1,0:T(8,128)(2,1)}) %all-gather.26.cloned.1.call-update) | async-done | bytes 8388624 | tf_op jit(solution)/shard_map/all_gather | solution.py:171
  477.5 14.4 fusion.147
  491.9 67.9 %all-gather.24.cloned.1.call-done = bf16[2048,2048]{1,0:T(8,128)(2,1)} async-done(((bf16[256,2048]{1,0:T(8,128)(2,1)}), bf16[2048,2048]{1,0:T(8,128)(2,1)}) %all-gather.24.cloned.1.call-update) | async-done | bytes 8388624 | tf_op jit(solution)/shard_map/all_gather | solution.py:170
  559.8 14.4 fusion.146
  574.2 68.2 %all-gather.28.cloned.1.call-done = bf16[2048,2048]{1,0:T(8,128)(2,1)} async-done(((bf16[2048,256]{1,0:T(8,128)(2,1)}), bf16[2048,2048]{1,0:T(8,128)(2,1)}) %all-gather.28.cloned.1.call-update) | async-done | bytes 8388624 | tf_op jit(solution)/shard_map/all_gather | solution.py:172
  642.4 21.8 %multiply_convert_fusion = (bf16[1024,2048]{1,0:T(8,128)(2,1)}, bf16[1024,2048]{1,0:T(8,128)(2,1)}, bf16[1024,2048]{1,0:T(8,128)(2,1)}) fusion(f32[1024,2048]{1,0:T(8,128)} %fusion.146, f32[1024,2048]{1,0:T(8,128)} %fusion.147, bf16[2048,2048]{1,0:T(8,128)(2,1)} %all-gather.28.cloned.1.call-done, bf16[1,1024,2048]{2,1,0:T(8,128)(2,1)} %param.23, ...), kind=kOutput, calls=%fused_computation.25 | convolution fusion | flops 8629780480 | bytes 41947136 | tf_op jit(solution)/shard_map/dot_general | solution.py:71
  664.2 12.9 fusion.148
  677.0 13.5 convolution_add_fusion
  690.7 170.3 %all-reduce.12.cloned.1.call-done = f32[1024,2048]{1,0:T(8,128)} async-done(((f32[1024,2048]{1,0:T(8,128)}), f32[1024,2048]{1,0:T(8,128)}) %all-reduce.12.cloned.1.call-update) | async-done | bytes 8388624 | tf_op jit(solution)/shard_map/psum | solution.py:259
  887.1 12.7 fusion.41
  899.8 13.3 add_bitcast_fusion.1
  932.9 14.0 convolution_convert_fusion
  1001.2 111.0 %all-reduce.16.cloned.1.call-done = (bf16[1024,2048]{1,0:T(8,128)(2,1)}, bf16[1024,4,256]{0,1,2:T(4,128)(2,1)}) async-done(((bf16[1024,2048]{1,0:T(8,128)(2,1)}, bf16[1024,4,256]{0,1,2:T(4,128)(2,1)}), (bf16[1024,2048]{1,0:T(8,128)(2,1)}, bf16[1024,4,256]{0,1,2:T(4,128)(2,1)})) %all-reduce.16.cloned.1.call-update) | async-done | bytes 6291472 | tf_op jit(solution)/shard_map/psum | solution.py:232
  1149.9 15.7 fusion.78
  1166.0 15.4 fusion.152
  1181.4 15.9 fusion.151
  1207.6 88.5 %all-reduce.14.cloned.1.call-done = f32[1024,2048]{1,0:T(8,128)} async-done(((f32[1024,2048]{1,0:T(8,128)}), f32[1024,2048]{1,0:T(8,128)}) %all-reduce.14.cloned.1.call-update) | async-done | bytes 8388624 | tf_op jit(solution)/shard_map/psum | solution.py:340
  1301.9 28.9 %all-reduce.3 = (f32[2048]{0:T(1024)S(1)}, f32[2048]{0:T(1024)S(1)}) all-reduce(f32[2048]{0:T(1024)S(1)} %get-tuple-element.13, f32[2048]{0:T(1024)S(1)} %copy-done.30), channel_id=4, replica_groups=mesh['dp'=8,'mp'=4] {'dp'}, use_global_device_ids=true, to_apply=%region_17.18.clone | all-reduce | flops 4096 | bytes 32768
  1343.8 43.1 %reduce-scatter.17.cloned.1.call-done = f32[512,256]{1,0:T(8,128)} async-done(((f32[512,2048]{1,0:T(8,128)}), f32[512,256]{1,0:T(8,128)}) %reduce-scatter.17.cloned.1.call-update) | async-done | bytes 524304 | tf_op jit(solution)/shard_map/reduce_scatter | solution.py:353
  1387.0 50.9 %reduce-scatter.11.cloned.1.call-done = f32[256,512]{1,0:T(8,128)} async-done(((f32[2048,512]{1,0:T(8,128)}), f32[256,512]{1,0:T(8,128)}) %reduce-scatter.11.cloned.1.call-update) | async-done | bytes 524304 | tf_op jit(solution)/shard_map/reduce_scatter | solution.py:350
  1437.9 36.7 %reduce-scatter.15.cloned.1.call-done = f32[256,4,64]{0,2,1:T(8,128)} async-done(((f32[2048,4,64]{0,2,1:T(8,128)}), f32[256,4,64]{0,2,1:T(8,128)}) %reduce-scatter.15.cloned.1.call-update) | async-done | bytes 262160 | tf_op jit(solution)/shard_map/reduce_scatter | solution.py:352
  1474.5 169.9 %reduce-scatter.23.cloned.1.call-done = f32[2048,256]{1,0:T(8,128)} async-done(((f32[2048,2048]{1,0:T(8,128)}), f32[2048,256]{1,0:T(8,128)}) %reduce-scatter.23.cloned.1.call-update) | async-done | bytes 2097168 | tf_op jit(solution)/shard_map/reduce_scatter | solution.py:265
  1644.4 169.4 %reduce-scatter.21.cloned.1.call-done = f32[256,2048]{1,0:T(8,128)} async-done(((f32[2048,2048]{1,0:T(8,128)}), f32[256,2048]{1,0:T(8,128)}) %reduce-scatter.21.cloned.1.call-update) | async-done | bytes 2097168 | tf_op jit(solution)/shard_map/reduce_scatter | solution.py:264
  1813.9 169.6 %reduce-scatter.19.cloned.1.call-done = f32[256,2048]{1,0:T(8,128)} async-done(((f32[2048,2048]{1,0:T(8,128)}), f32[256,2048]{1,0:T(8,128)}) %reduce-scatter.19.cloned.1.call-update) | async-done | bytes 2097168 | tf_op jit(solution)/shard_map/reduce_scatter | solution.py:263
  (187 shorter events, 237.1 us)
Async XLA Ops:
  7.2 29.1 %all-gather.12.cloned.1.call-start = ((), (), s32[]{:S(2)}) async-start(), calls=%async_computation.8 | async-start | bytes 1179648 | tf_op jit(solution)/shard_map/all_gather | solution.py:165
  7.9 52.6 %all-gather.18.cloned.1.call-start = ((), (), s32[]{:S(2)}) async-start(), calls=%async_computation.11 | async-start | bytes 1179648 | tf_op jit(solution)/shard_map/all_gather | solution.py:164
  8.7 81.2 %all-gather.16.cloned.1.call-start = ((), (), s32[]{:S(2)}) async-start(), calls=%async_computation.10 | async-start | bytes 2359296 | tf_op jit(solution)/shard_map/all_gather | solution.py:163
  9.4 117.6 %all-gather.14.cloned.1.call-start = ((), (), s32[]{:S(2)}) async-start(), calls=%async_computation.9 | async-start | bytes 2621440 | tf_op jit(solution)/shard_map/all_gather | solution.py:193
  23.5 69.5 %copy-start.26 = (f32[8,1,256]{2,1,0:T(1,128)}, f32[8,1,256]{2,1,0:T(1,128)S(1)}, u32[]{:S(2)}) copy-start(f32[8,1,256]{2,1,0:T(1,128)S(1)} %convert_element_type.215) | copy-start | bytes 24580
  26.6 66.4 %copy-start.28 = (f32[1024]{0:T(1024)}, f32[1024]{0:T(1024)S(1)}, u32[]{:S(2)}) copy-start(f32[1024]{0:T(1024)S(1)} %add_rsqrt_fusion.1) | copy-start | bytes 12292
  41.0 141.0 %all-gather.20.cloned.1.call-start = ((), (), s32[]{:S(2)}) async-start(), calls=%async_computation.12 | async-start | bytes 5242880 | tf_op jit(solution)/shard_map/all_gather | solution.py:192
  65.4 148.9 %all-gather.22.cloned.1.call-start = ((), (), s32[]{:S(2)}) async-start(), calls=%async_computation.13 | async-start | bytes 2359296 | tf_op jit(solution)/shard_map/all_gather | solution.py:166
  65.9 327.1 %all-reduce.10.cloned.1.call-start = ((), (), s32[]{:S(2)}) async-start(), calls=%async_computation.14 | async-start | bytes 16777216 | tf_op jit(solution)/shard_map/psum | solution.py:224
  68.6 113.4 %copy-start.7 = (f32[1024,128]{0,1:T(8,128)}, f32[1024,128]{0,1:T(8,128)S(1)}, u32[]{:S(2)}) copy-start(f32[1024,128]{0,1:T(8,128)S(1)} %get-tuple-element.40) | copy-start | bytes 1572868
  68.6 113.4 %copy-start.9 = (f32[1024,128]{0,1:T(8,128)}, f32[1024,128]{0,1:T(8,128)S(1)}, u32[]{:S(2)}) copy-start(f32[1024,128]{0,1:T(8,128)S(1)} %get-tuple-element.41) | copy-start | bytes 1572868
  98.1 89.4 %copy-start.22 = (bf16[1,1024,2,128]{1,3,2,0:T(8,128)(2,1)}, bf16[1,1024,2,128]{1,3,2,0:T(8,128)(2,1)S(1)}, u32[]{:S(2)}) copy-start(bf16[1,1024,2,128]{1,3,2,0:T(8,128)(2,1)S(1)} %get-tuple-element.30) | copy-start | bytes 1572868
  98.1 89.4 %copy-start.24 = (bf16[1,1024,2,128]{1,3,2,0:T(8,128)(2,1)}, bf16[1,1024,2,128]{1,3,2,0:T(8,128)(2,1)S(1)}, u32[]{:S(2)}) copy-start(bf16[1,1024,2,128]{1,3,2,0:T(8,128)(2,1)S(1)} %get-tuple-element.31) | copy-start | bytes 1572868
  193.2 28.5 %copy-start.14 = (bf16[1024,2,256]{0,2,1:T(8,128)(2,1)}, bf16[1024,2,256]{0,2,1:T(8,128)(2,1)S(1)}, u32[]{:S(2)}) copy-start(bf16[1024,2,256]{0,2,1:T(8,128)(2,1)S(1)} %pad_maximum_fusion) | copy-start | bytes 3145732
  221.7 255.8 %all-gather.26.cloned.1.call-start = ((), (), s32[]{:S(2)}) async-start(), calls=%async_computation.16 | async-start | bytes 9437184 | tf_op jit(solution)/shard_map/all_gather | solution.py:171
  222.5 337.3 %all-gather.24.cloned.1.call-start = ((), (), s32[]{:S(2)}) async-start(), calls=%async_computation.15 | async-start | bytes 9437184 | tf_op jit(solution)/shard_map/all_gather | solution.py:170
  223.2 419.2 %all-gather.28.cloned.1.call-start = ((), (), s32[]{:S(2)}) async-start(), calls=%async_computation.17 | async-start | bytes 9437184 | tf_op jit(solution)/shard_map/all_gather | solution.py:172
  223.8 637.2 %all-reduce.12.cloned.1.call-start = ((), (), s32[]{:S(2)}) async-start(), calls=%async_computation.18 | async-start | bytes 16777216 | tf_op jit(solution)/shard_map/psum | solution.py:259
  664.2 12.9 copy-start.34
  690.6 304.4 %reduce-scatter.9.cloned.1.call-start = ((), (), s32[]{:S(2)}) async-start(), calls=%async_computation.19 | async-start | bytes 2621440 | tf_op jit(solution)/shard_map/reduce_scatter | solution.py:309
  932.8 179.4 %all-reduce.16.cloned.1.call-start = ((), (), s32[]{:S(2)}) async-start(), calls=%async_computation.28 | async-start | bytes 12582912 | tf_op jit(solution)/shard_map/psum | solution.py:232
  932.9 14.0 copy-start.4
  966.2 329.9 %all-reduce.14.cloned.1.call-start = ((), (), s32[]{:S(2)}) async-start(), calls=%async_computation.20 | async-start | bytes 16777216 | tf_op jit(solution)/shard_map/psum | solution.py:340
  994.9 118.5 %copy-start.13 = (bf16[2048,4,64]{0,2,1:T(8,128)(2,1)S(1)}, bf16[2048,4,64]{0,2,1:T(8,128)(2,1)}, u32[]{:S(2)}) copy-start(bf16[2048,4,64]{0,2,1:T(8,128)(2,1)} %all-gather.12.cloned.1.call-done) | copy-start | bytes 3145732
  1123.8 220.0 %reduce-scatter.13.cloned.1.call-start = ((), (), s32[]{:S(2)}) async-start(), calls=%async_computation.22 | async-start | bytes 2359296 | tf_op jit(solution)/shard_map/reduce_scatter | solution.py:351
  1129.6 257.4 %reduce-scatter.17.cloned.1.call-start = ((), (), s32[]{:S(2)}) async-start(), calls=%async_computation.24 | async-start | bytes 4718592 | tf_op jit(solution)/shard_map/reduce_scatter | solution.py:353
  1137.6 300.3 %reduce-scatter.11.cloned.1.call-start = ((), (), s32[]{:S(2)}) async-start(), calls=%async_computation.21 | async-start | bytes 4718592 | tf_op jit(solution)/shard_map/reduce_scatter | solution.py:350
  1144.7 329.8 %reduce-scatter.15.cloned.1.call-start = ((), (), s32[]{:S(2)}) async-start(), calls=%async_computation.23 | async-start | bytes 2359296 | tf_op jit(solution)/shard_map/reduce_scatter | solution.py:352
  1149.9 494.6 %reduce-scatter.23.cloned.1.call-start = ((), (), s32[]{:S(2)}) async-start(), calls=%async_computation.27 | async-start | bytes 18874368 | tf_op jit(solution)/shard_map/reduce_scatter | solution.py:265
  1165.7 648.2 %reduce-scatter.21.cloned.1.call-start = ((), (), s32[]{:S(2)}) async-start(), calls=%async_computation.26 | async-start | bytes 18874368 | tf_op jit(solution)/shard_map/reduce_scatter | solution.py:264
  1181.4 802.1 %reduce-scatter.19.cloned.1.call-start = ((), (), s32[]{:S(2)}) async-start(), calls=%async_computation.25 | async-start | bytes 18874368 | tf_op jit(solution)/shard_map/reduce_scatter | solution.py:263
  1207.6 94.3 %copy-start.30 = (f32[2048]{0:T(1024)S(1)}, f32[2048]{0:T(1024)}, u32[]{:S(2)}) copy-start(f32[2048]{0:T(1024)} %get-tuple-element.11) | copy-start | bytes 24580
  (24 other events, 77.6 us)
Sparse Core Ops, SparseCore 0:
  9.6 26.6 all-gather.11
  37.9 22.5 all-gather.17
  62.1 27.6 all-gather.15
  92.1 34.7 all-gather.13
  129.3 52.6 all-gather.19
  183.4 30.8 all-gather.21
  221.8 171.1 all-reduce.9
  394.7 82.7 all-gather.25
  479.2 80.5 all-gather.23
  561.3 81.0 all-gather.27
  690.7 170.2 all-reduce.11
  932.9 35.8 reduce-scatter.8
  973.4 138.7 all-reduce.15
  1123.9 172.1 all-reduce.13
  1298.8 36.5 reduce-scatter.12
  1338.1 48.8 reduce-scatter.16
  1389.7 48.1 reduce-scatter.10
  1440.6 33.8 reduce-scatter.14
  1477.5 166.9 reduce-scatter.22
  1647.2 166.6 reduce-scatter.20
  1816.8 166.5 reduce-scatter.18
where the time goes:
time: 2000 us; the launch traced here: 1990 us
  waiting for transfers between devices  1530 us (76%)
  matrix products  285 us (14%)
  other arithmetic  65.5 us (3%)
  blocking collectives  54.4 us (3%)
  local copies, waits for them, and re-layouts  34.9 us (2%)
    psum x1, waiting for transfers between devices, local(): d_h2 = lax.psum(dot_cols(d_gate, wg_all) + dot_cols(d_up, wu_all), 'mp')  170 us
    reduce_scatter x1, waiting for transfers between devices, local(): lax.psum_scatter(down_grad, 'dp', scatter_dimension=1, tiled=True)  170 us
    reduce_scatter x1, waiting for transfers between devices, local(): lax.psum_scatter(gate_grad, 'dp', scatter_dimension=0, tiled=True)  170 us
    reduce_scatter x1, waiting for transfers between devices, local(): lax.psum_scatter(up_grad, 'dp', scatter_dimension=0, tiled=True)  169 us
    psum x1, waiting for transfers between devices, local(): attn_rows = lax.psum(matrix_multiply(context, wo_all), 'mp')  157 us
    psum x1, waiting for transfers between devices, local(): lax.psum(matrix_multiply(hidden, wd_all).astype(jnp.bfloat16), 'mp')  111 us
    psum x1, waiting for transfers between devices, local(): lax.psum(dot_cols(grad_q, wq_all) + dot_cols(gradient_keys, key_weight_fl...  88.5 us
    dot_general x7, matrix products, dot_cols(): lax.dot_general(left, right, (((1,), (1,)), ((), ())), preferred_element_...  75.9 us
  transfers between devices with their start and end apart: 21, of which 19 were waited for; matrix products, arithmetic and copies ran while one was open for 12% of the time, Pallas kernels for 0%

commit v1 on v0

v1 whole, which is shorter than its diff:
```python
import jax
import jax.numpy as jnp
from jax import lax
from jax.sharding import PartitionSpec as P

QUERY_HEADS = 8
KEY_VALUE_HEADS = 4
HEAD_SIZE = 256

eps_norm = 1e-06
rope_base = 1000042.0
neg_large = -1e30
bf16 = jnp.bfloat16
f32 = jnp.float32


def rope_tables(slot_length, size):
    half_size = size // 2
    inv_freq = rope_base ** (-(jnp.arange(half_size, dtype=f32) * 2.0 / size))
    angles = jnp.arange(slot_length, dtype=f32)[:, None] * inv_freq[None, :]
    return (jnp.cos(angles), jnp.sin(angles))


def rotate(values, cos_b, sin_b):
    half = values.shape[-1] // 2
    a, b = values[..., :half], values[..., half:]
    return jnp.concatenate([a * cos_b - b * sin_b, b * cos_b + a * sin_b], axis=-1)


def rotate_back(grads, cos_b, sin_b):
    half = grads.shape[-1] // 2
    a, b = grads[..., :half], grads[..., half:]
    return jnp.concatenate([a * cos_b + b * sin_b, b * cos_b - a * sin_b], axis=-1)


def mm(left, right):
    return lax.dot_general(left, right, (((1,), (0,)), ((), ())), preferred_element_type=f32)


def mm_t(left, right):
    return lax.dot_general(left, right, (((1,), (1,)), ((), ())), preferred_element_type=f32)


def mm_rows(left, right):
    return lax.dot_general(left, right, (((0,), (0,)), ((), ())), preferred_element_type=f32)


OVER_X = [(0, 1), (1, 0), (2, 3), (3, 2)]
OVER_Y = [(0, 2), (2, 0), (1, 3), (3, 1)]


def pick(blocks, which):
    return lax.dynamic_index_in_dim(blocks, which, 0, keepdims=False)


def scatter_rows(product, lefts, width):
    mp_size = lax.axis_size("mp")
    rows = lefts[0].shape[0]
    here = rows // mp_size
    if mp_size != 4:
        part = jnp.concatenate([product(lefts, 0), product(lefts, 1)], axis=1).astype(bf16)
        return lax.psum_scatter(part, "mp", scatter_dimension=0, tiled=True).astype(f32)
    me = lax.axis_index("mp")
    x, y = me % 2, me // 2
    half = width // 2

    def rows_x(which):
        return [
            lax.dynamic_index_in_dim(v.reshape(2, 2, here, v.shape[1]), which, 1, keepdims=False).reshape(
                2 * here, v.shape[1]
            )
            for v in lefts
        ]

    def rows_y(which):
        return [
            lax.dynamic_index_in_dim(v.reshape(2, 2 * here, v.shape[1]), which, 0, keepdims=False)
            for v in lefts
        ]

    away_a = lax.ppermute(product(rows_x(1 - x), 0).astype(bf16), "mp", OVER_X)
    away_b = lax.ppermute(product(rows_y(1 - y), 1).astype(bf16), "mp", OVER_Y)
    sum_a = (product(rows_x(x), 0) + away_a.astype(f32)).reshape(2, here, half)
    sum_b = (product(rows_y(y), 1) + away_b.astype(f32)).reshape(2, here, half)
    last_a = lax.ppermute(pick(sum_a, 1 - y).astype(bf16), "mp", OVER_Y)
    last_b = lax.ppermute(pick(sum_b, 1 - x).astype(bf16), "mp", OVER_X)
    return jnp.concatenate(
        [pick(sum_a, y) + last_a.astype(f32), pick(sum_b, x) + last_b.astype(f32)], axis=1
    )


def gather_rows(block):
    mp_size = lax.axis_size("mp")
    if mp_size != 4:
        return lax.all_gather(block, "mp", axis=0, tiled=True)
    me = lax.axis_index("mp")
    x, y = me % 2, me // 2
    here, width = block.shape
    half = width // 2
    own_a, own_b = block[:, :half], block[:, half:]

    def both(own, other, low):
        return jnp.where(low, own, other), jnp.where(low, other, own)

    got_a = lax.ppermute(own_a, "mp", OVER_Y)
    got_b = lax.ppermute(own_b, "mp", OVER_X)
    pair_a = jnp.stack(both(own_a, got_a, y == 0))
    pair_b = jnp.stack(both(own_b, got_b, x == 0))
    far_a = lax.ppermute(pair_a, "mp", OVER_X)
    far_b = lax.ppermute(pair_b, "mp", OVER_Y)
    all_a = jnp.stack(both(pair_a, far_a, x == 0), axis=1)
    all_b = jnp.stack(both(pair_b, far_b, y == 0), axis=0)
    return jnp.concatenate(
        [all_a.reshape(4 * here, half), all_b.reshape(4 * here, half)], axis=1
    )


def mask_block(first_row, block_rows, slots, seq_len):
    q_pos = first_row + jnp.arange(block_rows)
    k_pos = jnp.arange(slots)
    return (k_pos[None, :] <= q_pos[:, None]) & (k_pos[None, :] < seq_len)


def attend(queries, keys, values, seq_len, factor):
    slots = keys.shape[0]
    block_rows = min(512, slots)
    parts, totals = [], []
    for first_row in range(0, slots, block_rows):
        upto = first_row + block_rows
        raw = jnp.einsum(
            "qhd,kd->hqk", queries[first_row:upto], keys[:upto], preferred_element_type=f32
        )
        allowed = mask_block(first_row, block_rows, upto, seq_len)
        scores = jnp.where(allowed[None], raw * factor, neg_large)
        row_max = jnp.max(scores, axis=-1, keepdims=True)
        exps = jnp.exp(scores - row_max)
        total = jnp.sum(exps, axis=-1, keepdims=True)
        probs = (exps / total).astype(bf16)
        parts.append(
            jnp.einsum("hqk,kd->qhd", probs, values[:upto], preferred_element_type=f32).astype(bf16)
        )
        totals.append((row_max + jnp.log(total))[..., 0])
    return jnp.concatenate(parts, axis=0), jnp.concatenate(totals, axis=1)


def attend_back(queries, keys, values, grad_ctx, log_total, seq_len, factor):
    slots = keys.shape[0]
    block_rows = min(512, slots)
    dq_parts = []
    d_keys = jnp.zeros(keys.shape, f32)
    d_values = jnp.zeros(values.shape, f32)
    for first_row in range(0, slots, block_rows):
        upto = first_row + block_rows
        q_block = queries[first_row:upto]
        g_block = grad_ctx[first_row:upto]
        raw = jnp.einsum("qhd,kd->hqk", q_block, keys[:upto], preferred_element_type=f32)
        allowed = mask_block(first_row, block_rows, upto, seq_len)
        scores = jnp.where(allowed[None], raw * factor, neg_large)
        probs = jnp.exp(scores - log_total[:, first_row:upto, None])
        grad_p = jnp.einsum("qhd,kd->hqk", g_block, values[:upto], preferred_element_type=f32)
        inner = jnp.sum(probs * grad_p, axis=-1, keepdims=True)
        grad_s = (probs * (grad_p - inner) * factor).astype(bf16)
        dq_parts.append(
            jnp.einsum("hqk,kd->qhd", grad_s, keys[:upto], preferred_element_type=f32)
        )
        dk = jnp.einsum("hqk,qhd->kd", grad_s, q_block, preferred_element_type=f32)
        dv = jnp.einsum("hqk,qhd->kd", probs.astype(bf16), g_block, preferred_element_type=f32)
        d_keys = d_keys.at[:upto].add(dk)
        d_values = d_values.at[:upto].add(dv)
    return jnp.concatenate(dq_parts, axis=0), d_keys, d_values


def spread_heads(block):
    mp_size = lax.axis_size("mp")
    rows, heads, part = block.shape
    send = jnp.repeat(block, mp_size // heads, axis=1)
    got = lax.all_to_all(send, "mp", 1, 1, tiled=True)
    return got.reshape(rows, mp_size * part)


def collect_heads(block, heads):
    mp_size = lax.axis_size("mp")
    rows, size = block.shape
    got = lax.all_to_all(block.reshape(rows, mp_size, size // mp_size), "mp", 1, 1, tiled=True)
    got = got.reshape(rows, heads, mp_size // heads, size // mp_size)
    return jnp.sum(got.astype(f32), axis=2)


def gather_dp(block):
    return lax.all_gather(block, "dp", axis=0, tiled=True)


def reduce_dp(block):
    return lax.psum_scatter(block, "dp", scatter_dimension=0, tiled=True)


def local(
    x_in,
    lengths,
    gain_attn,
    query_weight,
    key_projection_matrix,
    value_projection_matrix,
    out_weight,
    gain_ffn,
    gate_weight,
    up_weight,
    down_weight,
    cotangent,
):
    _, slots, width = x_in.shape
    mp_size = lax.axis_size("mp")
    me = lax.axis_index("mp")
    heads_here = query_weight.shape[1] // HEAD_SIZE
    q_cols = query_weight.shape[1]
    factor = HEAD_SIZE ** (-0.5)
    here = slots // mp_size
    seq_len = lengths[0]
    cos_t, sin_t = rope_tables(slots, HEAD_SIZE)

    kv_block = jnp.concatenate(
        [spread_heads(key_projection_matrix), spread_heads(value_projection_matrix)], axis=1
    )
    gains = lax.all_gather(jnp.stack([gain_attn, gain_ffn]), "dp", axis=1, tiled=True).astype(f32)
    g_attn, g_ffn = gains[0], gains[1]
    w_q = gather_dp(query_weight)
    w_kv = gather_dp(kv_block)
    w_o = gather_dp(out_weight.T)
    w_g = gather_dp(gate_weight)
    w_u = gather_dp(up_weight)
    w_d = gather_dp(down_weight.T)

    tok = x_in[0].astype(f32)
    r1 = lax.rsqrt(jnp.mean(tok * tok, axis=-1, keepdims=True) + eps_norm)
    h_attn = (tok * r1 * g_attn).astype(bf16)
    cos_h, sin_h = cos_t[:, None, :], sin_t[:, None, :]
    queries = rotate(
        mm(h_attn, w_q).reshape(slots, heads_here, HEAD_SIZE), cos_h, sin_h
    ).astype(bf16)
    kv_lin = mm(h_attn, w_kv)
    keys = rotate(kv_lin[:, :HEAD_SIZE], cos_t, sin_t).astype(bf16)
    values = kv_lin[:, HEAD_SIZE:].astype(bf16)
    context, log_total = attend(queries, keys, values, seq_len, factor)
    context = context.reshape(slots, q_cols)

    half = width // 2

    def product_out(lefts, which):
        return mm_t(lefts[0], w_o[which * half : (which + 1) * half])

    attn_rows = scatter_rows(product_out, [context], width)
    tok_here = lax.dynamic_slice_in_dim(x_in[0], me * here, here, 0).astype(f32)
    mid = tok_here + attn_rows
    r2 = lax.rsqrt(jnp.mean(mid * mid, axis=-1, keepdims=True) + eps_norm)
    n2 = mid * r2
    h_ffn = gather_rows((n2 * g_ffn).astype(bf16))

    gate = mm(h_ffn, w_g)
    up = mm(h_ffn, w_u)
    sig = jax.nn.sigmoid(gate)
    hidden = (gate * sig * up).astype(bf16)

    valid = (jnp.arange(slots)[:, None] < seq_len).astype(bf16)
    grad_low = cotangent[0] * valid
    down_grad = mm_rows(grad_low, hidden).astype(bf16)
    down_out = reduce_dp(down_grad)

    d_hidden = mm(grad_low, w_d)
    d_gate = (d_hidden * up * sig * (1.0 + gate * (1.0 - sig))).astype(bf16)
    d_up = (d_hidden * gate * sig).astype(bf16)

    def product_h2(lefts, which):
        cols = slice(which * half, (which + 1) * half)
        return mm_t(lefts[0], w_g[cols]) + mm_t(lefts[1], w_u[cols])

    d_h2 = scatter_rows(product_h2, [d_gate, d_up], width)
    gate_out = reduce_dp(mm_rows(h_ffn, d_gate).astype(bf16))
    up_out = reduce_dp(mm_rows(h_ffn, d_up).astype(bf16))

    gain_ffn_part = jnp.sum(d_h2 * n2, axis=0)
    e2 = d_h2 * g_ffn
    grad_here = lax.dynamic_slice_in_dim(grad_low, me * here, here, 0).astype(f32)
    g1 = grad_here + r2 * (e2 - n2 * jnp.mean(e2 * n2, axis=-1, keepdims=True))
    g1_low = gather_rows(g1.astype(bf16))

    def product_ffn(lefts, which):
        return mm_t(lefts[0], w_d[which * half : (which + 1) * half])

    ffn_rows = scatter_rows(product_ffn, [hidden], width)
    layer_out = gather_rows((mid + ffn_rows).astype(bf16))

    d_context = mm(g1_low, w_o).astype(bf16).reshape(slots, heads_here, HEAD_SIZE)
    out_out = reduce_dp(mm_rows(g1_low, context).astype(bf16))
    dq, dk, dv = attend_back(
        queries, keys, values, d_context, log_total, seq_len, factor
    )
    d_q = rotate_back(dq, cos_h, sin_h).astype(bf16).reshape(slots, q_cols)
    d_kv = jnp.concatenate([rotate_back(dk, cos_t, sin_t), dv], axis=1).astype(bf16)
    q_out = reduce_dp(mm_rows(h_attn, d_q).astype(bf16))
    kv_out = reduce_dp(mm_rows(h_attn, d_kv).astype(bf16))

    def product_h1(lefts, which):
        cols = slice(which * half, (which + 1) * half)
        return mm_t(lefts[0], w_q[cols]) + mm_t(lefts[1], w_kv[cols])

    d_h1 = scatter_rows(product_h1, [d_q, d_kv], width)
    r1_here = lax.dynamic_slice_in_dim(r1, me * here, here, 0)
    n1 = tok_here * r1_here
    gain_attn_part = jnp.sum(d_h1 * n1, axis=0)
    e1 = d_h1 * g_attn
    grad_in = g1 + r1_here * (e1 - n1 * jnp.mean(e1 * n1, axis=-1, keepdims=True))
    grad_input = gather_rows(grad_in.astype(bf16)).astype(f32)

    gain_parts = lax.psum(jnp.stack([gain_attn_part, gain_ffn_part]), ("dp", "mp"))
    rows_here = gain_attn.shape[0]
    gain_grads = lax.dynamic_slice_in_dim(
        gain_parts, lax.axis_index("dp") * rows_here, rows_here, 1
    )
    key_grad = collect_heads(kv_out[:, :HEAD_SIZE], KEY_VALUE_HEADS)
    value_grad = collect_heads(kv_out[:, HEAD_SIZE:], KEY_VALUE_HEADS)
    return (
        layer_out[None],
        grad_input[None],
        gain_grads[0],
        q_out.astype(f32),
        key_grad,
        value_grad,
        out_out.T.astype(f32),
        gain_grads[1],
        gate_out.astype(f32),
        up_out.astype(f32),
        down_out.T.astype(f32),
    )


def solution(mesh):
    return jax.shard_map(
        local,
        mesh=mesh,
        in_specs=(
            P("dp", None, None),
            P("dp"),
            P("dp"),
            P("dp", "mp"),
            P("dp", None, "mp"),
            P("dp", None, "mp"),
            P("mp", "dp"),
            P("dp"),
            P("dp", "mp"),
            P("dp", "mp"),
            P("mp", "dp"),
            P("dp", None, None),
        ),
        out_specs=(
            P("dp", None, None),
            P("dp", None, None),
            P("dp"),
            P("dp", "mp"),
            P("dp", None, "mp"),
            P("dp", None, "mp"),
            P("mp", "dp"),
            P("dp"),
            P("dp", "mp"),
            P("dp", "mp"),
            P("mp", "dp"),
        ),
        check_vma=False,
    )
```

time: 2000 us -> 945 us (0.47)
  waiting for transfers between devices: 1530 us -> 440 us
  matrix products: 285 us -> 233 us
  starting transfers between devices: 1.31 us -> 47 us
  local copies, waits for them, and re-layouts: 34.9 us -> 65.4 us
  blocking collectives: 54.4 us -> 75.8 us
    psum x4 -> x0, waiting for transfers between devices: 527 us -> none  [the longest x1 170 us: local(): d_h2 = lax.psum(dot_cols(d_gate, wg_all) + dot_cols(d_up, wu_all), 'mp')]
    reduce_scatter x8 -> x6, waiting for transfers between devices: 640 us -> 118 us  [reduce_dp(): return lax.psum_scatter(block, 'dp', scatter_dimension=0, tiled=True)]
    all_gather x9 -> x6, waiting for transfers between devices: 361 us -> 149 us  [gather_dp(): return lax.all_gather(block, 'dp', axis=0, tiled=True)]
    ppermute x0 -> x32, waiting for transfers between devices: none -> 169 us  [the longest x4 42.4 us: gather_rows(): far_b = lax.ppermute(pair_b, 'mp', OVER_Y)]
    dot_general x35 -> x48, matrix products: 285 us -> 233 us  [the longest x24 71.9 us: mm_t(): lax.dot_general(left, right, (((1,), (1,)), ((), ())), preferred_element_...]
    psum x0 -> x1, blocking collectives: none -> 45.3 us  [local(): lax.psum(jnp.stack([gain_attn_part, gain_ffn_part]), ('dp', 'mp'))]
    ppermute x0 -> x32, starting transfers between devices: none -> 38.4 us  [the longest x4 6.26 us: gather_rows(): far_a = lax.ppermute(pair_a, 'mp', OVER_X)]
    unnamed x1 -> x0, blocking collectives: 28.9 us -> none
  transfers between devices with their start and end apart: 21 -> 46, of which waited for: 19 -> 32; matrix products, arithmetic and copies ran while one was open for 12% -> 29% of each run, Pallas kernels for 0% -> 0%
where the time goes in v1:
time: 945 us; the launch traced here: 941 us
  waiting for transfers between devices  440 us (47%)
  matrix products  233 us (25%)
  blocking collectives  75.8 us (8%)
  local copies, waits for them, and re-layouts  65.4 us (7%)
  other arithmetic  63.3 us (7%)
  starting transfers between devices  47 us (5%)
  between operations  16.5 us (2%)
    all_gather x6, waiting for transfers between devices, gather_dp(): return lax.all_gather(block, 'dp', axis=0, tiled=True)  149 us
    reduce_scatter x6, waiting for transfers between devices, reduce_dp(): return lax.psum_scatter(block, 'dp', scatter_dimension=0, tiled=True)  118 us
    dot_general x24, matrix products, mm_t(): lax.dot_general(left, right, (((1,), (1,)), ((), ())), preferred_element_...  71.9 us
    dot_general x6, matrix products, mm(): lax.dot_general(left, right, (((1,), (0,)), ((), ())), preferred_element_...  64.1 us
    dot_general x6, matrix products, mm_rows(): lax.dot_general(left, right, (((0,), (0,)), ((), ())), preferred_element_...  57.4 us
    psum x1, blocking collectives, local(): lax.psum(jnp.stack([gain_attn_part, gain_ffn_part]), ('dp', 'mp'))  45.3 us
    ppermute x4, waiting for transfers between devices, gather_rows(): far_b = lax.ppermute(pair_b, 'mp', OVER_Y)  42.4 us
    unnamed x144, local copies, waits for them, and re-layouts  37.5 us
  transfers between devices with their start and end apart: 46, of which 32 were waited for; matrix products, arithmetic and copies ran while one was open for 29% of the time, Pallas kernels for 0%

profile of v1, /device:TPU:0, one launch (start us, length us, event | category | flops | bytes accessed | tf_op | source)
XLA Modules:
  0.0 940.7 jit_solution(466775596118007731)
XLA Ops:
  8.0 10.2 %all_to_all.20 = bf16[256,4,64]{0,2,1:T(8,128)(2,1)S(1)} all-to-all(bf16[256,4,64]{0,2,1:T(8,128)(2,1)} %param.28), channel_id=1, replica_groups=mesh['dp'=8,'mp'=4] {'mp'}, dimensions={1} | all-to-all | bytes 262144 | tf_op jit(solution)/shard_map/all_to_all | solution.py:177
  18.2 8.3 all_to_all.21
  33.7 12.0 %all_gather.21 = bf16[2,2048]{1,0:T(2,128)(2,1)S(1)} all-gather(bf16[2,256]{1,0:T(2,128)(2,1)S(1)} %pad_maximum_fusion.34), channel_id=1, replica_groups=mesh['dp'=8,'mp'=4] {'dp'}, dimensions={1}, use_global_device_ids=true | all-gather | bytes 9216 | tf_op jit(solution)/shard_map/all_gather | solution.py:224
  56.1 17.9 %all-gather.7.cloned.1.call-done = bf16[2048,512]{0,1:T(8,128)(2,1)} async-done(((bf16[256,512]{0,1:T(8,128)(2,1)}), bf16[2048,512]{0,1:T(8,128)(2,1)}) %all-gather.7.cloned.1.call-update) | async-done | bytes 2097168 | tf_op jit(solution)/shard_map/all_gather | solution.py:190
  94.3 11.2 %all-gather.11.cloned.1.call-done = bf16[2048,512]{0,1:T(8,128)(2,1)} async-done(((bf16[256,512]{0,1:T(8,128)(2,1)}), bf16[2048,512]{0,1:T(8,128)(2,1)}) %all-gather.11.cloned.1.call-update) | async-done | bytes 2097168 | tf_op jit(solution)/shard_map/all_gather | solution.py:190
  125.0 9.1 collective-permute-done.2
  137.9 7.5 collective-permute-done
  167.0 9.1 collective-permute-done.4
  183.6 16.3 %collective-permute-done.7 = bf16[2,256,1024]{2,1,0:T(8,128)(2,1)S(1)} collective-permute-done((bf16[2,256,1024]{2,1,0:T(8,128)(2,1)S(1)}, bf16[2,256,1024]{2,1,0:T(8,128)(2,1)S(1)}, u32[]{:S(2)}, u32[]{:S(2)}) %collective-permute-start.7) | collective-permute-done | bytes 1048608 | tf_op jit(solution)/shard_map/ppermute | solution.py:110
  203.2 14.8 %fusion.237 = f32[1024,2048]{1,0:T(8,128)} fusion(bf16[1024,2048]{1,0:T(8,128)(2,1)} %bitcast_multiply_fusion.1, bf16[2048,2048]{0,1:T(8,128)(2,1)} %all-gather.17.cloned.1.call-done), kind=kOutput, calls=%fused_computation.365 | convolution fusion | flops 8589934592 | bytes 20971520 | tf_op jit(solution)/shard_map/dot_general | solution.py:37
  218.0 52.4 %all-gather.15.cloned.1.call-done = bf16[2048,2048]{1,0:T(8,128)(2,1)} async-done(((bf16[256,2048]{1,0:T(8,128)(2,1)}), bf16[2048,2048]{1,0:T(8,128)(2,1)}) %all-gather.15.cloned.1.call-update) | async-done | bytes 8388624 | tf_op jit(solution)/shard_map/all_gather | solution.py:190
  270.3 14.4 %fusion.223 = f32[1024,2048]{1,0:T(8,128)} fusion(bf16[2048,2048]{1,0:T(8,128)(2,1)} %all-gather.15.cloned.1.call-done, bf16[1024,1024]{1,0:T(8,128)(2,1)} %bitcast.429, bf16[1024,1024]{1,0:T(8,128)(2,1)} %bitcast.433), kind=kOutput, calls=%fused_computation.351 | convolution fusion | flops 8598323200 | bytes 20971520 | tf_op jit(solution)/shard_map/dot_general | solution.py:37
  284.8 67.6 %all-gather.13.cloned.1.call-done = bf16[2048,2048]{1,0:T(8,128)(2,1)} async-done(((bf16[256,2048]{1,0:T(8,128)(2,1)}), bf16[2048,2048]{1,0:T(8,128)(2,1)}) %all-gather.13.cloned.1.call-update) | async-done | bytes 8388624 | tf_op jit(solution)/shard_map/all_gather | solution.py:190
  352.4 21.8 %multiply_convert_fusion.1 = (bf16[1024,2048]{1,0:T(8,128)(2,1)}, bf16[1024,2048]{1,0:T(8,128)(2,1)}, bf16[1024,2048]{1,0:T(8,128)(2,1)}) fusion(f32[1024,2048]{1,0:T(8,128)} %fusion.237, f32[1024,2048]{1,0:T(8,128)} %fusion.223, bf16[2048,2048]{1,0:T(8,128)(2,1)} %all-gather.13.cloned.1.call-done, bf16[1024,1024]{1,0:T(8,128)(2,1)} %bitcast.430, ...), kind=kOutput, calls=%fused_computation.12 | convolution fusion | flops 8631877632 | bytes 41943040 | tf_op jit(solution)/shard_map/dot_general | solution.py:37
  374.2 6.3 fusion.92
  435.1 11.0 %collective-permute-done.16 = bf16[512,1024]{1,0:T(8,128)(2,1)S(1)} collective-permute-done((bf16[512,1024]{1,0:T(8,128)(2,1)S(1)}, bf16[512,1024]{1,0:T(8,128)(2,1)S(1)}, u32[]{:S(2)}, u32[]{:S(2)}) %collective-permute-start.16) | collective-permute-done | bytes 1048608 | tf_op jit(solution)/shard_map/ppermute | solution.py:81
  456.6 10.8 %collective-permute-done.19 = bf16[256,1024]{1,0:T(8,128)(2,1)S(1)} collective-permute-done((bf16[256,1024]{1,0:T(8,128)(2,1)S(1)}, bf16[256,1024]{1,0:T(8,128)(2,1)S(1)}, u32[]{:S(2)}, u32[]{:S(2)}) %collective-permute-start.19) | collective-permute-done | bytes 524320 | tf_op jit(solution)/shard_map/ppermute | solution.py:86
  481.2 7.8 collective-permute-done.20
  493.5 17.6 %collective-permute-done.23 = bf16[2,256,1024]{2,1,0:T(8,128)(2,1)S(1)} collective-permute-done((bf16[2,256,1024]{2,1,0:T(8,128)(2,1)S(1)}, bf16[2,256,1024]{2,1,0:T(8,128)(2,1)S(1)}, u32[]{:S(2)}, u32[]{:S(2)}) %collective-permute-start.23) | collective-permute-done | bytes 1048608 | tf_op jit(solution)/shard_map/ppermute | solution.py:110
  531.7 9.8 %fusion.115 = f32[1024,256]{0,1:T(8,128)} fusion(f32[1024,512,2]{1,0,2:T(8,128)} %fusion.188, f32[2,512,1024]{1,2,0:T(8,128)} %copy-done.21, f32[2,512]{1,0:T(2,128)S(1)} %log_add_fusion, f32[512,256]{0,1:T(8,128)} %fusion.125, bf16[1024,2,128]{0,2,1:T(8,128)(2,1)} %copy-done.44, bf16[1024,2,128]{0,2,1:T(8,128)(2,1)} %copy-done.42), kind=kOutput, calls=%fused_computation.153 | convolution fusion | flops 545523712 | bytes 11014144 | tf_op jit(solution)/shard_map/hqk,qhd->kd/dot_general | solution.py:166
  563.4 9.6 %fusion.113 = f32[512,2,256]{0,2,1:T(8,128)} fusion(f32[1024,512,2]{1,0,2:T(8,128)} %fusion.188, f32[2,512,1024]{1,2,0:T(8,128)} %copy-done.21, f32[2,512]{1,0:T(2,128)S(1)} %log_add_fusion, bf16[1024,128]{0,1:T(8,128)(2,1)} %copy-done.45, bf16[1024,128]{0,1:T(8,128)(2,1)} %copy-done.46), kind=kOutput, calls=%fused_computation.151 | convolution fusion | flops 545261568 | bytes 9965568 | tf_op jit(solution)/shard_map/hqk,kd->qhd/dot_general | solution.py:164
  579.9 14.1 %convolution_convert_fusion = bf16[2048,2048]{1,0:T(8,128)(2,1)} fusion(bf16[1024,2048]{1,0:T(8,128)(2,1)} %bitcast_multiply_fusion.1, bf16[1024,2048]{1,0:T(8,128)(2,1)} %get-tuple-element.117), kind=kOutput, calls=%fused_computation.15 | convolution fusion | flops 8594128896 | bytes 16777216 | tf_op jit(solution)/shard_map/dot_general | solution.py:45
  595.6 13.4 %convolution_convert_fusion.2 = bf16[2048,2048]{1,0:T(8,128)(2,1)} fusion(bf16[1024,2048]{1,0:T(8,128)(2,1)} %get-tuple-element.116, bf16[1024,1024]{1,0:T(8,128)(2,1)S(1)} %bitcast.431, bf16[1024,1024]{1,0:T(8,128)(2,1)} %bitcast.435), kind=kOutput, calls=%fused_computation.17 | convolution fusion | flops 8602517504 | bytes 16777216 | tf_op jit(solution)/shard_map/dot_general | solution.py:45
  609.1 13.6 %convolution_convert_fusion.1 = bf16[2048,2048]{1,0:T(8,128)(2,1)} fusion(bf16[1024,2048]{1,0:T(8,128)(2,1)} %get-tuple-element.118, bf16[1024,1024]{1,0:T(8,128)(2,1)S(1)} %bitcast.432, bf16[1024,1024]{1,0:T(8,128)(2,1)} %bitcast.436), kind=kOutput, calls=%fused_computation.16 | convolution fusion | flops 8602517504 | bytes 16777216 | tf_op jit(solution)/shard_map/dot_general | solution.py:45
  627.1 7.3 collective-permute-done.12
  663.4 13.3 %collective-permute-done.26 = bf16[512,1024]{1,0:T(8,128)(2,1)S(1)} collective-permute-done((bf16[512,1024]{1,0:T(8,128)(2,1)S(1)}, bf16[512,1024]{1,0:T(8,128)(2,1)S(1)}, u32[]{:S(2)}, u32[]{:S(2)}) %collective-permute-start.26) | collective-permute-done | bytes 1048608 | tf_op jit(solution)/shard_map/ppermute | solution.py:82
  679.0 6.8 collective-permute-done.24
  690.6 6.5 collective-permute-done.27
  706.3 8.5 collective-permute-done.15
  733.9 45.3 %psum.7 = f32[2,2048]{1,0:T(2,128)S(1)} all-reduce(f32[2,2048]{1,0:T(2,128)S(1)} %pad_maximum_fusion.33), channel_id=1, replica_groups=mesh['dp'=8,'mp'=4] {'dp','mp'}, use_global_device_ids=true, to_apply=%region_12.13 | all-reduce | flops 4096 | bytes 32768 | tf_op jit(solution)/shard_map/psum | solution.py:314
  809.8 31.0 %reduce-scatter.13.cloned.1.call-done = bf16[256,2048]{1,0:T(8,128)(2,1)} async-done(((bf16[2048,2048]{1,0:T(8,128)(2,1)}), bf16[256,2048]{1,0:T(8,128)(2,1)}) %reduce-scatter.13.cloned.1.call-update) | async-done | bytes 1048592 | tf_op jit(solution)/shard_map/reduce_scatter | solution.py:194
  843.6 87.3 %reduce-scatter.15.cloned.1.call-done = bf16[256,2048]{1,0:T(8,128)(2,1)} async-done(((bf16[2048,2048]{1,0:T(8,128)(2,1)}), bf16[256,2048]{1,0:T(8,128)(2,1)}) %reduce-scatter.15.cloned.1.call-update) | async-done | bytes 1048592 | tf_op jit(solution)/shard_map/reduce_scatter | solution.py:194
  (387 shorter events, 331.7 us)
Async XLA Ops:
  7.2 39.1 %all-gather.9.cloned.1.call-start = ((), (), s32[]{:S(2)}) async-start(), calls=%async_computation.11 | async-start | bytes 2359296 | tf_op jit(solution)/shard_map/all_gather | solution.py:190
  7.9 66.1 %all-gather.7.cloned.1.call-start = ((), (), s32[]{:S(2)}) async-start(), calls=%async_computation.10 | async-start | bytes 2359296 | tf_op jit(solution)/shard_map/all_gather | solution.py:190
  27.2 78.3 %all-gather.11.cloned.1.call-start = ((), (), s32[]{:S(2)}) async-start(), calls=%async_computation.12 | async-start | bytes 2359296 | tf_op jit(solution)/shard_map/all_gather | solution.py:190
  28.0 175.2 %all-gather.17.cloned.1.call-start = ((), (), s32[]{:S(2)}) async-start(), calls=%async_computation.15 | async-start | bytes 9437184 | tf_op jit(solution)/shard_map/all_gather | solution.py:190
  28.5 241.8 %all-gather.15.cloned.1.call-start = ((), (), s32[]{:S(2)}) async-start(), calls=%async_computation.14 | async-start | bytes 9437184 | tf_op jit(solution)/shard_map/all_gather | solution.py:190
  29.1 323.3 %all-gather.13.cloned.1.call-start = ((), (), s32[]{:S(2)}) async-start(), calls=%async_computation.13 | async-start | bytes 9437184 | tf_op jit(solution)/shard_map/all_gather | solution.py:190
  29.7 754.8 %reduce-scatter.9.cloned.1.call-start = ((), (), s32[]{:S(2)}) async-start(), calls=%async_computation.17 | async-start | bytes 2359296 | tf_op jit(solution)/shard_map/reduce_scatter | solution.py:194
  108.5 25.6 %collective-permute-start.2 = (bf16[512,1024]{1,0:T(8,128)(2,1)}, bf16[512,1024]{1,0:T(8,128)(2,1)}, u32[]{:S(2)}, u32[]{:S(2)}) collective-permute-start(bf16[512,1024]{1,0:T(8,128)(2,1)} %convolution_convert_fusion.5), channel_id=1, source_target_pairs={{0,2},{2,0},{1,3},{3,1},{4,6},{6,4},{5,7},{7,5},{8,10},{10,8},{9,1... | collective-permute-start | bytes 3145736 | tf_op jit(solution)/shard_map/ppermute | solution.py:82
  119.0 26.4 %collective-permute-start = (bf16[512,1024]{1,0:T(8,128)(2,1)}, bf16[512,1024]{1,0:T(8,128)(2,1)}, u32[]{:S(2)}, u32[]{:S(2)}) collective-permute-start(bf16[512,1024]{1,0:T(8,128)(2,1)} %convolution_convert_fusion.6), channel_id=1, source_target_pairs={{0,1},{1,0},{2,3},{3,2},{4,5},{5,4},{6,7},{7,6},{8,9},{9,8},{10,11... | collective-permute-start | bytes 3145736 | tf_op jit(solution)/shard_map/ppermute | solution.py:81
  178.7 21.2 %collective-permute-start.7 = (bf16[2,256,1024]{2,1,0:T(8,128)(2,1)S(1)}, bf16[2,256,1024]{2,1,0:T(8,128)(2,1)S(1)}, u32[]{:S(2)}, u32[]{:S(2)}) collective-permute-start(bf16[2,256,1024]{2,1,0:T(8,128)(2,1)S(1)} %pad_maximum_fusion.19), channel_id=1, source_target_pairs={{0,2},{2,0},{1,3},{3,1},{4,6},{6,4},{5,7},{7,5},{8,10},{10,8},{9,1... | collective-permute-start | bytes 3145736 | tf_op jit(solution)/shard_map/ppermute | solution.py:110
  179.5 22.0 %collective-permute-start.5 = (bf16[2,256,1024]{2,1,0:T(8,128)(2,1)S(1)}, bf16[2,256,1024]{2,1,0:T(8,128)(2,1)S(1)}, u32[]{:S(2)}, u32[]{:S(2)}) collective-permute-start(bf16[2,256,1024]{2,1,0:T(8,128)(2,1)S(1)} %pad_maximum_fusion.18), channel_id=1, source_target_pairs={{0,1},{1,0},{2,3},{3,2},{4,5},{5,4},{6,7},{7,6},{8,9},{9,8},{10,11... | collective-permute-start | bytes 3145736 | tf_op jit(solution)/shard_map/ppermute | solution.py:109
  380.5 41.3 %collective-permute-start.10 = (bf16[512,1024]{1,0:T(8,128)(2,1)}, bf16[512,1024]{1,0:T(8,128)(2,1)}, u32[]{:S(2)}, u32[]{:S(2)}) collective-permute-start(bf16[512,1024]{1,0:T(8,128)(2,1)} %fusion.92), channel_id=1, source_target_pairs={{0,2},{2,0},{1,3},{3,1},{4,6},{6,4},{5,7},{7,5},{8,10},{10,8},{9,1... | collective-permute-start | bytes 3145736 | tf_op jit(solution)/shard_map/ppermute | solution.py:82
  390.1 38.5 %collective-permute-start.18 = (bf16[512,1024]{1,0:T(8,128)(2,1)}, bf16[512,1024]{1,0:T(8,128)(2,1)}, u32[]{:S(2)}, u32[]{:S(2)}) collective-permute-start(bf16[512,1024]{1,0:T(8,128)(2,1)} %add_convert_fusion.2), channel_id=1, source_target_pairs={{0,2},{2,0},{1,3},{3,1},{4,6},{6,4},{5,7},{7,5},{8,10},{10,8},{9,1... | collective-permute-start | bytes 3145736 | tf_op jit(solution)/shard_map/ppermute | solution.py:82
  397.4 55.7 %collective-permute-start.8 = (bf16[512,1024]{1,0:T(8,128)(2,1)}, bf16[512,1024]{1,0:T(8,128)(2,1)S(1)}, u32[]{:S(2)}, u32[]{:S(2)}) collective-permute-start(bf16[512,1024]{1,0:T(8,128)(2,1)} %fusion.98), channel_id=1, source_target_pairs={{0,1},{1,0},{2,3},{3,2},{4,5},{5,4},{6,7},{7,6},{8,9},{9,8},{10,11... | collective-permute-start | bytes 3145736 | tf_op jit(solution)/shard_map/ppermute | solution.py:81
  410.8 35.4 %collective-permute-start.16 = (bf16[512,1024]{1,0:T(8,128)(2,1)S(1)}, bf16[512,1024]{1,0:T(8,128)(2,1)S(1)}, u32[]{:S(2)}, u32[]{:S(2)}) collective-permute-start(bf16[512,1024]{1,0:T(8,128)(2,1)S(1)} %add_convert_fusion.3), channel_id=1, source_target_pairs={{0,1},{1,0},{2,3},{3,2},{4,5},{5,4},{6,7},{7,6},{8,9},{9,8},{10,11... | collective-permute-start | bytes 3145736 | tf_op jit(solution)/shard_map/ppermute | solution.py:81
  425.5 42.9 %collective-permute-start.11 = (bf16[256,1024]{1,0:T(8,128)(2,1)S(1)}, bf16[256,1024]{1,0:T(8,128)(2,1)S(1)}, u32[]{:S(2)}, u32[]{:S(2)}) collective-permute-start(bf16[256,1024]{1,0:T(8,128)(2,1)S(1)} %fusion.172), channel_id=1, source_target_pairs={{0,1},{1,0},{2,3},{3,2},{4,5},{5,4},{6,7},{7,6},{8,9},{9,8},{10,11... | collective-permute-start | bytes 1572872 | tf_op jit(solution)/shard_map/ppermute | solution.py:86
  433.6 33.8 %collective-permute-start.19 = (bf16[256,1024]{1,0:T(8,128)(2,1)S(1)}, bf16[256,1024]{1,0:T(8,128)(2,1)S(1)}, u32[]{:S(2)}, u32[]{:S(2)}) collective-permute-start(bf16[256,1024]{1,0:T(8,128)(2,1)S(1)} %fusion.174), channel_id=1, source_target_pairs={{0,1},{1,0},{2,3},{3,2},{4,5},{5,4},{6,7},{7,6},{8,9},{9,8},{10,11... | collective-permute-start | bytes 1572872 | tf_op jit(solution)/shard_map/ppermute | solution.py:86
  491.3 19.8 %collective-permute-start.23 = (bf16[2,256,1024]{2,1,0:T(8,128)(2,1)S(1)}, bf16[2,256,1024]{2,1,0:T(8,128)(2,1)S(1)}, u32[]{:S(2)}, u32[]{:S(2)}) collective-permute-start(bf16[2,256,1024]{2,1,0:T(8,128)(2,1)S(1)} %pad_maximum_fusion.23), channel_id=1, source_target_pairs={{0,2},{2,0},{1,3},{3,1},{4,6},{6,4},{5,7},{7,5},{8,10},{10,8},{9,1... | collective-permute-start | bytes 3145736 | tf_op jit(solution)/shard_map/ppermute | solution.py:110
  491.9 20.4 %collective-permute-start.21 = (bf16[2,256,1024]{2,1,0:T(8,128)(2,1)S(1)}, bf16[2,256,1024]{2,1,0:T(8,128)(2,1)S(1)}, u32[]{:S(2)}, u32[]{:S(2)}) collective-permute-start(bf16[2,256,1024]{2,1,0:T(8,128)(2,1)S(1)} %pad_maximum_fusion.22), channel_id=1, source_target_pairs={{0,1},{1,0},{2,3},{3,2},{4,5},{5,4},{6,7},{7,6},{8,9},{9,8},{10,11... | collective-permute-start | bytes 3145736 | tf_op jit(solution)/shard_map/ppermute | solution.py:109
  552.5 248.2 %reduce-scatter.11.cloned.1.call-start = ((), (), s32[]{:S(2)}) async-start(), calls=%async_computation.18 | async-start | bytes 2359296 | tf_op jit(solution)/shard_map/reduce_scatter | solution.py:194
  559.7 243.1 %reduce-scatter.7.cloned.1.call-start = ((), (), s32[]{:S(2)}) async-start(), calls=%async_computation.16 | async-start | bytes 2359296 | tf_op jit(solution)/shard_map/reduce_scatter | solution.py:194
  579.8 226.7 %reduce-scatter.17.cloned.1.call-start = ((), (), s32[]{:S(2)}) async-start(), calls=%async_computation.21 | async-start | bytes 9437184 | tf_op jit(solution)/shard_map/reduce_scatter | solution.py:194
  594.0 246.8 %reduce-scatter.13.cloned.1.call-start = ((), (), s32[]{:S(2)}) async-start(), calls=%async_computation.19 | async-start | bytes 9437184 | tf_op jit(solution)/shard_map/reduce_scatter | solution.py:194
  609.0 321.8 %reduce-scatter.15.cloned.1.call-start = ((), (), s32[]{:S(2)}) async-start(), calls=%async_computation.20 | async-start | bytes 9437184 | tf_op jit(solution)/shard_map/reduce_scatter | solution.py:194
  657.2 19.5 %collective-permute-start.26 = (bf16[512,1024]{1,0:T(8,128)(2,1)S(1)}, bf16[512,1024]{1,0:T(8,128)(2,1)S(1)}, u32[]{:S(2)}, u32[]{:S(2)}) collective-permute-start(bf16[512,1024]{1,0:T(8,128)(2,1)S(1)} %add_convert_fusion), channel_id=1, source_target_pairs={{0,2},{2,0},{1,3},{3,1},{4,6},{6,4},{5,7},{7,5},{8,10},{10,8},{9,1... | collective-permute-start | bytes 3145736 | tf_op jit(solution)/shard_map/ppermute | solution.py:82
  660.5 25.4 %collective-permute-start.24 = (bf16[512,1024]{1,0:T(8,128)(2,1)S(1)}, bf16[512,1024]{1,0:T(8,128)(2,1)S(1)}, u32[]{:S(2)}, u32[]{:S(2)}) collective-permute-start(bf16[512,1024]{1,0:T(8,128)(2,1)S(1)} %add_convert_fusion.1), channel_id=1, source_target_pairs={{0,1},{1,0},{2,3},{3,2},{4,5},{5,4},{6,7},{7,6},{8,9},{9,8},{10,11... | collective-permute-start | bytes 3145736 | tf_op jit(solution)/shard_map/ppermute | solution.py:81
  677.6 19.5 %collective-permute-start.27 = (bf16[256,1024]{1,0:T(8,128)(2,1)S(1)}, bf16[256,1024]{1,0:T(8,128)(2,1)S(1)}, u32[]{:S(2)}, u32[]{:S(2)}) collective-permute-start(bf16[256,1024]{1,0:T(8,128)(2,1)S(1)} %fusion.176), channel_id=1, source_target_pairs={{0,1},{1,0},{2,3},{3,2},{4,5},{5,4},{6,7},{7,6},{8,9},{9,8},{10,11... | collective-permute-start | bytes 1572872 | tf_op jit(solution)/shard_map/ppermute | solution.py:86
  687.6 27.2 %collective-permute-start.15 = (bf16[2,256,1024]{2,1,0:T(8,128)(2,1)S(1)}, bf16[2,256,1024]{2,1,0:T(8,128)(2,1)S(1)}, u32[]{:S(2)}, u32[]{:S(2)}) collective-permute-start(bf16[2,256,1024]{2,1,0:T(8,128)(2,1)S(1)} %pad_maximum_fusion.21), channel_id=1, source_target_pairs={{0,2},{2,0},{1,3},{3,1},{4,6},{6,4},{5,7},{7,5},{8,10},{10,8},{9,1... | collective-permute-start | bytes 3145736 | tf_op jit(solution)/shard_map/ppermute | solution.py:110
  689.1 28.8 %collective-permute-start.13 = (bf16[2,256,1024]{2,1,0:T(8,128)(2,1)S(1)}, bf16[2,256,1024]{2,1,0:T(8,128)(2,1)S(1)}, u32[]{:S(2)}, u32[]{:S(2)}) collective-permute-start(bf16[2,256,1024]{2,1,0:T(8,128)(2,1)S(1)} %pad_maximum_fusion.20), channel_id=1, source_target_pairs={{0,1},{1,0},{2,3},{3,2},{4,5},{5,4},{6,7},{7,6},{8,9},{9,8},{10,11... | collective-permute-start | bytes 3145736 | tf_op jit(solution)/shard_map/ppermute | solution.py:109
  704.9 21.6 %collective-permute-start.30 = (bf16[256,1024]{1,0:T(8,128)(2,1)S(1)}, bf16[256,1024]{1,0:T(8,128)(2,1)S(1)}, u32[]{:S(2)}, u32[]{:S(2)}) collective-permute-start(bf16[256,1024]{1,0:T(8,128)(2,1)S(1)} %get-tuple-element.169), channel_id=1, source_target_pairs={{0,1},{1,0},{2,3},{3,2},{4,5},{5,4},{6,7},{7,6},{8,9},{9,8},{10,11... | collective-permute-start | bytes 1572872 | tf_op jit(solution)/shard_map/ppermute | solution.py:106
  727.7 52.1 %collective-permute-start.29 = (bf16[2,256,1024]{2,1,0:T(8,128)(2,1)}, bf16[2,256,1024]{2,1,0:T(8,128)(2,1)}, u32[]{:S(2)}, u32[]{:S(2)}) collective-permute-start(bf16[2,256,1024]{2,1,0:T(8,128)(2,1)} %pad_maximum_fusion.26), channel_id=1, source_target_pairs={{0,1},{1,0},{2,3},{3,2},{4,5},{5,4},{6,7},{7,6},{8,9},{9,8},{10,11... | collective-permute-start | bytes 3145736 | tf_op jit(solution)/shard_map/ppermute | solution.py:109
  730.9 50.8 %collective-permute-start.31 = (bf16[2,256,1024]{2,1,0:T(8,128)(2,1)}, bf16[2,256,1024]{2,1,0:T(8,128)(2,1)}, u32[]{:S(2)}, u32[]{:S(2)}) collective-permute-start(bf16[2,256,1024]{2,1,0:T(8,128)(2,1)} %pad_maximum_fusion.27), channel_id=1, source_target_pairs={{0,2},{2,0},{1,3},{3,1},{4,6},{6,4},{5,7},{7,5},{8,10},{10,8},{9,1... | collective-permute-start | bytes 3145736 | tf_op jit(solution)/shard_map/ppermute | solution.py:110
  (81 other events, 580.8 us)
Sparse Core Ops, SparseCore 0:
  9.6 31.8 all-gather.8
  43.6 30.3 all-gather.6
  75.6 29.8 all-gather.10
  107.0 81.5 all-gather.16
  190.1 80.2 all-gather.14
  271.8 80.5 all-gather.12
  552.7 33.2 reduce-scatter.8
  588.3 34.4 reduce-scatter.10
  625.1 34.3 reduce-scatter.6
  661.6 88.2 reduce-scatter.16
  752.2 88.5 reduce-scatter.12
  843.0 87.8 reduce-scatter.14

commit v2 on v1

v2 whole, which is shorter than its diff:
```python
import jax
import jax.numpy as jnp
from jax import lax
from jax.experimental import pallas as pl
from jax.experimental.pallas import tpu as pltpu
from jax.sharding import Mesh, PartitionSpec as P

QUERY_HEADS = 8
KEY_VALUE_HEADS = 4
HEAD_SIZE = 256

eps_norm = 1e-06
rope_base = 1000042.0
neg_large = -1e30
bf16 = jnp.bfloat16
f32 = jnp.float32


def rope_tables(slot_length, size):
    half_size = size // 2
    inv_freq = rope_base ** (-(jnp.arange(half_size, dtype=f32) * 2.0 / size))
    angles = jnp.arange(slot_length, dtype=f32)[:, None] * inv_freq[None, :]
    return (jnp.cos(angles), jnp.sin(angles))


def rotate(values, cos_b, sin_b):
    half = values.shape[-1] // 2
    a, b = values[..., :half], values[..., half:]
    return jnp.concatenate([a * cos_b - b * sin_b, b * cos_b + a * sin_b], axis=-1)


def rotate_back(grads, cos_b, sin_b):
    half = grads.shape[-1] // 2
    a, b = grads[..., :half], grads[..., half:]
    return jnp.concatenate([a * cos_b + b * sin_b, b * cos_b - a * sin_b], axis=-1)


def mm(left, right):
    return lax.dot_general(left, right, (((1,), (0,)), ((), ())), preferred_element_type=f32)


def mm_t(left, right):
    return lax.dot_general(left, right, (((1,), (1,)), ((), ())), preferred_element_type=f32)


def mm_rows(left, right):
    return lax.dot_general(left, right, (((0,), (0,)), ((), ())), preferred_element_type=f32)


DP = ("z", "core")
OVER_X = [(0, 1), (1, 0), (2, 3), (3, 2)]
OVER_Y = [(0, 2), (2, 0), (1, 3), (3, 1)]
OVER_CORE = [(0, 1), (1, 0)]


def send_x(v):
    return lax.ppermute(v, "mp", OVER_X)


def send_y(v):
    return lax.ppermute(v, "mp", OVER_Y)


def send_core(v):
    return lax.ppermute(v, "core", OVER_CORE)


def square():
    return lax.axis_size("mp") == 4


def after(value, *earlier):
    return lax.optimization_barrier((value,) + earlier)[0]


def relative_rows(v):
    if not square():
        return v
    me = lax.axis_index("mp")
    here = v.shape[0] // 4
    return jnp.concatenate(
        [lax.dynamic_slice_in_dim(v, jnp.bitwise_xor(me, m) * here, here, 0) for m in (0, 2, 1, 3)]
    )


def sequence_rows(v):
    if not square():
        return v
    me = lax.axis_index("mp")
    here = v.shape[0] // 4
    out = []
    for m in range(4):
        away = jnp.bitwise_xor(me, m)
        slot = (away % 2) * 2 + away // 2
        out.append(lax.dynamic_slice_in_dim(v, slot * here, here, 0))
    return jnp.concatenate(out)


def scatter_rows(blocks, hold=()):
    if not square():
        part = blocks(0, 4).astype(bf16)
        return lax.psum_scatter(part, "mp", scatter_dimension=0, tiled=True).astype(f32)
    far = blocks(2, 4)
    here = far.shape[0] // 2
    half = far.shape[1] // 2
    low = far.astype(bf16)
    if hold:
        low = after(low, *hold)
    p1 = send_x(low[here:, :half])
    q1 = send_y(low[here:, half:])
    p2 = send_x(low[:here, :half])
    near = blocks(0, 2)
    q2 = send_y(near[here:, half:].astype(bf16))
    q3 = send_y((near[here:, :half] + p1.astype(f32)).astype(bf16))
    p3 = send_x((far[:here, half:] + q1.astype(f32)).astype(bf16))
    own = near[:here]
    return jnp.concatenate(
        [
            own[:, :half] + p2.astype(f32) + q3.astype(f32),
            own[:, half:] + p3.astype(f32) + q2.astype(f32),
        ],
        axis=1,
    )


def assemble_kernel(slots_ref, own, x_a, x_b, y_a, y_b, d_a, d_b, out_ref):
    half = x_a.shape[1]
    step = pl.program_id(0)

    @pl.when(step == 0)
    def _():
        out_ref[...] = own[...].astype(out_ref.dtype)

    for i, (a, b) in enumerate([(y_a, y_b), (x_a, x_b), (d_a, d_b)]):

        @pl.when(step == i + 1)
        def _(a=a, b=b):
            out_ref[:, :half] = a[...].astype(out_ref.dtype)
            out_ref[:, half:] = b[...].astype(out_ref.dtype)


def assemble(slots, pieces, dtype):
    here, width = pieces[0].shape
    half = pieces[1].shape[1]
    return pl.pallas_call(
        assemble_kernel,
        name="assemble",
        grid_spec=pltpu.PrefetchScalarGridSpec(
            num_scalar_prefetch=1,
            grid=(4,),
            in_specs=[pl.BlockSpec((here, width), lambda i, s: (0, 0))]
            + [pl.BlockSpec((here, half), lambda i, s: (0, 0))] * 6,
            out_specs=pl.BlockSpec((here, width), lambda i, s: (s[i], 0)),
        ),
        out_shape=jax.ShapeDtypeStruct((4 * here, width), dtype),
        cost_estimate=pl.CostEstimate(flops=0, transcendentals=0, bytes_accessed=20 * here * width),
        compiler_params=pltpu.CompilerParams(vmem_limit_bytes=40 << 20),
    )(slots, *pieces)


def gather_rows(block, relative, dtype=bf16):
    if not square():
        return lax.all_gather(block, "mp", axis=0, tiled=True).astype(dtype)
    half = block.shape[1] // 2
    own_a, own_b = block[:, :half], block[:, half:]
    y_a = send_y(own_a)
    x_b = send_x(own_b)
    y_b = send_y(own_b)
    x_a = send_x(own_a)
    d_a = send_x(y_a)
    d_b = send_y(x_b)
    steps = jnp.arange(4, dtype=jnp.int32)
    if not relative:
        me = lax.axis_index("mp").astype(jnp.int32)
        steps = jnp.bitwise_xor(me, jnp.array([0, 2, 1, 3], jnp.int32))
    return assemble(steps, [block, x_a, x_b, y_a, y_b, d_a, d_b], dtype)


def sum_all(v):
    if not square() or lax.axis_size("z") != 4:
        return lax.psum(v, DP + ("mp",))
    v = v + send_x(v)
    v = v + send_y(v)
    v = v + send_core(v)
    v = v + lax.ppermute(v, "z", [(0, 1), (1, 0), (2, 3), (3, 2)])
    return v + lax.ppermute(v, "z", [(0, 3), (3, 0), (1, 2), (2, 1)])


def mask_block(first_row, block_rows, slots, seq_len):
    q_pos = first_row + jnp.arange(block_rows)
    k_pos = jnp.arange(slots)
    return (k_pos[None, :] <= q_pos[:, None]) & (k_pos[None, :] < seq_len)


def attend(queries, keys, values, seq_len, factor):
    slots = keys.shape[0]
    block_rows = min(512, slots)
    parts, totals = [], []
    for first_row in range(0, slots, block_rows):
        upto = first_row + block_rows
        raw = jnp.einsum(
            "qhd,kd->hqk", queries[first_row:upto], keys[:upto], preferred_element_type=f32
        )
        allowed = mask_block(first_row, block_rows, upto, seq_len)
        scores = jnp.where(allowed[None], raw * factor, neg_large)
        row_max = jnp.max(scores, axis=-1, keepdims=True)
        exps = jnp.exp(scores - row_max)
        total = jnp.sum(exps, axis=-1, keepdims=True)
        probs = (exps / total).astype(bf16)
        parts.append(
            jnp.einsum("hqk,kd->qhd", probs, values[:upto], preferred_element_type=f32).astype(bf16)
        )
        totals.append((row_max + jnp.log(total))[..., 0])
    return jnp.concatenate(parts, axis=0), jnp.concatenate(totals, axis=1)


def attend_back(queries, keys, values, grad_ctx, log_total, seq_len, factor):
    slots = keys.shape[0]
    block_rows = min(512, slots)
    dq_parts = []
    d_keys = jnp.zeros(keys.shape, f32)
    d_values = jnp.zeros(values.shape, f32)
    for first_row in range(0, slots, block_rows):
        upto = first_row + block_rows
        q_block = queries[first_row:upto]
        g_block = grad_ctx[first_row:upto]
        raw = jnp.einsum("qhd,kd->hqk", q_block, keys[:upto], preferred_element_type=f32)
        allowed = mask_block(first_row, block_rows, upto, seq_len)
        scores = jnp.where(allowed[None], raw * factor, neg_large)
        probs = jnp.exp(scores - log_total[:, first_row:upto, None])
        grad_p = jnp.einsum("qhd,kd->hqk", g_block, values[:upto], preferred_element_type=f32)
        inner = jnp.sum(probs * grad_p, axis=-1, keepdims=True)
        grad_s = (probs * (grad_p - inner) * factor).astype(bf16)
        dq_parts.append(
            jnp.einsum("hqk,kd->qhd", grad_s, keys[:upto], preferred_element_type=f32)
        )
        dk = jnp.einsum("hqk,qhd->kd", grad_s, q_block, preferred_element_type=f32)
        dv = jnp.einsum("hqk,qhd->kd", probs.astype(bf16), g_block, preferred_element_type=f32)
        d_keys = d_keys.at[:upto].add(dk)
        d_values = d_values.at[:upto].add(dv)
    return jnp.concatenate(dq_parts, axis=0), d_keys, d_values


def spread_heads(block):
    mp_size = lax.axis_size("mp")
    rows, n, heads, part = block.shape
    send = jnp.repeat(block, mp_size // heads, axis=2)
    got = lax.all_to_all(send, "mp", 2, 2, tiled=True)
    return got.reshape(rows, n * mp_size * part)


def collect_heads(block, heads):
    mp_size = lax.axis_size("mp")
    rows, n, size = block.shape
    part = size // mp_size
    got = lax.all_to_all(block.reshape(rows, n, mp_size, part), "mp", 2, 2, tiled=True)
    return jnp.sum(got.reshape(rows, n, heads, mp_size // heads, part).astype(f32), axis=3)


def gather_dp(block):
    return lax.all_gather(block, DP, axis=0, tiled=True)


def reduce_dp(block):
    return lax.psum_scatter(block, DP, scatter_dimension=0, tiled=True)


def gather_z(block):
    return lax.all_gather(block, "z", axis=0, tiled=True)


def reduce_z(block):
    return lax.psum_scatter(block, "z", scatter_dimension=0, tiled=True)


def to_core(block):
    rows, n, cols = block.shape
    core = lax.axis_index("core")
    m = cols // 2
    own = lax.dynamic_slice_in_dim(block, core * m, m, 2).reshape(rows, n * m)
    away = lax.dynamic_slice_in_dim(block, (1 - core) * m, m, 2).reshape(rows, n * m)
    got = send_core(away)
    return jnp.concatenate([jnp.where(core == 0, own, got), jnp.where(core == 0, got, own)])


def from_core(block, n):
    rows = block.shape[0] // 2
    m = block.shape[1] // n
    core = lax.axis_index("core")
    own = lax.dynamic_slice_in_dim(block, core * rows, rows, 0)
    away = lax.dynamic_slice_in_dim(block, (1 - core) * rows, rows, 0)
    got = send_core(away)
    low, high = jnp.where(core == 0, own, got), jnp.where(core == 0, got, own)
    return [
        jnp.concatenate([low[:, i * m : (i + 1) * m], high[:, i * m : (i + 1) * m]], axis=1)
        for i in range(n)
    ]


def ffn_forward_kernel(mine_ref, away_ref, g_ref, u_ref, hidden_ref, factor_ref):
    def run(h_ref):
        h = h_ref[...]
        gate = jnp.dot(h, g_ref[...], preferred_element_type=f32)
        up = jnp.dot(h, u_ref[...], preferred_element_type=f32)
        sig = 1.0 / (1.0 + jnp.exp(-gate))
        silu = gate * sig
        hidden_ref[...] = (silu * up).astype(bf16)
        factor_ref[0] = (up * sig * (1.0 + gate - silu)).astype(bf16)
        factor_ref[1] = silu.astype(bf16)

    pl.when(pl.program_id(0) == 0)(lambda: run(mine_ref))
    pl.when(pl.program_id(0) == 1)(lambda: run(away_ref))


def tile(size, most):
    while size % most:
        most //= 2
    return most


def ffn_forward(mine, away, w_gu):
    rows, width = mine.shape
    ff = w_gu.shape[1] // 2
    tn = tile(ff, 256)
    return pl.pallas_call(
        ffn_forward_kernel,
        name="ffn_forward",
        grid=(2, ff // tn),
        in_specs=[
            pl.BlockSpec((rows, width), lambda i, j: (0, 0)),
            pl.BlockSpec((rows, width), lambda i, j: (0, 0)),
            pl.BlockSpec((width, tn), lambda i, j: (0, j)),
            pl.BlockSpec((width, tn), lambda i, j: (0, j + ff // tn)),
        ],
        out_specs=[
            pl.BlockSpec((rows, tn), lambda i, j: (i, j)),
            pl.BlockSpec((2, rows, tn), lambda i, j: (0, i, j)),
        ],
        out_shape=[
            jax.ShapeDtypeStruct((2 * rows, ff), bf16),
            jax.ShapeDtypeStruct((2, 2 * rows, ff), bf16),
        ],
        cost_estimate=pl.CostEstimate(
            flops=8 * rows * width * ff,
            transcendentals=2 * rows * ff,
            bytes_accessed=4 * (rows * width + width * ff + 3 * rows * ff),
        ),
        compiler_params=pltpu.CompilerParams(vmem_limit_bytes=56 << 20),
    )(mine, away, w_gu, w_gu)


def rows_product_kernel(mine_ref, away_ref, right_mine_ref, right_away_ref, out_ref):
    def dot(left, right):
        return lax.dot_general(
            left[...], right[...], (((0,), (0,)), ((), ())), preferred_element_type=f32
        )

    out_ref[...] = (dot(mine_ref, right_mine_ref) + dot(away_ref, right_away_ref)).astype(bf16)


def rows_product(mine, away, right):
    rows, width = mine.shape
    cols = right.shape[1]
    tm = tile(width, 256)
    return pl.pallas_call(
        rows_product_kernel,
        name="rows_product",
        grid=(width // tm,),
        in_specs=[
            pl.BlockSpec((rows, tm), lambda i: (0, i)),
            pl.BlockSpec((rows, tm), lambda i: (0, i)),
            pl.BlockSpec((rows, cols), lambda i: (0, 0)),
            pl.BlockSpec((rows, cols), lambda i: (1, 0)),
        ],
        out_specs=pl.BlockSpec((tm, cols), lambda i: (i, 0)),
        out_shape=jax.ShapeDtypeStruct((width, cols), bf16),
        cost_estimate=pl.CostEstimate(
            flops=4 * rows * width * cols,
            transcendentals=0,
            bytes_accessed=4 * rows * (width + cols) + 2 * width * cols,
        ),
        compiler_params=pltpu.CompilerParams(vmem_limit_bytes=56 << 20),
    )(mine, away, right, right)


def ffn_backward_kernel(grad_ref, d_ref, factor_ref, out_ref, d_hidden_ref):
    @pl.when(pl.program_id(2) == 0)
    def _():
        d_hidden_ref[...] = jnp.dot(grad_ref[...], d_ref[...], preferred_element_type=f32)

    out_ref[...] = (d_hidden_ref[...] * factor_ref[0].astype(f32)).astype(bf16)


def ffn_backward(grad, w_d, factors):
    rows, width = grad.shape
    ff = w_d.shape[1]
    tm, tn = tile(rows, 1024), tile(ff, 512)
    return pl.pallas_call(
        ffn_backward_kernel,
        name="ffn_backward",
        grid=(rows // tm, ff // tn, 2),
        in_specs=[
            pl.BlockSpec((tm, width), lambda i, j, k: (i, 0)),
            pl.BlockSpec((width, tn), lambda i, j, k: (0, j)),
            pl.BlockSpec((1, tm, tn), lambda i, j, k: (k, i, j)),
        ],
        out_specs=pl.BlockSpec((tm, tn), lambda i, j, k: (i, j + k * (ff // tn))),
        out_shape=jax.ShapeDtypeStruct((rows, 2 * ff), bf16),
        scratch_shapes=[pltpu.VMEM((tm, tn), f32)],
        cost_estimate=pl.CostEstimate(
            flops=2 * rows * width * ff, transcendentals=0, bytes_accessed=2 * (rows * width + width * ff + 4 * rows * ff)
        ),
        compiler_params=pltpu.CompilerParams(vmem_limit_bytes=56 << 20),
    )(grad, w_d, factors)


def local(
    x_in,
    lengths,
    gain_attn,
    query_weight,
    key_projection_matrix,
    value_projection_matrix,
    out_weight,
    gain_ffn,
    gate_weight,
    up_weight,
    down_weight,
    cotangent,
):
    _, slots, width = x_in.shape
    mp_size = lax.axis_size("mp")
    me = lax.axis_index("mp")
    heads_here = query_weight.shape[1] // HEAD_SIZE
    q_cols = query_weight.shape[1]
    factor = HEAD_SIZE ** (-0.5)
    here = slots // mp_size
    quarter = slots // 4
    seq_len = lengths[0]
    cos_t, sin_t = rope_tables(slots, HEAD_SIZE)

    def own_rows(v):
        return lax.dynamic_slice_in_dim(v, me * here, here, 0)

    w_o = gather_dp(out_weight.T)
    kv_block = spread_heads(jnp.stack([key_projection_matrix, value_projection_matrix], axis=1))
    w_qkv = gather_dp(jnp.concatenate([query_weight, kv_block], axis=1))
    gains = lax.all_gather(jnp.stack([gain_attn, gain_ffn]), DP, axis=1, tiled=True).astype(f32)
    g_attn, g_ffn = gains[0], gains[1]
    ffn_block = to_core(jnp.stack([gate_weight, up_weight, down_weight.T], axis=1))
    ff = ffn_block.shape[1] // 3
    w_gu = gather_z(ffn_block[:, : 2 * ff])
    w_d = gather_z(ffn_block[:, 2 * ff :])

    tok = x_in[0].astype(f32)
    r1 = lax.rsqrt(jnp.mean(tok * tok, axis=-1, keepdims=True) + eps_norm)
    h_attn = (tok * r1 * g_attn).astype(bf16)
    valid = (jnp.arange(slots)[:, None] < seq_len).astype(bf16)
    grad_low = cotangent[0] * valid
    grad_mine = relative_rows(grad_low)
    grad_all = jnp.concatenate([grad_mine, send_core(grad_mine)])
    cos_h, sin_h = cos_t[:, None, :], sin_t[:, None, :]
    qkv = mm(h_attn, w_qkv)
    queries = rotate(
        qkv[:, :q_cols].reshape(slots, heads_here, HEAD_SIZE), cos_h, sin_h
    ).astype(bf16)
    keys = rotate(qkv[:, q_cols : q_cols + HEAD_SIZE], cos_t, sin_t).astype(bf16)
    values = qkv[:, q_cols + HEAD_SIZE :].astype(bf16)
    context, log_total = attend(queries, keys, values, seq_len, factor)
    context = relative_rows(context.reshape(slots, q_cols))

    attn_rows = scatter_rows(lambda i, j: mm_t(context[i * quarter : j * quarter], w_o))
    tok_here = own_rows(x_in[0]).astype(f32)
    mid = tok_here + attn_rows
    r2 = lax.rsqrt(jnp.mean(mid * mid, axis=-1, keepdims=True) + eps_norm)
    n2 = mid * r2
    h_mine = gather_rows((n2 * g_ffn).astype(bf16), True)
    h_away = send_core(h_mine)

    hidden, factors = ffn_forward(h_mine, h_away, w_gu)
    down_grad = mm_rows(grad_all, hidden).astype(bf16)
    down_out = reduce_z(down_grad)
    d_gu = ffn_backward(grad_all, w_d, factors)

    def with_core(left, product):
        away_high = send_core(product(left[slots + 2 * quarter :]).astype(bf16)).astype(f32)
        away_low = send_core(product(left[slots : slots + 2 * quarter]).astype(bf16)).astype(f32)

        def blocks(i, j):
            mine = product(left[i * quarter : j * quarter])
            if j - i == 4:
                return mine + jnp.concatenate([away_low, away_high])
            return mine + (away_high if i else away_low)

        return blocks

    d_h2 = scatter_rows(with_core(d_gu, lambda v: mm_t(v, w_gu)))
    gu_out = reduce_z(rows_product(h_mine, h_away, d_gu))

    gain_ffn_part = jnp.sum(d_h2 * n2, axis=0)
    e2 = d_h2 * g_ffn
    g1 = own_rows(grad_low).astype(f32) + r2 * (e2 - n2 * jnp.mean(e2 * n2, axis=-1, keepdims=True))
    g1_low = gather_rows(g1.astype(bf16), True)

    ffn_rows = scatter_rows(with_core(hidden, lambda v: mm_t(v, w_d)), hold=(g1_low,))
    layer_out = gather_rows((mid + ffn_rows).astype(bf16), False)

    d_context = sequence_rows(mm(g1_low, w_o).astype(bf16)).reshape(slots, heads_here, HEAD_SIZE)
    out_out = reduce_dp(mm_rows(g1_low, context).astype(bf16))
    dq, dk, dv = attend_back(queries, keys, values, d_context, log_total, seq_len, factor)
    d_q = rotate_back(dq, cos_h, sin_h).reshape(slots, q_cols)
    d_qkv = jnp.concatenate([d_q, rotate_back(dk, cos_t, sin_t), dv], axis=1).astype(bf16)
    qkv_out = reduce_dp(mm_rows(h_attn, d_qkv).astype(bf16))

    d_qkv_rel = relative_rows(d_qkv)
    d_h1 = scatter_rows(lambda i, j: mm_t(d_qkv_rel[i * quarter : j * quarter], w_qkv))
    r1_here = own_rows(r1)
    n1 = tok_here * r1_here
    gain_attn_part = jnp.sum(d_h1 * n1, axis=0)
    e1 = d_h1 * g_attn
    grad_in = g1 + r1_here * (e1 - n1 * jnp.mean(e1 * n1, axis=-1, keepdims=True))
    grad_input = gather_rows(grad_in.astype(bf16), False, f32)

    rows_here = gain_attn.shape[0]

    def gain_grad(part):
        total = sum_all(part.reshape(-1, 128)).reshape(-1)
        return lax.dynamic_slice_in_dim(total, lax.axis_index(DP) * rows_here, rows_here, 0)

    gate_out, up_out = from_core(gu_out, 2)
    (down_out,) = from_core(down_out, 1)
    kv_grad = collect_heads(
        qkv_out[:, q_cols:].reshape(rows_here, 2, HEAD_SIZE), KEY_VALUE_HEADS
    )
    return (
        layer_out[None],
        grad_input[None],
        gain_grad(gain_attn_part),
        qkv_out[:, :q_cols].astype(f32),
        kv_grad[:, 0],
        kv_grad[:, 1],
        out_out.T.astype(f32),
        gain_grad(gain_ffn_part),
        gate_out.astype(f32),
        up_out.astype(f32),
        down_out.T.astype(f32),
    )


def solution(mesh):
    dp_size, mp_size = mesh.shape["dp"], mesh.shape["mp"]
    split = Mesh(mesh.devices.reshape(dp_size // 2, 2, mp_size), ("z", "core", "mp"))
    return jax.shard_map(
        local,
        mesh=split,
        in_specs=(
            P(DP, None, None),
            P(DP),
            P(DP),
            P(DP, "mp"),
            P(DP, None, "mp"),
            P(DP, None, "mp"),
            P("mp", DP),
            P(DP),
            P(DP, "mp"),
            P(DP, "mp"),
            P("mp", DP),
            P(DP, None, None),
        ),
        out_specs=(
            P(DP, None, None),
            P(DP, None, None),
            P(DP),
            P(DP, "mp"),
            P(DP, None, "mp"),
            P(DP, None, "mp"),
            P("mp", DP),
            P(DP),
            P(DP, "mp"),
            P(DP, "mp"),
            P("mp", DP),
        ),
        check_vma=False,
    )
```

time: 945 us -> 751 us (0.79)
  waiting for transfers between devices: 440 us -> 317 us
  Pallas kernels: 0 us -> 89 us
  matrix products: 233 us -> 152 us
  blocking collectives: 75.8 us -> 12.2 us
  local copies, waits for them, and re-layouts: 65.4 us -> 44.8 us
  starting transfers between devices: 47 us -> 64.1 us
  other arithmetic: 63.3 us -> 48.9 us
    reduce_scatter x6 -> x4, waiting for transfers between devices: 118 us -> 0.03 us  [the longest x2 0.02 us: reduce_dp(): return lax.psum_scatter(block, DP, scatter_dimension=0, tiled=True)]
    pallas_call x0 -> x7, Pallas kernels: none -> 89 us  [the longest x1 26.1 us: ffn_forward(): pl.pallas_call(ffn_forward_kernel, name='ffn_forward', grid=(2, ff // tn)...]
    dot_general x6 -> x2, matrix products: 64.1 us -> 11.7 us  [mm(): lax.dot_general(left, right, (((1,), (0,)), ((), ())), preferred_element_...]
    psum x1 -> x0, blocking collectives: 45.3 us -> none  [local(): lax.psum(jnp.stack([gain_attn_part, gain_ffn_part]), ('dp', 'mp'))]
    all_gather x6 -> x4, waiting for transfers between devices: 149 us -> 117 us  [the longest x2 100 us: gather_z(): return lax.all_gather(block, 'z', axis=0, tiled=True)]
    dot_general x6 -> x3, matrix products: 57.4 us -> 28.9 us  [mm_rows(): lax.dot_general(left, right, (((0,), (0,)), ((), ())), preferred_element_...]
    unnamed x144 -> x113, local copies, waits for them, and re-layouts: 37.5 us -> 16.1 us
    ppermute x32 -> x67, waiting for transfers between devices: 169 us -> 190 us  [the longest x26 114 us: send_y(): return lax.ppermute(v, 'mp', OVER_Y)]
  transfers between devices with their start and end apart: 46 -> 77, of which waited for: 32 -> 43; matrix products, arithmetic and copies ran while one was open for 29% -> 31% of each run, Pallas kernels for 0% -> 12%
where the time goes in v2:
time: 751 us; the launch traced here: 744 us
  waiting for transfers between devices  317 us (42%)
  matrix products  152 us (20%)
  Pallas kernels  89 us (12%)
  starting transfers between devices  64.1 us (9%)
  other arithmetic  48.9 us (7%)
  local copies, waits for them, and re-layouts  44.8 us (6%)
  between operations  16.3 us (2%)
  blocking collectives  12.2 us (2%)
    ppermute x26, waiting for transfers between devices, send_y(): return lax.ppermute(v, 'mp', OVER_Y)  114 us
    all_gather x2, waiting for transfers between devices, gather_z(): return lax.all_gather(block, 'z', axis=0, tiled=True)  100 us
    ppermute x26, waiting for transfers between devices, send_x(): return lax.ppermute(v, 'mp', OVER_X)  67.2 us
    dot_general x12, matrix products, mm_t(): lax.dot_general(left, right, (((1,), (1,)), ((), ())), preferred_element_...  62.2 us
    dot_general x3, matrix products, mm_rows(): lax.dot_general(left, right, (((0,), (0,)), ((), ())), preferred_element_...  28.9 us
    ppermute x26, starting transfers between devices, send_x(): return lax.ppermute(v, 'mp', OVER_X)  27.8 us
    pallas_call x1, Pallas kernels, ffn_forward(): pl.pallas_call(ffn_forward_kernel, name='ffn_forward', grid=(2, ff // tn)...  26.1 us
    ppermute x26, starting transfers between devices, send_y(): return lax.ppermute(v, 'mp', OVER_Y)  25.5 us
  transfers between devices with their start and end apart: 77, of which 43 were waited for; matrix products, arithmetic and copies ran while one was open for 31% of the time, Pallas kernels for 12%

profile of v2, /device:TPU:0, one launch (start us, length us, event | category | flops | bytes accessed | tf_op | source)
XLA Modules:
  0.0 743.9 jit_solution(447917336922394780)
XLA Ops:
  30.3 12.2 %all_gather.15 = bf16[2,2048]{1,0:T(2,128)(2,1)S(1)} all-gather(bf16[2,256]{1,0:T(2,128)(2,1)S(1)} %pad_maximum_fusion.17), channel_id=1, replica_groups=mesh['z'=4,'core'=2,'mp'=4] {'z','core'}, dimensions={1}, use_global_device_ids=true | all-gather | bytes 9216 | tf_op jit(solution)/shard_map/all_gather | solution.py:448
  52.0 16.5 %all-gather.5.cloned.1.call-done = bf16[2048,1024]{0,1:T(8,128)(2,1)} async-done(((bf16[256,1024]{0,1:T(8,128)(2,1)}), bf16[2048,1024]{0,1:T(8,128)(2,1)}) %all-gather.5.cloned.1.call-update) | async-done | bytes 4194320 | tf_op jit(solution)/shard_map/all_gather | solution.py:261
  68.5 9.4 %fusion.162 = (bf16[1024,1024]{0,1:T(8,128)(2,1)}, f32[1024,1024]{0,1:T(8,128)S(1)}) fusion(bf16[2048,1024]{0,1:T(8,128)(2,1)} %all-gather.5.cloned.1.call-done, bf16[1,1024,2048]{2,1,0:T(8,128)(2,1)} %param.26, f32[2048]{0:T(1024)S(1)} %bitcast.216, f32[1024]{0:T(1024)S(1)} %add_rsqrt_fusion), kind=kOutput, calls=%fused_computation.291 | convolution fusion | flops 4304404480 | bytes 14692352 | tf_op jit(solution)/shard_map/dot_general | solution.py:39
  108.7 8.5 %collective-permute-done.3 = bf16[256,1024]{1,0:T(8,128)(2,1)S(1)} collective-permute-done((bf16[256,1024]{1,0:T(8,128)(2,1)S(1)}, bf16[256,1024]{1,0:T(8,128)(2,1)S(1)}, u32[]{:S(2)}, u32[]{:S(2)}) %collective-permute-start.3) | collective-permute-done | bytes 524320 | tf_op jit(solution)/shard_map/ppermute | solution.py:61
  120.8 7.7 %collective-permute-done.5 = bf16[256,1024]{1,0:T(8,128)(2,1)S(1)} collective-permute-done((bf16[256,1024]{1,0:T(8,128)(2,1)S(1)}, bf16[256,1024]{1,0:T(8,128)(2,1)S(1)}, u32[]{:S(2)}, u32[]{:S(2)}) %collective-permute-start.5) | collective-permute-done | bytes 524320 | tf_op jit(solution)/shard_map/ppermute | solution.py:61
  130.1 10.2 %collective-permute-done.4 = bf16[256,1024]{1,0:T(8,128)(2,1)S(1)} collective-permute-done((bf16[256,1024]{1,0:T(8,128)(2,1)S(1)}, bf16[256,1024]{1,0:T(8,128)(2,1)S(1)}, u32[]{:S(2)}, u32[]{:S(2)}) %collective-permute-start.4) | collective-permute-done | bytes 524320 | tf_op jit(solution)/shard_map/ppermute | solution.py:57
  147.5 10.4 %collective-permute-done.7.x_b = bf16[256,1024]{1,0:T(8,128)(2,1)S(1)} collective-permute-done((bf16[256,1024]{1,0:T(8,128)(2,1)S(1)}, bf16[256,1024]{1,0:T(8,128)(2,1)S(1)}, u32[]{:S(2)}, u32[]{:S(2)}) %collective-permute-start.7) | collective-permute-done | bytes 524320 | tf_op jit(solution)/shard_map/ppermute | solution.py:57
  162.2 8.4 %collective-permute-done.9.y_b = bf16[256,1024]{1,0:T(8,128)(2,1)S(1)} collective-permute-done((bf16[256,1024]{1,0:T(8,128)(2,1)S(1)}, bf16[256,1024]{1,0:T(8,128)(2,1)S(1)}, u32[]{:S(2)}, u32[]{:S(2)}) %collective-permute-start.9) | collective-permute-done | bytes 524320 | tf_op jit(solution)/shard_map/ppermute | solution.py:61
  170.6 9.1 %collective-permute-done.11.d_b = bf16[256,1024]{1,0:T(8,128)(2,1)S(1)} collective-permute-done((bf16[256,1024]{1,0:T(8,128)(2,1)S(1)}, bf16[256,1024]{1,0:T(8,128)(2,1)S(1)}, u32[]{:S(2)}, u32[]{:S(2)}) %collective-permute-start.11) | collective-permute-done | bytes 524320 | tf_op jit(solution)/shard_map/ppermute | solution.py:61
  190.8 59.2 %all-gather.9.cloned.1.call-done.g_ref.u_ref = bf16[2048,2048]{1,0:T(8,128)(2,1)} async-done(((bf16[512,2048]{1,0:T(8,128)(2,1)}), bf16[2048,2048]{1,0:T(8,128)(2,1)}) %all-gather.9.cloned.1.call-update) | async-done | bytes 8388624 | tf_op jit(solution)/shard_map/all_gather | solution.py:269
  250.1 26.1 %ffn_forward.1 = (bf16[2048,1024]{1,0:T(8,128)(2,1)}, bf16[2,2048,1024]{2,1,0:T(8,128)(2,1)}) custom-call(bf16[1024,2048]{1,0:T(8,128)(2,1)} %assemble.4.mine_ref, bf16[1024,2048]{1,0:T(8,128)(2,1)} %collective-permute-done.12.away_ref, bf16[2048,2048]{1,0:T(8,128)(2,1)} %all-gather.9.cloned.1.call-done.g_ref.u_ref, ...), custom_call_target="tpu_custom_call" | custom-call | flops 17179869184 | bytes 29360128 | tf_op jit(solution)/shard_map/ffn_forward/pallas_call | solution.py:325
  276.2 14.0 %convolution_convert_fusion.1 = bf16[2048,1024]{1,0:T(8,128)(2,1)} fusion(bf16[2048,2048]{1,0:T(8,128)(2,1)} %constant_dynamic-update-slice_fusion.grad_ref, bf16[2048,1024]{1,0:T(8,128)(2,1)} %get-tuple-element.78), kind=kOutput, calls=%fused_computation.23 | convolution fusion | flops 8592031744 | bytes 16777216 | tf_op jit(solution)/shard_map/dot_general | solution.py:47
  290.3 40.8 %all-gather.11.cloned.1.call-done.d_ref = bf16[2048,1024]{1,0:T(8,128)(2,1)} async-done(((bf16[512,1024]{1,0:T(8,128)(2,1)}), bf16[2048,1024]{1,0:T(8,128)(2,1)}) %all-gather.11.cloned.1.call-update) | async-done | bytes 4194320 | tf_op jit(solution)/shard_map/all_gather | solution.py:269
  331.1 23.9 %ffn_backward.1.right_mine_ref.right_away_ref = bf16[2048,2048]{1,0:T(8,128)(2,1)} custom-call(bf16[2048,2048]{1,0:T(8,128)(2,1)} %constant_dynamic-update-slice_fusion.grad_ref, bf16[2048,1024]{1,0:T(8,128)(2,1)} %all-gather.11.cloned.1.call-done.d_ref, bf16[2,2048,1024]{2,1,0:T(8,128)(2,1)} %get-tuple-element.79.factor_ref), custom_call_target="tpu_custom_call" | custom-call | flops 8589934592 | bytes 29360128 | tf_op jit(solution)/shard_map/ffn_backward/pallas_call | solution.py:398
  355.0 23.9 %rows_product.1 = bf16[2048,2048]{1,0:T(8,128)(2,1)} custom-call(bf16[1024,2048]{1,0:T(8,128)(2,1)} %assemble.4.mine_ref, bf16[1024,2048]{1,0:T(8,128)(2,1)} %collective-permute-done.12.away_ref, bf16[2048,2048]{1,0:T(8,128)(2,1)} %ffn_backward.1.right_mine_ref.right_away_ref, bf16[2048,2048]{1,0:T(8,128)(2,1)} %ffn_backward.1.right_mine_ref.right_away_ref), custom_call_target="tpu_custom_call" | custom-call | flops 17179869184 | bytes 25165824 | tf_op jit(solution)/shard_map/rows_product/pallas_call | solution.py:365
  379.1 9.9 %convolution_convert_fusion.5 = bf16[512,2048]{1,0:T(8,128)(2,1)} fusion(bf16[2048,2048]{1,0:T(8,128)(2,1)} %all-gather.9.cloned.1.call-done.g_ref.u_ref, bf16[2048,2048]{1,0:T(8,128)(2,1)} %ffn_backward.1.right_mine_ref.right_away_ref), kind=kOutput, calls=%fused_computation.32 | convolution fusion | flops 4296015872 | bytes 12582912 | tf_op jit(solution)/shard_map/dot_general | solution.py:43
  389.1 8.6 %convolution_convert_fusion.6 = bf16[512,2048]{1,0:T(8,128)(2,1)S(1)} fusion(bf16[2048,2048]{1,0:T(8,128)(2,1)} %all-gather.9.cloned.1.call-done.g_ref.u_ref, bf16[2048,2048]{1,0:T(8,128)(2,1)} %ffn_backward.1.right_mine_ref.right_away_ref), kind=kOutput, calls=%fused_computation.33 | convolution fusion | flops 4296015872 | bytes 12582912 | tf_op jit(solution)/shard_map/dot_general | solution.py:43
  398.3 9.1 %fusion.166 = (bf16[512,2048]{1,0:T(8,128)(2,1)S(1)}, f32[512,2048]{1,0:T(8,128)S(1)}) fusion(bf16[512,2048]{1,0:T(8,128)(2,1)} %collective-permute-done.18, bf16[2048,2048]{1,0:T(8,128)(2,1)} %all-gather.9.cloned.1.call-done.g_ref.u_ref, bf16[2048,2048]{1,0:T(8,128)(2,1)} %ffn_backward.1.right_mine_ref.right_away_ref), kind=kOutput, calls=%fused_computation.295 | convolution fusion | flops 4298113024 | bytes 18874368 | tf_op jit(solution)/shard_map/dot_general | solution.py:43
  410.7 8.0 %convert_add_fusion.1 = f32[512,2048]{1,0:T(8,128)S(1)} fusion(bf16[512,2048]{1,0:T(8,128)(2,1)S(1)} %collective-permute-done.17, bf16[2048,2048]{1,0:T(8,128)(2,1)} %all-gather.9.cloned.1.call-done.g_ref.u_ref, bf16[2048,2048]{1,0:T(8,128)(2,1)} %ffn_backward.1.right_mine_ref.right_away_ref), kind=kOutput, calls=%fused_computation.17 | convolution fusion | flops 4297064448 | bytes 16777216 | tf_op jit(solution)/shard_map/dot_general | solution.py:43
  435.3 10.0 %collective-permute-done.23 = bf16[256,1024]{1,0:T(8,128)(2,1)S(1)} collective-permute-done((bf16[256,1024]{1,0:T(8,128)(2,1)S(1)}, bf16[256,1024]{1,0:T(8,128)(2,1)S(1)}, u32[]{:S(2)}, u32[]{:S(2)}) %collective-permute-start.23) | collective-permute-done | bytes 524320 | tf_op jit(solution)/shard_map/ppermute | solution.py:57
  456.8 8.9 %collective-permute-done.61 = f32[16,128]{1,0:T(8,128)S(1)} collective-permute-done((f32[16,128]{1,0:T(8,128)S(1)}, f32[16,128]{1,0:T(8,128)S(1)}, u32[]{:S(2)}, u32[]{:S(2)}) %collective-permute-start.61) | collective-permute-done | bytes 8224 | tf_op jit(solution)/shard_map/ppermute | solution.py:61
  479.3 6.3 collective-permute-done.30.d_b
  494.4 6.3 convolution_convert_fusion.2
  521.8 9.5 %fusion.45 = f32[512,2,256]{2,0,1:T(8,128)} fusion(f32[1024,512,2]{1,0,2:T(8,128)} %fusion.118, f32[2,512,1024]{1,2,0:T(8,128)} %copy-done.18, f32[2,512]{1,0:T(2,128)S(1)} %log_add_fusion, bf16[1024,128]{0,1:T(8,128)(2,1)S(1)} %copy-done.38, bf16[1024,128]{0,1:T(8,128)(2,1)S(1)} %copy-done.40), kind=kOutput, calls=%fused_computation.90 | convolution fusion | flops 545261568 | bytes 9965568 | tf_op jit(solution)/shard_map/hqk,kd->qhd/dot_general | solution.py:235
  531.3 9.7 %fusion.47 = f32[1024,256]{0,1:T(8,128)} fusion(f32[1024,512,2]{1,0,2:T(8,128)} %fusion.118, f32[2,512,1024]{1,2,0:T(8,128)} %copy-done.18, f32[2,512]{1,0:T(2,128)S(1)} %log_add_fusion, f32[512,256]{0,1:T(8,128)} %fusion.57, bf16[1024,2,128]{2,0,1:T(8,128)(2,1)} %copy-done.34, bf16[1024,2,128]{2,0,1:T(8,128)(2,1)} %copy-done.33), kind=kOutput, calls=%fused_computation.92 | convolution fusion | flops 545523712 | bytes 11014144 | tf_op jit(solution)/shard_map/hqk,qhd->kd/dot_general | solution.py:237
  553.1 8.5 %convolution_convert_fusion = bf16[2048,1024]{1,0:T(8,128)(2,1)} fusion(bf16[1,1024,2048]{2,1,0:T(8,128)(2,1)S(1)} %copy-done.6, f32[2048]{0:T(1024)S(1)} %bitcast.217, f32[1024]{0:T(1024)S(1)} %add_rsqrt_fusion, bf16[1024,256]{0,1:T(8,128)(2,1)S(1)} %fusion.51, bf16[1024,128]{0,1:T(8,128)(2,1)S(1)} %get-tuple-element.182, ...), kind=kOutput, calls=%fused_computation.22 | convolution fusion | flops 4313841664 | bytes 10498048 | tf_op jit(solution)/shard_map/dot_general | solution.py:47
  579.7 14.1 %collective-permute-done.46 = bf16[256,1024]{1,0:T(8,128)(2,1)S(1)} collective-permute-done((bf16[256,1024]{1,0:T(8,128)(2,1)S(1)}, bf16[256,1024]{1,0:T(8,128)(2,1)S(1)}, u32[]{:S(2)}, u32[]{:S(2)}) %collective-permute-start.46) | collective-permute-done | bytes 524320 | tf_op jit(solution)/shard_map/ppermute | solution.py:61
  598.7 6.3 collective-permute-done.48
  610.1 9.8 %collective-permute-done.47 = bf16[256,1024]{1,0:T(8,128)(2,1)S(1)} collective-permute-done((bf16[256,1024]{1,0:T(8,128)(2,1)S(1)}, bf16[256,1024]{1,0:T(8,128)(2,1)S(1)}, u32[]{:S(2)}, u32[]{:S(2)}) %collective-permute-start.47) | collective-permute-done | bytes 524320 | tf_op jit(solution)/shard_map/ppermute | solution.py:57
  655.3 9.2 %collective-permute-done.39.y_a = bf16[256,1024]{1,0:T(8,128)(2,1)} collective-permute-done((bf16[256,1024]{1,0:T(8,128)(2,1)}, bf16[256,1024]{1,0:T(8,128)(2,1)}, u32[]{:S(2)}, u32[]{:S(2)}) %collective-permute-start.39) | collective-permute-done | bytes 524320 | tf_op jit(solution)/shard_map/ppermute | solution.py:61
  666.6 8.3 %collective-permute-done.50.x_b = bf16[256,1024]{1,0:T(8,128)(2,1)} collective-permute-done((bf16[256,1024]{1,0:T(8,128)(2,1)}, bf16[256,1024]{1,0:T(8,128)(2,1)}, u32[]{:S(2)}, u32[]{:S(2)}) %collective-permute-start.50) | collective-permute-done | bytes 524320 | tf_op jit(solution)/shard_map/ppermute | solution.py:57
  676.6 10.4 %collective-permute-done.42.d_b = bf16[256,1024]{1,0:T(8,128)(2,1)} collective-permute-done((bf16[256,1024]{1,0:T(8,128)(2,1)S(1)}, bf16[256,1024]{1,0:T(8,128)(2,1)}, u32[]{:S(2)}, u32[]{:S(2)}) %collective-permute-start.42) | collective-permute-done | bytes 524320 | tf_op jit(solution)/shard_map/ppermute | solution.py:61
  (393 shorter events, 294.3 us)
Async XLA Ops:
  14.1 54.4 %all-gather.5.cloned.1.call-start = ((), (), s32[]{:S(2)}) async-start(), calls=%async_computation.6 | async-start | bytes 4718592 | tf_op jit(solution)/shard_map/all_gather | solution.py:261
  20.4 78.8 %all-gather.7.cloned.1.call-start = ((), (), s32[]{:S(2)}) async-start(), calls=%async_computation.7 | async-start | bytes 2359296 | tf_op jit(solution)/shard_map/all_gather | solution.py:261
  21.1 228.9 %all-gather.9.cloned.1.call-start = ((), (), s32[]{:S(2)}) async-start(), calls=%async_computation.8 | async-start | bytes 10485760 | tf_op jit(solution)/shard_map/all_gather | solution.py:269
  50.8 280.3 %all-gather.11.cloned.1.call-start = ((), (), s32[]{:S(2)}) async-start(), calls=%async_computation.9 | async-start | bytes 5242880 | tf_op jit(solution)/shard_map/all_gather | solution.py:269
  107.5 22.6 %collective-permute-start = (bf16[256,1024]{1,0:T(8,128)(2,1)S(1)}, bf16[256,1024]{1,0:T(8,128)(2,1)S(1)}, u32[]{:S(2)}, u32[]{:S(2)}) collective-permute-start(bf16[256,1024]{1,0:T(8,128)(2,1)S(1)} %get-tuple-element.174), channel_id=1, source_target_pairs={{0,1},{1,0},{2,3},{3,2},{4,5},{5,4},{6,7},{7,6},{8,9},{9,8},{10,11... | collective-permute-start | bytes 1572872 | tf_op jit(solution)/shard_map/ppermute | solution.py:57
  117.4 23.0 %collective-permute-start.4 = (bf16[256,1024]{1,0:T(8,128)(2,1)S(1)}, bf16[256,1024]{1,0:T(8,128)(2,1)S(1)}, u32[]{:S(2)}, u32[]{:S(2)}) collective-permute-start(bf16[256,1024]{1,0:T(8,128)(2,1)S(1)} %fusion.75), channel_id=1, source_target_pairs={{0,1},{1,0},{2,3},{3,2},{4,5},{5,4},{6,7},{7,6},{8,9},{9,8},{10,11... | collective-permute-start | bytes 1572872 | tf_op jit(solution)/shard_map/ppermute | solution.py:57
  145.4 25.2 %collective-permute-start.9 = (bf16[256,1024]{1,0:T(8,128)(2,1)S(1)}, bf16[256,1024]{1,0:T(8,128)(2,1)S(1)}, u32[]{:S(2)}, u32[]{:S(2)}) collective-permute-start(bf16[256,1024]{1,0:T(8,128)(2,1)S(1)} %get-tuple-element.197), channel_id=1, source_target_pairs={{0,2},{2,0},{1,3},{3,1},{4,6},{6,4},{5,7},{7,5},{8,10},{10,8},{9,1... | collective-permute-start | bytes 1572872 | tf_op jit(solution)/shard_map/ppermute | solution.py:61
  146.9 23.6 %collective-permute-start.6 = (bf16[256,1024]{1,0:T(8,128)(2,1)S(1)}, bf16[256,1024]{1,0:T(8,128)(2,1)S(1)}, u32[]{:S(2)}, u32[]{:S(2)}) collective-permute-start(bf16[256,1024]{1,0:T(8,128)(2,1)S(1)} %get-tuple-element.198), channel_id=1, source_target_pairs={{0,1},{1,0},{2,3},{3,2},{4,5},{5,4},{6,7},{7,6},{8,9},{9,8},{10,11... | collective-permute-start | bytes 1572872 | tf_op jit(solution)/shard_map/ppermute | solution.py:57
  184.4 504.0 %reduce-scatter.11.cloned.1.call-start = ((), (), s32[]{:S(2)}) async-start(), calls=%async_computation.13 | async-start | bytes 5242880 | tf_op jit(solution)/shard_map/reduce_scatter | solution.py:273
  290.3 422.3 %reduce-scatter.9.cloned.1.call-start = ((), (), s32[]{:S(2)}) async-start(), calls=%async_computation.12 | async-start | bytes 10485760 | tf_op jit(solution)/shard_map/reduce_scatter | solution.py:273
  378.8 336.1 %reduce-scatter.7.cloned.1.call-start = ((), (), s32[]{:S(2)}) async-start(), calls=%async_computation.11 | async-start | bytes 2359296 | tf_op jit(solution)/shard_map/reduce_scatter | solution.py:265
  422.0 23.3 %collective-permute-start.23 = (bf16[256,1024]{1,0:T(8,128)(2,1)S(1)}, bf16[256,1024]{1,0:T(8,128)(2,1)S(1)}, u32[]{:S(2)}, u32[]{:S(2)}) collective-permute-start(bf16[256,1024]{1,0:T(8,128)(2,1)S(1)} %fusion.70), channel_id=1, source_target_pairs={{0,1},{1,0},{2,3},{3,2},{4,5},{5,4},{6,7},{7,6},{8,9},{9,8},{10,11... | collective-permute-start | bytes 1572872 | tf_op jit(solution)/shard_map/ppermute | solution.py:57
  429.6 37.6 %collective-permute-start.14 = (bf16[512,2048]{1,0:T(8,128)(2,1)S(1)}, bf16[512,2048]{1,0:T(8,128)(2,1)S(1)}, u32[]{:S(2)}, u32[]{:S(2)}) collective-permute-start(bf16[512,2048]{1,0:T(8,128)(2,1)S(1)} %convolution_convert_fusion.4), channel_id=1, source_target_pairs={{0,4},{4,0},{1,5},{5,1},{2,6},{6,2},{3,7},{7,3},{8,12},{12,8},{9,1... | collective-permute-start | bytes 6291464 | tf_op jit(solution)/shard_map/ppermute | solution.py:65
  472.7 89.0 %collective-permute-start.15 = (bf16[512,2048]{1,0:T(8,128)(2,1)}, bf16[512,2048]{1,0:T(8,128)(2,1)}, u32[]{:S(2)}, u32[]{:S(2)}) collective-permute-start(bf16[512,2048]{1,0:T(8,128)(2,1)} %convolution_convert_fusion.3), channel_id=1, source_target_pairs={{0,4},{4,0},{1,5},{5,1},{2,6},{6,2},{3,7},{7,3},{8,12},{12,8},{9,1... | collective-permute-start | bytes 6291464 | tf_op jit(solution)/shard_map/ppermute | solution.py:65
  477.0 90.4 %collective-permute-start.63 = (f32[16,128]{1,0:T(8,128)S(1)}, f32[16,128]{1,0:T(8,128)S(1)}, u32[]{:S(2)}, u32[]{:S(2)}) collective-permute-start(f32[16,128]{1,0:T(8,128)S(1)} %add.387), channel_id=1, source_target_pairs={{0,8},{8,0},{16,24},{24,16},{1,9},{9,1},{17,25},{25,17},{2,10},{10... | collective-permute-start | bytes 24584 | tf_op jit(solution)/shard_map/ppermute | solution.py:185
  500.8 217.5 %reduce-scatter.5.cloned.1.call-start = ((), (), s32[]{:S(2)}) async-start(), calls=%async_computation.10 | async-start | bytes 4718592 | tf_op jit(solution)/shard_map/reduce_scatter | solution.py:265
  567.6 29.2 %collective-permute-start.34 = (bf16[256,1024]{1,0:T(8,128)(2,1)S(1)}, bf16[256,1024]{1,0:T(8,128)(2,1)S(1)}, u32[]{:S(2)}, u32[]{:S(2)}) collective-permute-start(bf16[256,1024]{1,0:T(8,128)(2,1)S(1)} %get-tuple-element.169), channel_id=1, source_target_pairs={{0,2},{2,0},{1,3},{3,1},{4,6},{6,4},{5,7},{7,5},{8,10},{10,8},{9,1... | collective-permute-start | bytes 1572872 | tf_op jit(solution)/shard_map/ppermute | solution.py:61
  568.1 28.2 %collective-permute-start.32 = (bf16[256,1024]{1,0:T(8,128)(2,1)S(1)}, bf16[256,1024]{1,0:T(8,128)(2,1)S(1)}, u32[]{:S(2)}, u32[]{:S(2)}) collective-permute-start(bf16[256,1024]{1,0:T(8,128)(2,1)S(1)} %get-tuple-element.170), channel_id=1, source_target_pairs={{0,1},{1,0},{2,3},{3,2},{4,5},{5,4},{6,7},{7,6},{8,9},{9,8},{10,11... | collective-permute-start | bytes 1572872 | tf_op jit(solution)/shard_map/ppermute | solution.py:57
  579.3 25.8 %collective-permute-start.48 = (bf16[256,1024]{1,0:T(8,128)(2,1)S(1)}, bf16[256,1024]{1,0:T(8,128)(2,1)S(1)}, u32[]{:S(2)}, u32[]{:S(2)}) collective-permute-start(bf16[256,1024]{1,0:T(8,128)(2,1)S(1)} %slice.597), channel_id=1, source_target_pairs={{0,2},{2,0},{1,3},{3,1},{4,6},{6,4},{5,7},{7,5},{8,10},{10,8},{9,1... | collective-permute-start | bytes 1572872 | tf_op jit(solution)/shard_map/ppermute | solution.py:61
  595.4 24.5 %collective-permute-start.47 = (bf16[256,1024]{1,0:T(8,128)(2,1)S(1)}, bf16[256,1024]{1,0:T(8,128)(2,1)S(1)}, u32[]{:S(2)}, u32[]{:S(2)}) collective-permute-start(bf16[256,1024]{1,0:T(8,128)(2,1)S(1)} %fusion.63), channel_id=1, source_target_pairs={{0,1},{1,0},{2,3},{3,2},{4,5},{5,4},{6,7},{7,6},{8,9},{9,8},{10,11... | collective-permute-start | bytes 1572872 | tf_op jit(solution)/shard_map/ppermute | solution.py:57
  596.2 25.1 %collective-permute-start.45 = (bf16[256,1024]{1,0:T(8,128)(2,1)S(1)}, bf16[256,1024]{1,0:T(8,128)(2,1)S(1)}, u32[]{:S(2)}, u32[]{:S(2)}) collective-permute-start(bf16[256,1024]{1,0:T(8,128)(2,1)S(1)} %fusion.65), channel_id=1, source_target_pairs={{0,2},{2,0},{1,3},{3,1},{4,6},{6,4},{5,7},{7,5},{8,10},{10,8},{9,1... | collective-permute-start | bytes 1572872 | tf_op jit(solution)/shard_map/ppermute | solution.py:61
  596.8 30.7 %collective-permute-start.36 = (bf16[256,1024]{1,0:T(8,128)(2,1)S(1)}, bf16[256,1024]{1,0:T(8,128)(2,1)S(1)}, u32[]{:S(2)}, u32[]{:S(2)}) collective-permute-start(bf16[256,1024]{1,0:T(8,128)(2,1)S(1)} %slice.598), channel_id=1, source_target_pairs={{0,2},{2,0},{1,3},{3,1},{4,6},{6,4},{5,7},{7,5},{8,10},{10,8},{9,1... | collective-permute-start | bytes 1572872 | tf_op jit(solution)/shard_map/ppermute | solution.py:61
  605.0 43.4 %collective-permute-start.64 = (f32[16,128]{1,0:T(8,128)S(1)}, f32[16,128]{1,0:T(8,128)S(1)}, u32[]{:S(2)}, u32[]{:S(2)}) collective-permute-start(f32[16,128]{1,0:T(8,128)S(1)} %add.388), channel_id=1, source_target_pairs={{0,24},{24,0},{8,16},{16,8},{1,25},{25,1},{9,17},{17,9},{2,26},{26... | collective-permute-start | bytes 24584 | tf_op jit(solution)/shard_map/ppermute | solution.py:186
  640.6 23.9 %collective-permute-start.39 = (bf16[256,1024]{1,0:T(8,128)(2,1)}, bf16[256,1024]{1,0:T(8,128)(2,1)}, u32[]{:S(2)}, u32[]{:S(2)}) collective-permute-start(bf16[256,1024]{1,0:T(8,128)(2,1)} %get-tuple-element.194), channel_id=1, source_target_pairs={{0,2},{2,0},{1,3},{3,1},{4,6},{6,4},{5,7},{7,5},{8,10},{10,8},{9,1... | collective-permute-start | bytes 1572872 | tf_op jit(solution)/shard_map/ppermute | solution.py:61
  652.4 22.5 %collective-permute-start.50 = (bf16[256,1024]{1,0:T(8,128)(2,1)}, bf16[256,1024]{1,0:T(8,128)(2,1)}, u32[]{:S(2)}, u32[]{:S(2)}) collective-permute-start(bf16[256,1024]{1,0:T(8,128)(2,1)} %get-tuple-element.187), channel_id=1, source_target_pairs={{0,1},{1,0},{2,3},{3,2},{4,5},{5,4},{6,7},{7,6},{8,9},{9,8},{10,11... | collective-permute-start | bytes 1572872 | tf_op jit(solution)/shard_map/ppermute | solution.py:57
  653.3 22.5 %collective-permute-start.51 = (bf16[256,1024]{1,0:T(8,128)(2,1)}, bf16[256,1024]{1,0:T(8,128)(2,1)}, u32[]{:S(2)}, u32[]{:S(2)}) collective-permute-start(bf16[256,1024]{1,0:T(8,128)(2,1)} %get-tuple-element.188), channel_id=1, source_target_pairs={{0,2},{2,0},{1,3},{3,1},{4,6},{6,4},{5,7},{7,5},{8,10},{10,8},{9,1... | collective-permute-start | bytes 1572872 | tf_op jit(solution)/shard_map/ppermute | solution.py:61
  654.0 33.0 %collective-permute-start.42 = (bf16[256,1024]{1,0:T(8,128)(2,1)S(1)}, bf16[256,1024]{1,0:T(8,128)(2,1)}, u32[]{:S(2)}, u32[]{:S(2)}) collective-permute-start(bf16[256,1024]{1,0:T(8,128)(2,1)S(1)} %collective-permute-done.38.x_b), channel_id=1, source_target_pairs={{0,2},{2,0},{1,3},{3,1},{4,6},{6,4},{5,7},{7,5},{8,10},{10,8},{9,1... | collective-permute-start | bytes 1572872 | tf_op jit(solution)/shard_map/ppermute | solution.py:61
  664.5 25.8 %collective-permute-start.41 = (bf16[256,1024]{1,0:T(8,128)(2,1)}, bf16[256,1024]{1,0:T(8,128)(2,1)}, u32[]{:S(2)}, u32[]{:S(2)}) collective-permute-start(bf16[256,1024]{1,0:T(8,128)(2,1)} %collective-permute-done.39.y_a), channel_id=1, source_target_pairs={{0,1},{1,0},{2,3},{3,2},{4,5},{5,4},{6,7},{7,6},{8,9},{9,8},{10,11... | collective-permute-start | bytes 1572872 | tf_op jit(solution)/shard_map/ppermute | solution.py:57
  665.3 32.9 %collective-permute-start.52 = (bf16[256,1024]{1,0:T(8,128)(2,1)}, bf16[256,1024]{1,0:T(8,128)(2,1)}, u32[]{:S(2)}, u32[]{:S(2)}) collective-permute-start(bf16[256,1024]{1,0:T(8,128)(2,1)} %get-tuple-element.187), channel_id=1, source_target_pairs={{0,2},{2,0},{1,3},{3,1},{4,6},{6,4},{5,7},{7,5},{8,10},{10,8},{9,1... | collective-permute-start | bytes 1572872 | tf_op jit(solution)/shard_map/ppermute | solution.py:61
  674.8 23.4 %collective-permute-start.49 = (bf16[256,1024]{1,0:T(8,128)(2,1)}, bf16[256,1024]{1,0:T(8,128)(2,1)}, u32[]{:S(2)}, u32[]{:S(2)}) collective-permute-start(bf16[256,1024]{1,0:T(8,128)(2,1)} %get-tuple-element.188), channel_id=1, source_target_pairs={{0,1},{1,0},{2,3},{3,2},{4,5},{5,4},{6,7},{7,6},{8,9},{9,8},{10,11... | collective-permute-start | bytes 1572872 | tf_op jit(solution)/shard_map/ppermute | solution.py:57
  675.7 28.4 %collective-permute-start.54 = (bf16[256,1024]{1,0:T(8,128)(2,1)}, bf16[256,1024]{1,0:T(8,128)(2,1)}, u32[]{:S(2)}, u32[]{:S(2)}) collective-permute-start(bf16[256,1024]{1,0:T(8,128)(2,1)} %collective-permute-done.50.x_b), channel_id=1, source_target_pairs={{0,2},{2,0},{1,3},{3,1},{4,6},{6,4},{5,7},{7,5},{8,10},{10,8},{9,1... | collective-permute-start | bytes 1572872 | tf_op jit(solution)/shard_map/ppermute | solution.py:61
  690.3 26.7 %collective-permute-start.66 = (bf16[256,1024]{1,0:T(8,128)(2,1)}, bf16[256,1024]{1,0:T(8,128)(2,1)}, u32[]{:S(2)}, u32[]{:S(2)}) collective-permute-start(bf16[256,1024]{1,0:T(8,128)(2,1)} %constant_dynamic-slice_fusion), channel_id=1, source_target_pairs={{0,4},{4,0},{1,5},{5,1},{2,6},{6,2},{3,7},{7,3},{8,12},{12,8},{9,1... | collective-permute-start | bytes 1572872 | tf_op jit(solution)/shard_map/ppermute | solution.py:65
  (96 other events, 966.3 us)
Sparse Core Ops, SparseCore 0:
  20.5 47.9 all-gather.4
  70.1 29.0 all-gather.6
  101.3 148.6 all-gather.8
  252.1 78.9 all-gather.10
  333.2 75.2 reduce-scatter.10
  410.9 145.1 reduce-scatter.8
  558.5 36.4 reduce-scatter.6
  597.4 48.7 reduce-scatter.4

commit v3 on v2

v3 whole, which is shorter than its diff:
```python
import functools

import jax
import jax.numpy as jnp
from jax import lax
from jax.experimental import pallas as pl
from jax.experimental.pallas import tpu as pltpu
from jax.sharding import Mesh, PartitionSpec as P

QUERY_HEADS = 8
KEY_VALUE_HEADS = 4
HEAD_SIZE = 256

eps_norm = 1e-06
rope_base = 1000042.0
neg_large = -1e30
bf16 = jnp.bfloat16
f32 = jnp.float32


def rope_tables(slot_length, size):
    half_size = size // 2
    inv_freq = rope_base ** (-(jnp.arange(half_size, dtype=f32) * 2.0 / size))
    angles = jnp.arange(slot_length, dtype=f32)[:, None] * inv_freq[None, :]
    return (jnp.cos(angles), jnp.sin(angles))


def rotate(values, cos_b, sin_b):
    half = values.shape[-1] // 2
    a, b = values[..., :half], values[..., half:]
    return jnp.concatenate([a * cos_b - b * sin_b, b * cos_b + a * sin_b], axis=-1)


def rotate_back(grads, cos_b, sin_b):
    half = grads.shape[-1] // 2
    a, b = grads[..., :half], grads[..., half:]
    return jnp.concatenate([a * cos_b + b * sin_b, b * cos_b - a * sin_b], axis=-1)


def mm(left, right):
    return lax.dot_general(left, right, (((1,), (0,)), ((), ())), preferred_element_type=f32)


def mm_t(left, right):
    return lax.dot_general(left, right, (((1,), (1,)), ((), ())), preferred_element_type=f32)


def mm_rows(left, right):
    return lax.dot_general(left, right, (((0,), (0,)), ((), ())), preferred_element_type=f32)


DP = ("z", "core")
OVER_X = [(0, 1), (1, 0), (2, 3), (3, 2)]
OVER_Y = [(0, 2), (2, 0), (1, 3), (3, 1)]
OVER_CORE = [(0, 1), (1, 0)]


def send_x(v):
    return lax.ppermute(v, "mp", OVER_X)


def send_y(v):
    return lax.ppermute(v, "mp", OVER_Y)


def send_core(v):
    return lax.ppermute(v, "core", OVER_CORE)


def square():
    return lax.axis_size("mp") == 4


def tie(*values):
    return lax.optimization_barrier(values)


def block_orders():
    steps = jnp.arange(4, dtype=jnp.int32)
    if not square():
        return steps, steps
    me = lax.axis_index("mp").astype(jnp.int32)
    away = jnp.bitwise_xor(me, steps)
    return jnp.bitwise_xor(me, jnp.array([0, 2, 1, 3], jnp.int32)), (away % 2) * 2 + away // 2


def tile(size, most):
    while size % most:
        most //= 2
    return most


def column_product_kernel(left_ref, right_ref, out_ref):
    out_ref[...] = mm(left_ref[...], right_ref[...]).astype(out_ref.dtype)


def column_product(left, right, first, cols, dtype):
    rows, depth = left.shape
    tn = tile(cols, 256)
    return pl.pallas_call(
        column_product_kernel,
        name="column_product",
        grid=(cols // tn,),
        in_specs=[
            pl.BlockSpec((rows, depth), lambda j: (0, 0)),
            pl.BlockSpec((depth, tn), lambda j: (0, first // tn + j)),
        ],
        out_specs=pl.BlockSpec((rows, tn), lambda j: (0, j)),
        out_shape=jax.ShapeDtypeStruct((rows, cols), dtype),
        cost_estimate=pl.CostEstimate(
            flops=2 * rows * depth * cols, transcendentals=0, bytes_accessed=2 * (rows + cols) * depth + 4 * rows * cols
        ),
        compiler_params=pltpu.CompilerParams(vmem_limit_bytes=56 << 20),
    )(left, right)


def transposed_product_kernel(groups, added, left_ref, right_ref, *refs):
    outs = refs[-sum(len(g) for g in groups) :]
    steps = pl.num_programs(0) // len(groups)
    if len(left_ref.shape) == 2:
        total = mm_t(left_ref[...], right_ref[...])
    else:
        depth = left_ref.shape[2]
        total = mm_t(left_ref[0], right_ref[:, :depth]) + mm_t(left_ref[1], right_ref[:, depth:])
    if added:
        total = total + refs[0][...].astype(f32)
    size = total.shape[0] // 4
    for i, group in enumerate(groups):

        @pl.when(pl.program_id(0) // steps == i)
        def _(first=sum(len(g) for g in groups[:i]), group=group):
            for out, blocks in zip(outs[first : first + len(group)], group):
                for place, block in enumerate(blocks):
                    part = total[block * size : (block + 1) * size]
                    out[place * size : (place + 1) * size] = part.astype(out.dtype)


def transposed_product(left, sequence, rows, right, first, groups, add=None, earlier=()):
    depth = left.shape[-1]
    pair = left.ndim == 3
    deep = 2 * depth if pair else depth
    cols = right.shape[0] // len(groups)
    tn = tile(cols, 512)
    steps = cols // tn
    size = rows // 4
    adds = [] if add is None else [add]

    def at(i):
        return lambda j: (0, jnp.clip(j - i * steps, 0, steps - 1))

    return pl.pallas_call(
        functools.partial(transposed_product_kernel, groups, add is not None),
        name="transposed_product",
        grid=(len(groups) * steps,),
        in_specs=[
            pl.BlockSpec((2, rows, depth), lambda j: (0, sequence, 0))
            if pair
            else pl.BlockSpec((rows, depth), lambda j: (sequence, 0)),
            pl.BlockSpec((tn, deep), lambda j: (j, first // deep)),
        ]
        + [pl.BlockSpec((rows, tn), lambda j: (0, j))] * len(adds)
        + [pl.BlockSpec(memory_space=pl.ANY)] * len(earlier),
        out_specs=[
            pl.BlockSpec((len(blocks) * size, tn), at(i))
            for i, group in enumerate(groups)
            for blocks in group
        ],
        out_shape=[
            jax.ShapeDtypeStruct((len(blocks) * size, cols), f32 if blocks == (0,) else bf16)
            for group in groups
            for blocks in group
        ],
        cost_estimate=pl.CostEstimate(
            flops=2 * rows * deep * right.shape[0],
            transcendentals=0,
            bytes_accessed=2 * (rows + right.shape[0]) * deep + 2 * rows * right.shape[0],
        ),
        compiler_params=pltpu.CompilerParams(vmem_limit_bytes=56 << 20),
    )(left, right, *adds, *earlier)


WHOLE = (((0, 1, 2, 3),),)
PIECES = (((0,), (1,), (2, 3)), ((0,), (2,), (1, 3)))


def away_product(left, right, rows, earlier=()):
    return transposed_product(left, 1, rows, right, 0, WHOLE, earlier=earlier)[0]


def scatter_product(left, right, first, rows, add=None, earlier=()):
    groups = PIECES if square() else WHOLE
    return transposed_product(left, 0, rows, right, first, groups, add, earlier)


def scatter_near(pieces):
    if not square():
        return ()
    return send_x(pieces[2]), send_y(pieces[5])


def scatter_middle(pieces, near):
    if not square():
        return ()
    own_a, y_a, _, own_b, x_b, _ = pieces
    size = own_a.shape[0]
    return (
        (y_a.astype(f32) + near[0][size:].astype(f32)).astype(bf16),
        (x_b.astype(f32) + near[1][size:].astype(f32)).astype(bf16),
    )


def scatter_far(middle):
    if not square():
        return ()
    return send_y(middle[0]), send_x(middle[1])


def scatter_end(pieces, near, far):
    if not square():
        return lax.psum_scatter(pieces[0], "mp", scatter_dimension=0, tiled=True).astype(f32)
    size = pieces[0].shape[0]
    kept = [
        own + got[:size].astype(f32) + last.astype(f32)
        for own, got, last in zip((pieces[0], pieces[3]), near, far)
    ]
    return jnp.concatenate(kept, axis=1)


def scatter_rows(pieces):
    near = scatter_near(pieces)
    return scatter_end(pieces, near, scatter_far(scatter_middle(pieces, near)))


def assemble_kernel(order_ref, own, over_x, over_y, diag_a, diag_b, out_ref):
    half = diag_a.shape[1]
    for i, ref in enumerate([own, over_y, over_x]):

        @pl.when(pl.program_id(0) == i)
        def _(ref=ref):
            out_ref[...] = ref[...].astype(out_ref.dtype)

    @pl.when(pl.program_id(0) == 3)
    def _():
        out_ref[:, :half] = diag_a[...].astype(out_ref.dtype)
        out_ref[:, half:] = diag_b[...].astype(out_ref.dtype)


def assemble(order, pieces, dtype):
    here, width = pieces[0].shape
    return pl.pallas_call(
        assemble_kernel,
        name="assemble",
        grid_spec=pltpu.PrefetchScalarGridSpec(
            num_scalar_prefetch=1,
            grid=(4,),
            in_specs=[pl.BlockSpec((here, piece.shape[1]), lambda i, s: (0, 0)) for piece in pieces],
            out_specs=pl.BlockSpec((here, width), lambda i, s: (s[i], 0)),
        ),
        out_shape=jax.ShapeDtypeStruct((4 * here, width), dtype),
        cost_estimate=pl.CostEstimate(flops=0, transcendentals=0, bytes_accessed=20 * here * width),
        compiler_params=pltpu.CompilerParams(vmem_limit_bytes=40 << 20),
    )(order, *pieces)


def exchange_near(block):
    if not square():
        return (lax.all_gather(block, "mp", axis=0, tiled=True),)
    return send_x(block), send_y(block)


def exchange_middle(near):
    if not square():
        return ()
    half = near[0].shape[1] // 2
    return near[1][:, :half], near[0][:, half:]


def exchange_far(middle):
    if not square():
        return ()
    return send_x(middle[0]), send_y(middle[1])


def exchange_rows(block):
    near = exchange_near(block)
    return (block, *near, *exchange_far(exchange_middle(near)))


def join_rows(pieces, relative, dtype=bf16):
    if not square():
        return pieces[1].astype(dtype)
    order = jnp.arange(4, dtype=jnp.int32) if relative else block_orders()[0]
    return assemble(order, pieces, dtype)


def sum_mp(v):
    if not square():
        return lax.psum(v, "mp")
    v = v + send_x(v)
    return v + send_y(v)


def allowed_block(i, size, seq_len):
    shape = (size, (i + 1) * size)
    q_pos = i * size + lax.broadcasted_iota(jnp.int32, shape, 0)
    k_pos = lax.broadcasted_iota(jnp.int32, shape, 1)
    return (k_pos <= q_pos) & (k_pos < seq_len)


def probabilities(queries, keys, i, size, seq_len):
    factor = HEAD_SIZE ** (-0.5)
    scores = mm_t(queries, keys) * factor
    scores = jnp.where(allowed_block(i, size, seq_len), scores, neg_large)
    exps = jnp.exp(scores - jnp.max(scores, axis=-1, keepdims=True))
    return exps * (1.0 / jnp.sum(exps, axis=-1, keepdims=True))


def block_rows(order_ref, i, size):
    return pl.ds(pl.multiple_of(order_ref[i] * size, size), size)


def load_keys(order_ref, k_ref, v_ref, cos_ref, sin_ref, keys, values, size):
    for i in range(keys.shape[0] // size):
        rows = block_rows(order_ref, i, size)
        here = pl.ds(i * size, size)
        keys[here] = rotate(k_ref[rows], cos_ref[here], sin_ref[here]).astype(bf16)
        values[here] = v_ref[rows].astype(bf16)


def attention_forward_kernel(
    order_ref, len_ref, q_ref, k_ref, v_ref, cos_ref, sin_ref, out_ref, keys, values
):
    blocks = order_ref.shape[0]
    size = keys.shape[0] // blocks
    seq_len = len_ref[0]

    @pl.when(pl.program_id(0) == 0)
    def _():
        load_keys(order_ref, k_ref, v_ref, cos_ref, sin_ref, keys, values, size)

    for i in range(blocks):
        rows = block_rows(order_ref, i, size)
        here = pl.ds(i * size, size)
        upto = (i + 1) * size
        queries = rotate(q_ref[rows], cos_ref[here], sin_ref[here]).astype(bf16)
        probs = probabilities(queries, keys[:upto], i, size, seq_len).astype(bf16)
        out_ref[rows] = mm(probs, values[:upto]).astype(bf16)


def attention_backward_kernel(
    order_ref, len_ref, q_ref, k_ref, v_ref, cos_ref, sin_ref, g_ref, out_ref, keys, values, d_keys, d_values
):
    blocks = order_ref.shape[0]
    size = keys.shape[0] // blocks
    seq_len = len_ref[0]
    step = pl.program_id(0)
    heads = pl.num_programs(0) - 2
    factor = HEAD_SIZE ** (-0.5)

    @pl.when(step == 0)
    def _():
        load_keys(order_ref, k_ref, v_ref, cos_ref, sin_ref, keys, values, size)
        d_keys[...] = jnp.zeros_like(d_keys)
        d_values[...] = jnp.zeros_like(d_values)

    @pl.when(step < heads)
    def _():
        for i in range(blocks):
            rows = block_rows(order_ref, i, size)
            here = pl.ds(i * size, size)
            upto = (i + 1) * size
            cos_b, sin_b = cos_ref[here], sin_ref[here]
            queries = rotate(q_ref[rows], cos_b, sin_b).astype(bf16)
            grads = g_ref[rows]
            probs = probabilities(queries, keys[:upto], i, size, seq_len)
            d_values[:upto] += mm_rows(probs.astype(bf16), grads)
            d_probs = mm_t(grads, values[:upto])
            inner = jnp.sum(probs * d_probs, axis=-1, keepdims=True)
            d_scores = (probs * (d_probs - inner) * factor).astype(bf16)
            d_keys[:upto] += mm_rows(d_scores, queries)
            out_ref[rows] = rotate_back(mm(d_scores, keys[:upto]), cos_b, sin_b).astype(bf16)

    @pl.when(step == heads)
    def _():
        for i in range(blocks):
            here = pl.ds(i * size, size)
            out_ref[block_rows(order_ref, i, size)] = rotate_back(
                d_keys[here], cos_ref[here], sin_ref[here]
            ).astype(bf16)

    @pl.when(step == heads + 1)
    def _():
        for i in range(blocks):
            out_ref[block_rows(order_ref, i, size)] = d_values[pl.ds(i * size, size)].astype(bf16)


def attention_specs(slots, heads):
    half = HEAD_SIZE // 2
    return [
        pl.BlockSpec((slots, HEAD_SIZE), lambda h, o, n: (0, jnp.minimum(h, heads - 1))),
        pl.BlockSpec((slots, HEAD_SIZE), lambda h, o, n: (0, heads)),
        pl.BlockSpec((slots, HEAD_SIZE), lambda h, o, n: (0, heads + 1)),
        pl.BlockSpec((slots, half), lambda h, o, n: (0, 0)),
        pl.BlockSpec((slots, half), lambda h, o, n: (0, 0)),
    ]


def attention_forward(order, length, qkv, tables):
    slots = qkv.shape[0]
    heads = qkv.shape[1] // HEAD_SIZE - 2
    return pl.pallas_call(
        attention_forward_kernel,
        name="attention_forward",
        grid_spec=pltpu.PrefetchScalarGridSpec(
            num_scalar_prefetch=2,
            grid=(heads,),
            in_specs=attention_specs(slots, heads),
            out_specs=pl.BlockSpec((slots, HEAD_SIZE), lambda h, o, n: (0, h)),
            scratch_shapes=[pltpu.VMEM((slots, HEAD_SIZE), bf16)] * 2,
        ),
        out_shape=jax.ShapeDtypeStruct((slots, heads * HEAD_SIZE), bf16),
        cost_estimate=pl.CostEstimate(
            flops=3 * heads * slots * slots * HEAD_SIZE,
            transcendentals=heads * slots * slots,
            bytes_accessed=8 * slots * HEAD_SIZE * (heads + 2),
        ),
        compiler_params=pltpu.CompilerParams(vmem_limit_bytes=56 << 20),
    )(order, length, qkv, qkv, qkv, *tables)


def attention_backward(order, length, qkv, tables, d_context):
    slots = qkv.shape[0]
    heads = qkv.shape[1] // HEAD_SIZE - 2
    return pl.pallas_call(
        attention_backward_kernel,
        name="attention_backward",
        grid_spec=pltpu.PrefetchScalarGridSpec(
            num_scalar_prefetch=2,
            grid=(heads + 2,),
            in_specs=attention_specs(slots, heads)
            + [pl.BlockSpec((slots, HEAD_SIZE), lambda h, o, n: (0, jnp.minimum(h, heads - 1)))],
            out_specs=pl.BlockSpec((slots, HEAD_SIZE), lambda h, o, n: (0, h)),
            scratch_shapes=[pltpu.VMEM((slots, HEAD_SIZE), bf16)] * 2
            + [pltpu.VMEM((slots, HEAD_SIZE), f32)] * 2,
        ),
        out_shape=jax.ShapeDtypeStruct((slots, (heads + 2) * HEAD_SIZE), bf16),
        cost_estimate=pl.CostEstimate(
            flops=7 * heads * slots * slots * HEAD_SIZE,
            transcendentals=heads * slots * slots,
            bytes_accessed=8 * slots * HEAD_SIZE * (heads + 2),
        ),
        compiler_params=pltpu.CompilerParams(vmem_limit_bytes=56 << 20),
    )(order, length, qkv, qkv, qkv, *tables, d_context)


def attention_products_kernel(g1_ref, context_ref, h_ref, d_qkv_ref, *refs):
    out_ref = refs[-1]
    cols = context_ref.shape[1]
    out_ref[:, :cols] = mm_rows(g1_ref[...], context_ref[...]).astype(bf16)
    out_ref[:, cols:] = mm_rows(h_ref[...], d_qkv_ref[...]).astype(bf16)


def attention_products(g1, context, h, d_qkv, *earlier):
    rows, width = g1.shape
    cols, more = context.shape[1], d_qkv.shape[1]
    tm = tile(width, 512)
    return pl.pallas_call(
        attention_products_kernel,
        name="attention_products",
        grid=(width // tm,),
        in_specs=[
            pl.BlockSpec((rows, tm), lambda i: (0, i)),
            pl.BlockSpec((rows, cols), lambda i: (0, 0)),
            pl.BlockSpec((rows, tm), lambda i: (0, i)),
            pl.BlockSpec((rows, more), lambda i: (0, 0)),
        ]
        + [pl.BlockSpec(memory_space=pl.ANY)] * len(earlier),
        out_specs=pl.BlockSpec((tm, cols + more), lambda i: (i, 0)),
        out_shape=jax.ShapeDtypeStruct((width, cols + more), bf16),
        cost_estimate=pl.CostEstimate(
            flops=2 * rows * width * (cols + more),
            transcendentals=0,
            bytes_accessed=4 * rows * width + 2 * (rows + width) * (cols + more),
        ),
        compiler_params=pltpu.CompilerParams(vmem_limit_bytes=56 << 20),
    )(g1, context, h, d_qkv, *earlier)


def prepare_kernel(order_ref, len_ref, x_ref, grad_ref, x_out, grad_out):
    size = x_ref.shape[0]
    first = order_ref[pl.program_id(0)] * size
    pos = first + lax.broadcasted_iota(jnp.int32, (size, 1), 0)
    x_out[...] = x_ref[...]
    grad_out[...] = jnp.where(pos < len_ref[0], grad_ref[...].astype(f32), 0.0).astype(bf16)


def prepare(order, length, x_in, cotangent):
    slots, width = x_in.shape
    size = slots // 4
    source = pl.BlockSpec((size, width), lambda i, o, n: (o[i], 0))
    target = pl.BlockSpec((size, width), lambda i, o, n: (i, 0))
    return pl.pallas_call(
        prepare_kernel,
        name="prepare",
        grid_spec=pltpu.PrefetchScalarGridSpec(
            num_scalar_prefetch=2, grid=(4,), in_specs=[source] * 2, out_specs=[target] * 2
        ),
        out_shape=[jax.ShapeDtypeStruct(x_in.shape, bf16)] * 2,
        cost_estimate=pl.CostEstimate(flops=0, transcendentals=0, bytes_accessed=8 * slots * width),
        compiler_params=pltpu.CompilerParams(vmem_limit_bytes=40 << 20),
    )(order, length, x_in, cotangent)


def spread_heads(block):
    mp_size = lax.axis_size("mp")
    rows, n, heads, part = block.shape
    send = jnp.repeat(block, mp_size // heads, axis=2)
    got = lax.all_to_all(send, "mp", 2, 2, tiled=True)
    return got.reshape(rows, n * mp_size * part)


def collect_heads(block, heads):
    mp_size = lax.axis_size("mp")
    rows, n, size = block.shape
    part = size // mp_size
    got = lax.all_to_all(block.reshape(rows, n, mp_size, part), "mp", 2, 2, tiled=True)
    return jnp.sum(got.reshape(rows, n, heads, mp_size // heads, part).astype(f32), axis=3)


def gather_dp(block):
    return lax.all_gather(block, DP, axis=0, tiled=True)


def reduce_dp(block):
    return lax.psum_scatter(block, DP, scatter_dimension=0, tiled=True)


def gather_z(block):
    return lax.all_gather(block, "z", axis=0, tiled=True)


def reduce_z(block):
    return lax.psum_scatter(block, "z", scatter_dimension=0, tiled=True)


def to_core(block):
    rows, n, cols = block.shape
    core = lax.axis_index("core")
    m = cols // 2
    own = lax.dynamic_slice_in_dim(block, core * m, m, 2).reshape(rows, n * m)
    away = lax.dynamic_slice_in_dim(block, (1 - core) * m, m, 2).reshape(rows, n * m)
    got = send_core(away)
    return jnp.concatenate([jnp.where(core == 0, own, got), jnp.where(core == 0, got, own)])


def own_half_kernel(transpose, core_ref, own_ref, got_ref, *refs):
    out_ref = refs[-1]
    value = jnp.where(pl.program_id(0) == core_ref[0], own_ref[...].astype(f32), got_ref[...].astype(f32))
    out_ref[...] = value.T if transpose else value


def from_core(block, n, transpose=False, earlier=()):
    rows = block.shape[0] // 2
    m = block.shape[1] // n
    core = lax.axis_index("core").astype(jnp.int32)
    got = send_core(lax.dynamic_slice_in_dim(block, (1 - core) * rows, rows, 0))
    out_block = (m, rows) if transpose else (rows, m)
    out_shape = (2 * m, rows) if transpose else (rows, 2 * m)
    return [
        pl.pallas_call(
            functools.partial(own_half_kernel, transpose),
            name="own_half",
            grid_spec=pltpu.PrefetchScalarGridSpec(
                num_scalar_prefetch=1,
                grid=(2,),
                in_specs=[
                    pl.BlockSpec((rows, m), lambda h, c, i=i: (c[0], i)),
                    pl.BlockSpec((rows, m), lambda h, c, i=i: (0, i)),
                ]
                + [pl.BlockSpec(memory_space=pl.ANY)] * len(earlier),
                out_specs=pl.BlockSpec(out_block, lambda h, c: (h, 0) if transpose else (0, h)),
            ),
            out_shape=jax.ShapeDtypeStruct(out_shape, f32),
            cost_estimate=pl.CostEstimate(flops=0, transcendentals=0, bytes_accessed=12 * rows * m),
            compiler_params=pltpu.CompilerParams(vmem_limit_bytes=40 << 20),
        )(core.reshape(1), block, got, *earlier)
        for i in range(n)
    ]


def ffn_forward_kernel(mine_ref, away_ref, g_ref, u_ref, hidden_ref, factor_ref):
    def run(h_ref):
        h = h_ref[...]
        gate = jnp.dot(h, g_ref[...], preferred_element_type=f32)
        up = jnp.dot(h, u_ref[...], preferred_element_type=f32)
        sig = 1.0 / (1.0 + jnp.exp(-gate))
        silu = gate * sig
        hidden_ref[...] = (silu * up).astype(bf16)
        factor_ref[0] = (up * sig * (1.0 + gate - silu)).astype(bf16)
        factor_ref[1] = silu.astype(bf16)

    pl.when(pl.program_id(0) == 0)(lambda: run(mine_ref))
    pl.when(pl.program_id(0) == 1)(lambda: run(away_ref))


def ffn_forward(mine, away, w_gu):
    rows, width = mine.shape
    ff = w_gu.shape[1] // 2
    tn = tile(ff, 256)
    return pl.pallas_call(
        ffn_forward_kernel,
        name="ffn_forward",
        grid=(2, ff // tn),
        in_specs=[
            pl.BlockSpec((rows, width), lambda i, j: (0, 0)),
            pl.BlockSpec((rows, width), lambda i, j: (0, 0)),
            pl.BlockSpec((width, tn), lambda i, j: (0, j)),
            pl.BlockSpec((width, tn), lambda i, j: (0, j + ff // tn)),
        ],
        out_specs=[
            pl.BlockSpec((rows, tn), lambda i, j: (i, j)),
            pl.BlockSpec((2, rows, tn), lambda i, j: (0, i, j)),
        ],
        out_shape=[
            jax.ShapeDtypeStruct((2 * rows, ff), bf16),
            jax.ShapeDtypeStruct((2, 2 * rows, ff), bf16),
        ],
        cost_estimate=pl.CostEstimate(
            flops=8 * rows * width * ff,
            transcendentals=2 * rows * ff,
            bytes_accessed=4 * (rows * width + width * ff + 3 * rows * ff),
        ),
        compiler_params=pltpu.CompilerParams(vmem_limit_bytes=56 << 20),
    )(mine, away, w_gu, w_gu)


def rows_product_kernel(mine_ref, away_ref, right_mine_ref, right_away_ref, *refs):
    out_ref = refs[-1]
    cols = right_mine_ref.shape[2]
    for i in range(2):
        out_ref[:, i * cols : (i + 1) * cols] = (
            mm_rows(mine_ref[...], right_mine_ref[i]) + mm_rows(away_ref[...], right_away_ref[i])
        ).astype(bf16)


def rows_product(mine, away, right, part, parts, into=None, earlier=()):
    rows, width = mine.shape
    cols = 2 * right.shape[2]
    tm = tile(width // parts, 256)
    steps = width // parts // tm
    more = ([] if into is None else [into]) + list(earlier)
    return pl.pallas_call(
        rows_product_kernel,
        name="rows_product",
        grid=(steps,),
        in_specs=[
            pl.BlockSpec((rows, tm), lambda i: (0, part * steps + i)),
            pl.BlockSpec((rows, tm), lambda i: (0, part * steps + i)),
            pl.BlockSpec((2, rows, cols // 2), lambda i: (0, 0, 0)),
            pl.BlockSpec((2, rows, cols // 2), lambda i: (0, 1, 0)),
        ]
        + [pl.BlockSpec(memory_space=pl.ANY)] * len(more),
        out_specs=pl.BlockSpec((tm, cols), lambda i: (part * steps + i, 0)),
        out_shape=jax.ShapeDtypeStruct((width, cols), bf16),
        input_output_aliases={} if into is None else {4: 0},
        cost_estimate=pl.CostEstimate(
            flops=4 * rows * width * cols // parts,
            transcendentals=0,
            bytes_accessed=(4 * rows * width + 2 * width * cols) // parts + 4 * rows * cols,
        ),
        compiler_params=pltpu.CompilerParams(vmem_limit_bytes=56 << 20),
    )(mine, away, right, right, *more)


def ffn_backward_kernel(grad_ref, d_ref, factor_ref, earlier_ref, out_ref):
    d_hidden = mm(grad_ref[...], d_ref[...])
    for i in range(2):
        out_ref[i] = (d_hidden * factor_ref[i].astype(f32)).astype(bf16)


def ffn_backward(grad, w_d, factors, earlier):
    rows, width = grad.shape
    ff = w_d.shape[1]
    tm, tn = tile(rows, 1024), tile(ff, 256)
    return pl.pallas_call(
        ffn_backward_kernel,
        name="ffn_backward",
        grid=(rows // tm, ff // tn),
        in_specs=[
            pl.BlockSpec((tm, width), lambda i, j: (i, 0)),
            pl.BlockSpec((width, tn), lambda i, j: (0, j)),
            pl.BlockSpec((2, tm, tn), lambda i, j: (0, i, j)),
            pl.BlockSpec(memory_space=pl.ANY),
        ],
        out_specs=pl.BlockSpec((2, tm, tn), lambda i, j: (0, i, j)),
        out_shape=jax.ShapeDtypeStruct((2, rows, ff), bf16),
        cost_estimate=pl.CostEstimate(
            flops=2 * rows * width * ff, transcendentals=0, bytes_accessed=2 * (rows * width + width * ff + 4 * rows * ff)
        ),
        compiler_params=pltpu.CompilerParams(vmem_limit_bytes=56 << 20),
    )(grad, w_d, factors, earlier)


def local(
    x_in,
    lengths,
    gain_attn,
    query_weight,
    key_projection_matrix,
    value_projection_matrix,
    out_weight,
    gain_ffn,
    gate_weight,
    up_weight,
    down_weight,
    cotangent,
):
    _, slots, width = x_in.shape
    mp_size = lax.axis_size("mp")
    me = lax.axis_index("mp")
    q_cols = query_weight.shape[1]
    here = slots // mp_size
    quarter = slots // 4
    tables = rope_tables(slots, HEAD_SIZE)
    sequence_block, relative_place = block_orders()

    def own_rows(v):
        return v[:here] if square() else lax.dynamic_slice_in_dim(v, me * here, here, 0)

    x_rel, grad_mine = prepare(sequence_block, lengths, x_in[0], cotangent[0])
    kv_block = spread_heads(jnp.stack([key_projection_matrix, value_projection_matrix], axis=1))
    w_attn = gather_dp(jnp.concatenate([query_weight, kv_block, out_weight.T], axis=1))
    o_first = q_cols + 2 * HEAD_SIZE
    ffn_block = to_core(jnp.stack([gate_weight, up_weight, down_weight.T], axis=1))
    ff = ffn_block.shape[1] // 3
    w_gu = gather_z(ffn_block[:, : 2 * ff])
    w_d = gather_z(ffn_block[:, 2 * ff :])
    gains = lax.all_gather(jnp.stack([gain_attn, gain_ffn]), DP, axis=1, tiled=True).astype(f32)
    g_attn, g_ffn = gains[0], gains[1]

    tok = x_rel.astype(f32)
    r1 = lax.rsqrt(jnp.mean(tok * tok, axis=-1, keepdims=True) + eps_norm)
    h_attn = (tok * r1 * g_attn).astype(bf16)
    grad_all = jnp.concatenate([grad_mine, send_core(grad_mine)])
    qkv = column_product(h_attn, w_attn, 0, o_first, f32)
    context = attention_forward(relative_place, lengths, qkv, tables)

    attn_rows = scatter_rows(scatter_product(context, w_attn, o_first, slots))
    tok_here = own_rows(x_rel).astype(f32)
    mid = tok_here + attn_rows
    r2 = lax.rsqrt(jnp.mean(mid * mid, axis=-1, keepdims=True) + eps_norm)
    n2 = mid * r2
    h_mine = join_rows(exchange_rows((n2 * g_ffn).astype(bf16)), True)
    h_away = send_core(h_mine)

    hidden, factors = ffn_forward(h_mine, h_away, w_gu)
    down_grad = mm_rows(grad_all, hidden).astype(bf16)
    down_out = reduce_z(down_grad)

    ffn_away = away_product(hidden, w_d, slots, (down_grad,))
    ffn_add = send_core(ffn_away)
    d_gu = ffn_backward(grad_all, w_d, factors, ffn_away)
    gu_grad = rows_product(h_mine, h_away, d_gu, 0, 1, earlier=(d_gu,))
    gu_out = reduce_z(gu_grad)
    ffn_pieces = scatter_product(hidden, w_d, 0, slots, ffn_add, (gu_grad,))
    ffn_near = scatter_near(ffn_pieces)
    h2_away = away_product(d_gu, w_gu, slots, (ffn_pieces[-1],))
    h2_add = send_core(h2_away)
    ffn_middle = scatter_middle(ffn_pieces, ffn_near)
    ffn_far = scatter_far(ffn_middle)
    h2_pieces = scatter_product(d_gu, w_gu, 0, slots, h2_add)
    h2_pieces, ffn_far = tie(h2_pieces, ffn_far)
    ffn_rows = scatter_end(ffn_pieces, ffn_near, ffn_far)
    d_h2 = scatter_rows(h2_pieces)

    e2 = d_h2 * g_ffn
    g1 = own_rows(grad_mine).astype(f32) + r2 * (e2 - n2 * jnp.mean(e2 * n2, axis=-1, keepdims=True))
    g1_low = join_rows(exchange_rows(g1.astype(bf16)), True)

    layer_block, g1_low = tie((mid + ffn_rows).astype(bf16), g1_low)
    layer_near = exchange_near(layer_block)
    d_context = column_product(g1_low, w_attn, o_first, q_cols, bf16)
    d_qkv = attention_backward(relative_place, lengths, qkv, tables, d_context)
    layer_middle = exchange_middle(layer_near)
    attn_grads = attention_products(g1_low, context, h_attn, d_qkv, *layer_middle)
    attn_out = reduce_dp(attn_grads)
    layer_far = exchange_far(layer_middle)
    h1_pieces = scatter_product(d_qkv, w_attn, 0, slots, earlier=(attn_grads,))
    h1_pieces, layer_far = tie(h1_pieces, layer_far)
    layer_out = join_rows((layer_block, *layer_near, *layer_far), False)
    d_h1 = scatter_rows(h1_pieces)
    r1_here = own_rows(r1)
    n1 = tok_here * r1_here
    e1 = d_h1 * g_attn
    grad_in = g1 + r1_here * (e1 - n1 * jnp.mean(e1 * n1, axis=-1, keepdims=True))
    grad_pieces = exchange_rows(grad_in.astype(bf16))

    rows_here = gain_attn.shape[0]

    (down_out,) = from_core(down_out, 1, True)
    gate_out, up_out = from_core(gu_out, 2, earlier=(down_out,))
    out_out, q_out = attn_out[:, :q_cols], attn_out[:, q_cols : 2 * q_cols].astype(f32)
    kv_out = attn_out[:, 2 * q_cols :]
    kv_grad = collect_heads(kv_out.reshape(rows_here, 2, HEAD_SIZE), KEY_VALUE_HEADS)

    def row_sums(*pairs):
        return sum(jnp.sum(w.astype(f32) * g.astype(f32), axis=1) for w, g in pairs)

    gain_sums = sum_mp(
        jnp.stack(
            [
                row_sums((query_weight, q_out), (kv_block, kv_out)),
                row_sums((gate_weight, gate_out), (up_weight, up_out)),
            ]
        )
    )
    gain_attn_grad = gain_sums[0] / gain_attn.astype(f32)
    gain_ffn_grad = gain_sums[1] / gain_ffn.astype(f32)
    grad_pieces, kv_grad, down_out, gate_out, up_out = tie(
        grad_pieces, kv_grad, down_out, gate_out, up_out
    )
    grad_input = join_rows(grad_pieces, False, f32)
    return (
        layer_out[None],
        grad_input[None],
        gain_attn_grad,
        q_out,
        kv_grad[:, 0],
        kv_grad[:, 1],
        out_out.T.astype(f32),
        gain_ffn_grad,
        gate_out,
        up_out,
        down_out,
    )


def solution(mesh):
    dp_size, mp_size = mesh.shape["dp"], mesh.shape["mp"]
    split = Mesh(mesh.devices.reshape(dp_size // 2, 2, mp_size), ("z", "core", "mp"))
    return jax.shard_map(
        local,
        mesh=split,
        in_specs=(
            P(DP, None, None),
            P(DP),
            P(DP),
            P(DP, "mp"),
            P(DP, None, "mp"),
            P(DP, None, "mp"),
            P("mp", DP),
            P(DP),
            P(DP, "mp"),
            P(DP, "mp"),
            P("mp", DP),
            P(DP, None, None),
        ),
        out_specs=(
            P(DP, None, None),
            P(DP, None, None),
            P(DP),
            P(DP, "mp"),
            P(DP, None, "mp"),
            P(DP, None, "mp"),
            P("mp", DP),
            P(DP),
            P(DP, "mp"),
            P(DP, "mp"),
            P("mp", DP),
        ),
        check_vma=False,
    )
```

time: 751 us -> 675 us (0.90)
  matrix products: 152 us -> 14 us
  Pallas kernels: 89 us -> 204 us
  waiting for transfers between devices: 317 us -> 288 us
  starting transfers between devices: 64.1 us -> 47.3 us
    dot_general x26 -> x0, matrix products: 123 us -> none  [the longest x12 62.2 us: mm_t(): lax.dot_general(left, right, (((1,), (1,)), ((), ())), preferred_element_...]
    pallas_call x1 -> x16, Pallas kernels: 23.9 us -> 147 us  [the longest x6 64.3 us: transposed_product(): pl.pallas_call(functools.partial(transposed_product_kernel, groups, add i...]
    ppermute x26 -> x17, waiting for transfers between devices: 67.2 us -> 110 us  [send_x(): return lax.ppermute(v, 'mp', OVER_X)]
    ppermute x26 -> x17, waiting for transfers between devices: 114 us -> 75.7 us  [send_y(): return lax.ppermute(v, 'mp', OVER_Y)]
    all_gather x2, waiting for transfers between devices: 100 us -> 72.7 us  [gather_z(): return lax.all_gather(block, 'z', axis=0, tiled=True)]
    dot_general x3 -> x1, matrix products: 28.9 us -> 14 us  [mm_rows(): lax.dot_general(left, right, (((0,), (0,)), ((), ())), preferred_element_...]
    convert_element_type x15 -> x12, other arithmetic: 7.74 us -> 19.4 us  [the longest x4 5.14 us: scatter_middle(): (x_b.astype(f32) + near[1][size:].astype(f32)).astype(bf16)]
    ppermute x26 -> x17, starting transfers between devices: 27.8 us -> 17.3 us  [send_x(): return lax.ppermute(v, 'mp', OVER_X)]
  transfers between devices with their start and end apart: 77 -> 49, of which waited for: 43 -> 25; matrix products, arithmetic and copies ran while one was open for 31% -> 12% of each run, Pallas kernels for 12% -> 30%
where the time goes in v3:
time: 675 us; the launch traced here: 670 us
  waiting for transfers between devices  288 us (43%)
  Pallas kernels  204 us (30%)
  starting transfers between devices  47.3 us (7%)
  other arithmetic  45.3 us (7%)
  local copies, waits for them, and re-layouts  42.6 us (6%)
  between operations  15.7 us (2%)
  matrix products  14 us (2%)
  blocking collectives  12.6 us (2%)
    ppermute x17, waiting for transfers between devices, send_x(): return lax.ppermute(v, 'mp', OVER_X)  110 us
    ppermute x17, waiting for transfers between devices, send_y(): return lax.ppermute(v, 'mp', OVER_Y)  75.7 us
    all_gather x2, waiting for transfers between devices, gather_z(): return lax.all_gather(block, 'z', axis=0, tiled=True)  72.7 us
    pallas_call x6, Pallas kernels, transposed_product(): pl.pallas_call(functools.partial(transposed_product_kernel, groups, add i...  64.3 us
    pallas_call x1, Pallas kernels, ffn_forward(): pl.pallas_call(ffn_forward_kernel, name='ffn_forward', grid=(2, ff // tn)...  26.3 us
    pallas_call x1, Pallas kernels, rows_product(): pl.pallas_call(rows_product_kernel, name='rows_product', grid=(steps,), i...  23.9 us
    unnamed x115, local copies, waits for them, and re-layouts  23.3 us
    all_gather x1, waiting for transfers between devices, gather_dp(): return lax.all_gather(block, DP, axis=0, tiled=True)  22.3 us
  transfers between devices with their start and end apart: 49, of which 25 were waited for; matrix products, arithmetic and copies ran while one was open for 12% of the time, Pallas kernels for 30%

profile of v3, /device:TPU:0, one launch (start us, length us, event | category | flops | bytes accessed | tf_op | source)
XLA Modules:
  0.0 669.6 jit_solution(7825039048623567943)
XLA Ops:
  37.3 5.6 prepare.1
  42.9 12.6 %all_gather.12 = bf16[2,2048]{1,0:T(2,128)(2,1)S(1)} all-gather(bf16[2,256]{1,0:T(2,128)(2,1)S(1)} %pad_maximum_fusion.5), channel_id=1, replica_groups=mesh['z'=4,'core'=2,'mp'=4] {'z','core'}, dimensions={1}, use_global_device_ids=true | all-gather | bytes 9216 | tf_op jit(solution)/shard_map/all_gather | solution.py:738
  63.4 22.3 %all-gather.4.cloned.1.call-done.right_ref = bf16[2048,1536]{1,0:T(8,128)(2,1)} async-done(((bf16[256,1536]{1,0:T(8,128)(2,1)}), bf16[2048,1536]{1,0:T(8,128)(2,1)}) %all-gather.4.cloned.1.call-update) | async-done | bytes 6291472 | tf_op jit(solution)/shard_map/all_gather | solution.py:531
  85.6 9.0 %column_product.2.q_ref.k_ref.v_ref = f32[1024,1024]{1,0:T(8,128)} custom-call(bf16[1024,2048]{1,0:T(8,128)(2,1)} %fusion.2.left_ref.h_ref, bf16[2048,1536]{1,0:T(8,128)(2,1)} %all-gather.4.cloned.1.call-done.right_ref), custom_call_target="tpu_custom_call" | custom-call | flops 4294967296 | bytes 12582912 | tf_op jit(solution)/shard_map/column_product/pallas_call | solution.py:100
  94.6 8.2 %attention_forward.1.left_ref.context_ref = bf16[1024,512]{1,0:T(8,128)(2,1)} custom-call(s32[4]{0:T(128)} %fusion.15.order_ref, s32[1]{0:T(128)S(6)} %copy.57.len_ref, f32[1024,1024]{1,0:T(8,128)} %column_product.2.q_ref.k_ref.v_ref, f32[1024,1024]{1,0:T(8,128)} %column_product.2.q_ref.k_ref.v_ref, f32[1024,1024]{1,0:T(8,128)} %column_product.2.q_ref.k_ref.v_ref, ...), custom_call_target="tpu_custom_call" | custom-call | flops 1610612736 | bytes 8388608 | tf_op jit(solution)/shard_map/attention_forward/pallas_call | solution.py:411
  102.9 7.1 %transposed_product.6 = (f32[256,1024]{1,0:T(8,128)}, bf16[256,1024]{1,0:T(8,128)(2,1)}, bf16[512,1024]{1,0:T(8,128)(2,1)}, f32[256,1024]{1,0:T(8,128)}, bf16[25...) custom-call(bf16[1024,512]{1,0:T(8,128)(2,1)} %attention_forward.1.left_ref.context_ref, ...), custom_call_target="tpu_custom_call" | custom-call | flops 2147483648 | bytes 7340032 | tf_op jit(solution)/shard_map/transposed_product/pallas_call | solution.py:151
  113.0 22.5 %collective-permute-done = bf16[512,1024]{1,0:T(8,128)(2,1)S(1)} collective-permute-done((bf16[512,1024]{1,0:T(8,128)(2,1)}, bf16[512,1024]{1,0:T(8,128)(2,1)S(1)}, u32[]{:S(2)}, u32[]{:S(2)}) %collective-permute-start) | collective-permute-done | bytes 1048608 | tf_op jit(solution)/shard_map/ppermute | solution.py:59
  141.3 9.0 %collective-permute-done.1 = bf16[256,1024]{1,0:T(8,128)(2,1)S(1)} collective-permute-done((bf16[256,1024]{1,0:T(8,128)(2,1)S(1)}, bf16[256,1024]{1,0:T(8,128)(2,1)S(1)}, u32[]{:S(2)}, u32[]{:S(2)}) %collective-permute-start.1) | collective-permute-done | bytes 524320 | tf_op jit(solution)/shard_map/ppermute | solution.py:63
  156.3 21.1 %collective-permute-done.5.over_y = bf16[256,2048]{1,0:T(8,128)(2,1)S(1)} collective-permute-done((bf16[256,2048]{1,0:T(8,128)(2,1)S(1)}, bf16[256,2048]{1,0:T(8,128)(2,1)S(1)}, u32[]{:S(2)}, u32[]{:S(2)}) %collective-permute-start.5) | collective-permute-done | bytes 1048608 | tf_op jit(solution)/shard_map/ppermute | solution.py:63
  180.2 9.2 %collective-permute-done.6.diag_a = bf16[256,1024]{1,0:T(8,128)(2,1)S(1)} collective-permute-done((bf16[256,1024]{1,0:T(8,128)(2,1)S(1)}, bf16[256,1024]{1,0:T(8,128)(2,1)S(1)}, u32[]{:S(2)}, u32[]{:S(2)}) %collective-permute-start.6) | collective-permute-done | bytes 524320 | tf_op jit(solution)/shard_map/ppermute | solution.py:59
  204.2 31.9 %all-gather.6.cloned.1.call-done.g_ref.u_ref.right_ref = bf16[2048,2048]{1,0:T(8,128)(2,1)} async-done(((bf16[512,2048]{1,0:T(8,128)(2,1)}), bf16[2048,2048]{1,0:T(8,128)(2,1)}) %all-gather.6.cloned.1.call-update) | async-done | bytes 8388624 | tf_op jit(solution)/shard_map/all_gather | solution.py:539
  236.1 26.3 %ffn_forward.1 = (bf16[2048,1024]{1,0:T(8,128)(2,1)}, bf16[2,2048,1024]{2,1,0:T(8,128)(2,1)}) custom-call(bf16[1024,2048]{1,0:T(8,128)(2,1)} %assemble.4.mine_ref, bf16[1024,2048]{1,0:T(8,128)(2,1)} %collective-permute-done.8.away_ref, bf16[2048,2048]{1,0:T(8,128)(2,1)} %all-gather.6.cloned.1.call-done.g_ref.u_ref.right_ref, ...), custom_call_target="tpu_custom_call" | custom-call | flops 17179869184 | bytes 29360128 | tf_op jit(solution)/shard_map/ffn_forward/pallas_call | solution.py:610
  262.4 14.0 %convolution_convert_fusion.refs_0_ = bf16[2048,1024]{1,0:T(8,128)(2,1)} fusion(bf16[2048,2048]{1,0:T(8,128)(2,1)} %constant_dynamic-update-slice_fusion.grad_ref, bf16[2048,1024]{1,0:T(8,128)(2,1)} %get-tuple-element.73.left_ref), kind=kOutput, calls=%fused_computation.5 | convolution fusion | flops 8592031744 | bytes 16777216 | tf_op jit(solution)/shard_map/dot_general | solution.py:49
  276.5 40.8 %all-gather.8.cloned.1.call-done.right_ref.d_ref = bf16[2048,1024]{1,0:T(8,128)(2,1)} async-done(((bf16[512,1024]{1,0:T(8,128)(2,1)}), bf16[2048,1024]{1,0:T(8,128)(2,1)}) %all-gather.8.cloned.1.call-update) | async-done | bytes 4194320 | tf_op jit(solution)/shard_map/all_gather | solution.py:539
  317.3 8.8 %transposed_product.7.earlier_ref = bf16[1024,2048]{1,0:T(8,128)(2,1)} custom-call(bf16[2048,1024]{1,0:T(8,128)(2,1)} %get-tuple-element.73.left_ref, bf16[2048,1024]{1,0:T(8,128)(2,1)} %all-gather.8.cloned.1.call-done.right_ref.d_ref, bf16[2048,1024]{1,0:T(8,128)(2,1)} %convolution_convert_fusion.refs_0_), custom_call_target="tpu_custom_call" | custom-call | flops 4294967296 | bytes 10485760 | tf_op jit(solution)/shard_map/transposed_product/pallas_call | solution.py:151
  326.1 18.0 %ffn_backward.1.right_mine_ref.right_away_ref.refs_0_.left_ref = bf16[2,2048,1024]{2,1,0:T(8,128)(2,1)} custom-call(bf16[2048,2048]{1,0:T(8,128)(2,1)} %constant_dynamic-update-slice_fusion.grad_ref, bf16[2048,1024]{1,0:T(8,128)(2,1)} %all-gather.8.cloned.1.call-done.right_ref.d_ref, bf16[2,2048,1024]{2,1,0:T(8,128)(2,1)} %get-tuple-element.75.factor_ref, ...), custom_call_target="tpu_custom_call" | custom-call | flops 8589934592 | bytes 29360128 | tf_op jit(solution)/shard_map/ffn_backward/pallas_call | solution.py:685
  344.1 23.9 %rows_product.1.refs_1_ = bf16[2048,2048]{1,0:T(8,128)(2,1)} custom-call(bf16[1024,2048]{1,0:T(8,128)(2,1)} %assemble.4.mine_ref, bf16[1024,2048]{1,0:T(8,128)(2,1)} %collective-permute-done.8.away_ref, bf16[2,2048,1024]{2,1,0:T(8,128)(2,1)} %ffn_backward.1.right_mine_ref.right_away_ref.refs_0_.left_ref, ...), custom_call_target="tpu_custom_call" | custom-call | flops 17179869184 | bytes 25165824 | tf_op jit(solution)/shard_map/rows_product/pallas_call | solution.py:652
  368.5 10.1 %transposed_product.8 = (f32[256,1024]{1,0:T(8,128)}, bf16[256,1024]{1,0:T(8,128)(2,1)}, bf16[512,1024]{1,0:T(8,128)(2,1)}, f32[256,1024]{1,0:T(8,128)}, bf16[25...) custom-call(bf16[2048,1024]{1,0:T(8,128)(2,1)} %get-tuple-element.73.left_ref, ...), custom_call_target="tpu_custom_call" | custom-call | flops 4294967296 | bytes 10485760 | tf_op jit(solution)/shard_map/transposed_product/pallas_call | solution.py:151
  378.6 14.0 %transposed_product.9 = bf16[1024,2048]{1,0:T(8,128)(2,1)} custom-call(bf16[2,2048,1024]{2,1,0:T(8,128)(2,1)} %ffn_backward.1.right_mine_ref.right_away_ref.refs_0_.left_ref, bf16[2048,2048]{1,0:T(8,128)(2,1)} %all-gather.6.cloned.1.call-done.g_ref.u_ref.right_ref, bf16[512,1024]{1,0:T(8,128)(2,1)} %get-tuple-element.78.refs_0_), custom_call_target="tpu_custom_call" | custom-call | flops 8589934592 | bytes 16777216 | tf_op jit(solution)/shard_map/transposed_product/pallas_call | solution.py:151
  396.1 22.1 %collective-permute-done.12 = bf16[512,1024]{1,0:T(8,128)(2,1)S(1)} collective-permute-done((bf16[512,1024]{1,0:T(8,128)(2,1)S(1)}, bf16[512,1024]{1,0:T(8,128)(2,1)S(1)}, u32[]{:S(2)}, u32[]{:S(2)}) %collective-permute-start.12) | collective-permute-done | bytes 1048608 | tf_op jit(solution)/shard_map/ppermute | solution.py:59
  421.7 14.9 %transposed_product.10 = (f32[256,1024]{1,0:T(8,128)}, bf16[256,1024]{1,0:T(8,128)(2,1)}, bf16[512,1024]{1,0:T(8,128)(2,1)}, f32[256,1024]{1,0:T(8,128)}, bf16[2...) custom-call(bf16[2,2048,1024]{2,1,0:T(8,128)(2,1)} %ffn_backward.1.right_mine_ref.right_away_ref.refs_0_.left_ref, ...), custom_call_target="tpu_custom_call" | custom-call | flops 8589934592 | bytes 16777216 | tf_op jit(solution)/shard_map/transposed_product/pallas_call | solution.py:151
  438.2 22.6 %collective-permute-done.17 = bf16[512,1024]{1,0:T(8,128)(2,1)S(1)} collective-permute-done((bf16[512,1024]{1,0:T(8,128)(2,1)}, bf16[512,1024]{1,0:T(8,128)(2,1)S(1)}, u32[]{:S(2)}, u32[]{:S(2)}) %collective-permute-start.17) | collective-permute-done | bytes 1048608 | tf_op jit(solution)/shard_map/ppermute | solution.py:59
  465.4 8.4 %collective-permute-done.18 = bf16[256,1024]{1,0:T(8,128)(2,1)S(1)} collective-permute-done((bf16[256,1024]{1,0:T(8,128)(2,1)S(1)}, bf16[256,1024]{1,0:T(8,128)(2,1)S(1)}, u32[]{:S(2)}, u32[]{:S(2)}) %collective-permute-start.18) | collective-permute-done | bytes 524320 | tf_op jit(solution)/shard_map/ppermute | solution.py:63
  481.6 20.8 %collective-permute-done.22.over_y = bf16[256,2048]{1,0:T(8,128)(2,1)S(1)} collective-permute-done((bf16[256,2048]{1,0:T(8,128)(2,1)S(1)}, bf16[256,2048]{1,0:T(8,128)(2,1)S(1)}, u32[]{:S(2)}, u32[]{:S(2)}) %collective-permute-start.22) | collective-permute-done | bytes 1048608 | tf_op jit(solution)/shard_map/ppermute | solution.py:63
  506.0 7.8 %collective-permute-done.23.diag_a = bf16[256,1024]{1,0:T(8,128)(2,1)S(1)} collective-permute-done((bf16[256,1024]{1,0:T(8,128)(2,1)S(1)}, bf16[256,1024]{1,0:T(8,128)(2,1)S(1)}, u32[]{:S(2)}, u32[]{:S(2)}) %collective-permute-start.23) | collective-permute-done | bytes 524320 | tf_op jit(solution)/shard_map/ppermute | solution.py:59
  518.7 5.8 column_product.3.g_ref
  524.6 13.1 %attention_backward.1.d_qkv_ref.left_ref = bf16[1024,1024]{1,0:T(8,128)(2,1)} custom-call(s32[4]{0:T(128)} %fusion.15.order_ref, s32[1]{0:T(128)S(6)} %copy.57.len_ref, f32[1024,1024]{1,0:T(8,128)} %column_product.2.q_ref.k_ref.v_ref, f32[1024,1024]{1,0:T(8,128)} %column_product.2.q_ref.k_ref.v_ref, f32[1024,1024]{1,0:T(8,128)} %column_product.2.q_ref.k_ref.v_ref, ...), custom_call_target="tpu_custom_call" | custom-call | flops 3758096384 | bytes 8388608 | tf_op jit(solution)/shard_map/attention_backward/pallas_call | solution.py:434
  540.4 11.4 %attention_products.1.refs_0_ = bf16[2048,1536]{1,0:T(8,128)(2,1)} custom-call(bf16[1024,2048]{1,0:T(8,128)(2,1)} %copy-done.4, bf16[1024,512]{1,0:T(8,128)(2,1)} %attention_forward.1.left_ref.context_ref, bf16[1024,2048]{1,0:T(8,128)(2,1)} %fusion.2.left_ref.h_ref, bf16[1024,1024]{1,0:T(8,128)(2,1)} %attention_backward.1.d_qkv_ref.left_ref, ...), custom_call_target="tpu_custom_call" | custom-call | flops 6442450944 | bytes 17825792 | tf_op jit(solution)/shard_map/attention_products/pallas_call | solution.py:467
  554.2 9.4 %transposed_product.11 = (f32[256,1024]{1,0:T(8,128)}, bf16[256,1024]{1,0:T(8,128)(2,1)}, bf16[512,1024]{1,0:T(8,128)(2,1)}, f32[256,1024]{1,0:T(8,128)}, bf16[2...) custom-call(bf16[1024,1024]{1,0:T(8,128)(2,1)} %attention_backward.1.d_qkv_ref.left_ref, ...), custom_call_target="tpu_custom_call" | custom-call | flops 4294967296 | bytes 10485760 | tf_op jit(solution)/shard_map/transposed_product/pallas_call | solution.py:151
  567.1 19.4 %collective-permute-done.29 = bf16[512,1024]{1,0:T(8,128)(2,1)S(1)} collective-permute-done((bf16[512,1024]{1,0:T(8,128)(2,1)}, bf16[512,1024]{1,0:T(8,128)(2,1)S(1)}, u32[]{:S(2)}, u32[]{:S(2)}) %collective-permute-start.29) | collective-permute-done | bytes 1048608 | tf_op jit(solution)/shard_map/ppermute | solution.py:59
  647.3 7.4 %collective-permute-done.40 = f32[2,256]{1,0:T(2,128)S(1)} collective-permute-done((f32[2,256]{1,0:T(2,128)S(1)}, f32[2,256]{1,0:T(2,128)S(1)}, u32[]{:S(2)}, u32[]{:S(2)}) %collective-permute-start.40) | collective-permute-done | bytes 2080 | tf_op jit(solution)/shard_map/ppermute | solution.py:63
  656.8 5.7 assemble.7
  (286 shorter events, 170.5 us)
Async XLA Ops:
  14.1 71.5 %all-gather.4.cloned.1.call-start = ((), (), s32[]{:S(2)}) async-start(), calls=%async_computation.5 | async-start | bytes 7077888 | tf_op jit(solution)/shard_map/all_gather | solution.py:531
  20.6 215.5 %all-gather.6.cloned.1.call-start = ((), (), s32[]{:S(2)}) async-start(), calls=%async_computation.6 | async-start | bytes 10485760 | tf_op jit(solution)/shard_map/all_gather | solution.py:539
  34.3 283.0 %all-gather.8.cloned.1.call-start = ((), (), s32[]{:S(2)}) async-start(), calls=%async_computation.7 | async-start | bytes 5242880 | tf_op jit(solution)/shard_map/all_gather | solution.py:539
  109.9 25.6 %collective-permute-start = (bf16[512,1024]{1,0:T(8,128)(2,1)}, bf16[512,1024]{1,0:T(8,128)(2,1)S(1)}, u32[]{:S(2)}, u32[]{:S(2)}) collective-permute-start(bf16[512,1024]{1,0:T(8,128)(2,1)} %get-tuple-element.68), channel_id=1, source_target_pairs={{0,1},{1,0},{2,3},{3,2},{4,5},{5,4},{6,7},{7,6},{8,9},{9,8},{10,11... | collective-permute-start | bytes 3145736 | tf_op jit(solution)/shard_map/ppermute | solution.py:59
  111.6 26.8 %collective-permute-start.2 = (bf16[512,1024]{1,0:T(8,128)(2,1)}, bf16[512,1024]{1,0:T(8,128)(2,1)S(1)}, u32[]{:S(2)}, u32[]{:S(2)}) collective-permute-start(bf16[512,1024]{1,0:T(8,128)(2,1)} %get-tuple-element.71), channel_id=1, source_target_pairs={{0,2},{2,0},{1,3},{3,1},{4,6},{6,4},{5,7},{7,5},{8,10},{10,8},{9,1... | collective-permute-start | bytes 3145736 | tf_op jit(solution)/shard_map/ppermute | solution.py:63
  153.9 23.5 %collective-permute-start.5 = (bf16[256,2048]{1,0:T(8,128)(2,1)S(1)}, bf16[256,2048]{1,0:T(8,128)(2,1)S(1)}, u32[]{:S(2)}, u32[]{:S(2)}) collective-permute-start(bf16[256,2048]{1,0:T(8,128)(2,1)S(1)} %multiply_convert_fusion.own), channel_id=1, source_target_pairs={{0,2},{2,0},{1,3},{3,1},{4,6},{6,4},{5,7},{7,5},{8,10},{10,8},{9,1... | collective-permute-start | bytes 3145736 | tf_op jit(solution)/shard_map/ppermute | solution.py:63
  154.8 24.2 %collective-permute-start.4 = (bf16[256,2048]{1,0:T(8,128)(2,1)S(1)}, bf16[256,2048]{1,0:T(8,128)(2,1)S(1)}, u32[]{:S(2)}, u32[]{:S(2)}) collective-permute-start(bf16[256,2048]{1,0:T(8,128)(2,1)S(1)} %multiply_convert_fusion.own), channel_id=1, source_target_pairs={{0,1},{1,0},{2,3},{3,2},{4,5},{5,4},{6,7},{7,6},{8,9},{9,8},{10,11... | collective-permute-start | bytes 3145736 | tf_op jit(solution)/shard_map/ppermute | solution.py:59
  180.2 19.2 %collective-permute-start.10 = (bf16[1024,2048]{1,0:T(8,128)(2,1)}, bf16[1024,2048]{1,0:T(8,128)(2,1)}, u32[]{:S(2)}, u32[]{:S(2)}) collective-permute-start(bf16[1024,2048]{1,0:T(8,128)(2,1)} %get-tuple-element.74), channel_id=1, source_target_pairs={{0,4},{4,0},{1,5},{5,1},{2,6},{6,2},{3,7},{7,3},{8,12},{12,8},{9,1... | collective-permute-start | bytes 12582920 | tf_op jit(solution)/shard_map/ppermute | solution.py:67
  193.3 42.8 %collective-permute-start.8 = (bf16[1024,2048]{1,0:T(8,128)(2,1)}, bf16[1024,2048]{1,0:T(8,128)(2,1)}, u32[]{:S(2)}, u32[]{:S(2)}) collective-permute-start(bf16[1024,2048]{1,0:T(8,128)(2,1)} %assemble.4.mine_ref), channel_id=1, source_target_pairs={{0,4},{4,0},{1,5},{5,1},{2,6},{6,2},{3,7},{7,3},{8,12},{12,8},{9,1... | collective-permute-start | bytes 12582920 | tf_op jit(solution)/shard_map/ppermute | solution.py:67
  194.4 398.5 %reduce-scatter.6.cloned.1.call-start = ((), (), s32[]{:S(2)}) async-start(), calls=%async_computation.9 | async-start | bytes 5242880 | tf_op jit(solution)/shard_map/reduce_scatter | solution.py:543
  276.5 328.9 %reduce-scatter.8.cloned.1.call-start = ((), (), s32[]{:S(2)}) async-start(), calls=%async_computation.10 | async-start | bytes 10485760 | tf_op jit(solution)/shard_map/reduce_scatter | solution.py:543
  326.1 42.4 %collective-permute-start.11 = (bf16[1024,2048]{1,0:T(8,128)(2,1)}, bf16[1024,2048]{1,0:T(8,128)(2,1)}, u32[]{:S(2)}, u32[]{:S(2)}) collective-permute-start(bf16[1024,2048]{1,0:T(8,128)(2,1)} %transposed_product.7.earlier_ref), channel_id=1, source_target_pairs={{0,4},{4,0},{1,5},{5,1},{2,6},{6,2},{3,7},{7,3},{8,12},{12,8},{9,1... | collective-permute-start | bytes 12582920 | tf_op jit(solution)/shard_map/ppermute | solution.py:67
  368.0 254.6 %reduce-scatter.4.cloned.1.call-start = ((), (), s32[]{:S(2)}) async-start(), calls=%async_computation.8 | async-start | bytes 7077888 | tf_op jit(solution)/shard_map/reduce_scatter | solution.py:535
  392.6 29.1 %collective-permute-start.13 = (bf16[1024,2048]{1,0:T(8,128)(2,1)}, bf16[1024,2048]{1,0:T(8,128)(2,1)}, u32[]{:S(2)}, u32[]{:S(2)}) collective-permute-start(bf16[1024,2048]{1,0:T(8,128)(2,1)} %transposed_product.9), channel_id=1, source_target_pairs={{0,4},{4,0},{1,5},{5,1},{2,6},{6,2},{3,7},{7,3},{8,12},{12,8},{9,1... | collective-permute-start | bytes 12582920 | tf_op jit(solution)/shard_map/ppermute | solution.py:67
  393.1 25.1 %collective-permute-start.12 = (bf16[512,1024]{1,0:T(8,128)(2,1)S(1)}, bf16[512,1024]{1,0:T(8,128)(2,1)S(1)}, u32[]{:S(2)}, u32[]{:S(2)}) collective-permute-start(bf16[512,1024]{1,0:T(8,128)(2,1)S(1)} %copy-done.53), channel_id=1, source_target_pairs={{0,1},{1,0},{2,3},{3,2},{4,5},{5,4},{6,7},{7,6},{8,9},{9,8},{10,11... | collective-permute-start | bytes 3145736 | tf_op jit(solution)/shard_map/ppermute | solution.py:59
  394.6 25.4 %collective-permute-start.15 = (bf16[512,1024]{1,0:T(8,128)(2,1)S(1)}, bf16[512,1024]{1,0:T(8,128)(2,1)S(1)}, u32[]{:S(2)}, u32[]{:S(2)}) collective-permute-start(bf16[512,1024]{1,0:T(8,128)(2,1)S(1)} %copy-done.52), channel_id=1, source_target_pairs={{0,2},{2,0},{1,3},{3,1},{4,6},{6,4},{5,7},{7,5},{8,10},{10,8},{9,1... | collective-permute-start | bytes 3145736 | tf_op jit(solution)/shard_map/ppermute | solution.py:63
  418.4 18.2 %collective-permute-start.14 = (bf16[256,1024]{1,0:T(8,128)(2,1)S(1)}, bf16[256,1024]{1,0:T(8,128)(2,1)S(1)}, u32[]{:S(2)}, u32[]{:S(2)}) collective-permute-start(bf16[256,1024]{1,0:T(8,128)(2,1)S(1)} %add_convert_fusion.5), channel_id=1, source_target_pairs={{0,2},{2,0},{1,3},{3,1},{4,6},{6,4},{5,7},{7,5},{8,10},{10,8},{9,1... | collective-permute-start | bytes 1572872 | tf_op jit(solution)/shard_map/ppermute | solution.py:63
  420.2 16.4 %collective-permute-start.16 = (bf16[256,1024]{1,0:T(8,128)(2,1)S(1)}, bf16[256,1024]{1,0:T(8,128)(2,1)S(1)}, u32[]{:S(2)}, u32[]{:S(2)}) collective-permute-start(bf16[256,1024]{1,0:T(8,128)(2,1)S(1)} %add_convert_fusion.4), channel_id=1, source_target_pairs={{0,1},{1,0},{2,3},{3,2},{4,5},{5,4},{6,7},{7,6},{8,9},{9,8},{10,11... | collective-permute-start | bytes 1572872 | tf_op jit(solution)/shard_map/ppermute | solution.py:59
  436.7 24.1 %collective-permute-start.17 = (bf16[512,1024]{1,0:T(8,128)(2,1)}, bf16[512,1024]{1,0:T(8,128)(2,1)S(1)}, u32[]{:S(2)}, u32[]{:S(2)}) collective-permute-start(bf16[512,1024]{1,0:T(8,128)(2,1)} %get-tuple-element.91), channel_id=1, source_target_pairs={{0,1},{1,0},{2,3},{3,2},{4,5},{5,4},{6,7},{7,6},{8,9},{9,8},{10,11... | collective-permute-start | bytes 3145736 | tf_op jit(solution)/shard_map/ppermute | solution.py:59
  437.3 25.3 %collective-permute-start.19 = (bf16[512,1024]{1,0:T(8,128)(2,1)}, bf16[512,1024]{1,0:T(8,128)(2,1)S(1)}, u32[]{:S(2)}, u32[]{:S(2)}) collective-permute-start(bf16[512,1024]{1,0:T(8,128)(2,1)} %get-tuple-element.94), channel_id=1, source_target_pairs={{0,2},{2,0},{1,3},{3,1},{4,6},{6,4},{5,7},{7,5},{8,10},{10,8},{9,1... | collective-permute-start | bytes 3145736 | tf_op jit(solution)/shard_map/ppermute | solution.py:63
  480.1 22.3 %collective-permute-start.22 = (bf16[256,2048]{1,0:T(8,128)(2,1)S(1)}, bf16[256,2048]{1,0:T(8,128)(2,1)S(1)}, u32[]{:S(2)}, u32[]{:S(2)}) collective-permute-start(bf16[256,2048]{1,0:T(8,128)(2,1)S(1)} %get-tuple-element.156.own), channel_id=1, source_target_pairs={{0,2},{2,0},{1,3},{3,1},{4,6},{6,4},{5,7},{7,5},{8,10},{10,8},{9,1... | collective-permute-start | bytes 3145736 | tf_op jit(solution)/shard_map/ppermute | solution.py:63
  481.0 23.4 %collective-permute-start.21 = (bf16[256,2048]{1,0:T(8,128)(2,1)S(1)}, bf16[256,2048]{1,0:T(8,128)(2,1)S(1)}, u32[]{:S(2)}, u32[]{:S(2)}) collective-permute-start(bf16[256,2048]{1,0:T(8,128)(2,1)S(1)} %get-tuple-element.156.own), channel_id=1, source_target_pairs={{0,1},{1,0},{2,3},{3,2},{4,5},{5,4},{6,7},{7,6},{8,9},{9,8},{10,11... | collective-permute-start | bytes 3145736 | tf_op jit(solution)/shard_map/ppermute | solution.py:59
  516.8 21.7 %collective-permute-start.26 = (bf16[256,2048]{1,0:T(8,128)(2,1)S(1)}, bf16[256,2048]{1,0:T(8,128)(2,1)S(1)}, u32[]{:S(2)}, u32[]{:S(2)}) collective-permute-start(bf16[256,2048]{1,0:T(8,128)(2,1)S(1)} %get-tuple-element.96.own), channel_id=1, source_target_pairs={{0,2},{2,0},{1,3},{3,1},{4,6},{6,4},{5,7},{7,5},{8,10},{10,8},{9,1... | collective-permute-start | bytes 3145736 | tf_op jit(solution)/shard_map/ppermute | solution.py:63
  518.1 21.4 %collective-permute-start.25 = (bf16[256,2048]{1,0:T(8,128)(2,1)S(1)}, bf16[256,2048]{1,0:T(8,128)(2,1)S(1)}, u32[]{:S(2)}, u32[]{:S(2)}) collective-permute-start(bf16[256,2048]{1,0:T(8,128)(2,1)S(1)} %get-tuple-element.96.own), channel_id=1, source_target_pairs={{0,1},{1,0},{2,3},{3,2},{4,5},{5,4},{6,7},{7,6},{8,9},{9,8},{10,11... | collective-permute-start | bytes 3145736 | tf_op jit(solution)/shard_map/ppermute | solution.py:59
  565.2 21.2 %collective-permute-start.29 = (bf16[512,1024]{1,0:T(8,128)(2,1)}, bf16[512,1024]{1,0:T(8,128)(2,1)S(1)}, u32[]{:S(2)}, u32[]{:S(2)}) collective-permute-start(bf16[512,1024]{1,0:T(8,128)(2,1)} %get-tuple-element.107), channel_id=1, source_target_pairs={{0,1},{1,0},{2,3},{3,2},{4,5},{5,4},{6,7},{7,6},{8,9},{9,8},{10,11... | collective-permute-start | bytes 3145736 | tf_op jit(solution)/shard_map/ppermute | solution.py:59
  566.1 23.3 %collective-permute-start.31 = (bf16[512,1024]{1,0:T(8,128)(2,1)}, bf16[512,1024]{1,0:T(8,128)(2,1)S(1)}, u32[]{:S(2)}, u32[]{:S(2)}) collective-permute-start(bf16[512,1024]{1,0:T(8,128)(2,1)} %get-tuple-element.110), channel_id=1, source_target_pairs={{0,2},{2,0},{1,3},{3,1},{4,6},{6,4},{5,7},{7,5},{8,10},{10,8},{9,1... | collective-permute-start | bytes 3145736 | tf_op jit(solution)/shard_map/ppermute | solution.py:63
  594.9 16.8 %collective-permute-start.37 = (bf16[256,1024]{1,0:T(8,128)(2,1)}, bf16[256,1024]{1,0:T(8,128)(2,1)}, u32[]{:S(2)}, u32[]{:S(2)}) collective-permute-start(bf16[256,1024]{1,0:T(8,128)(2,1)} %constant_dynamic-slice_fusion.1), channel_id=1, source_target_pairs={{0,4},{4,0},{1,5},{5,1},{2,6},{6,2},{3,7},{7,3},{8,12},{12,8},{9,1... | collective-permute-start | bytes 1572872 | tf_op jit(solution)/shard_map/ppermute | solution.py:67
  609.9 25.4 %collective-permute-start.34 = (bf16[256,2048]{1,0:T(8,128)(2,1)S(1)}, bf16[256,2048]{1,0:T(8,128)(2,1)}, u32[]{:S(2)}, u32[]{:S(2)}) collective-permute-start(bf16[256,2048]{1,0:T(8,128)(2,1)S(1)} %fusion.9.own), channel_id=1, source_target_pairs={{0,2},{2,0},{1,3},{3,1},{4,6},{6,4},{5,7},{7,5},{8,10},{10,8},{9,1... | collective-permute-start | bytes 3145736 | tf_op jit(solution)/shard_map/ppermute | solution.py:63
  611.4 26.1 %collective-permute-start.33 = (bf16[256,2048]{1,0:T(8,128)(2,1)S(1)}, bf16[256,2048]{1,0:T(8,128)(2,1)}, u32[]{:S(2)}, u32[]{:S(2)}) collective-permute-start(bf16[256,2048]{1,0:T(8,128)(2,1)S(1)} %fusion.9.own), channel_id=1, source_target_pairs={{0,1},{1,0},{2,3},{3,2},{4,5},{5,4},{6,7},{7,6},{8,9},{9,8},{10,11... | collective-permute-start | bytes 3145736 | tf_op jit(solution)/shard_map/ppermute | solution.py:59
  624.7 16.1 %collective-permute-start.39 = (f32[2,256]{1,0:T(2,128)S(1)}, f32[2,256]{1,0:T(2,128)S(1)}, u32[]{:S(2)}, u32[]{:S(2)}) collective-permute-start(f32[2,256]{1,0:T(2,128)S(1)} %pad_maximum_fusion.4), channel_id=1, source_target_pairs={{0,1},{1,0},{2,3},{3,2},{4,5},{5,4},{6,7},{7,6},{8,9},{9,8},{10,11... | collective-permute-start | bytes 6152 | tf_op jit(solution)/shard_map/ppermute | solution.py:59
  637.2 18.7 %collective-permute-start.35 = (bf16[256,1024]{1,0:T(8,128)(2,1)}, bf16[256,1024]{1,0:T(8,128)(2,1)S(1)}, u32[]{:S(2)}, u32[]{:S(2)}) collective-permute-start(bf16[256,1024]{1,0:T(8,128)(2,1)} %slice.179), channel_id=1, source_target_pairs={{0,1},{1,0},{2,3},{3,2},{4,5},{5,4},{6,7},{7,6},{8,9},{9,8},{10,11... | collective-permute-start | bytes 1572872 | tf_op jit(solution)/shard_map/ppermute | solution.py:59
  639.4 16.6 %collective-permute-start.36 = (bf16[256,1024]{1,0:T(8,128)(2,1)}, bf16[256,1024]{1,0:T(8,128)(2,1)S(1)}, u32[]{:S(2)}, u32[]{:S(2)}) collective-permute-start(bf16[256,1024]{1,0:T(8,128)(2,1)} %slice.180), channel_id=1, source_target_pairs={{0,2},{2,0},{1,3},{3,1},{4,6},{6,4},{5,7},{7,5},{8,10},{10,8},{9,1... | collective-permute-start | bytes 1572872 | tf_op jit(solution)/shard_map/ppermute | solution.py:63
  (72 other events, 617.4 us)
Sparse Core Ops, SparseCore 0:
  20.7 64.8 all-gather.3
  87.8 148.3 all-gather.5
  238.3 78.9 all-gather.7
  319.5 75.2 reduce-scatter.5
  397.7 144.9 reduce-scatter.7
  551.9 69.2 reduce-scatter.3

commit v4 on v3

--- a/solution.py
+++ b/solution.py
@@ -192,6 +192,24 @@
     return transposed_product(left, 0, rows, right, first, groups, add, earlier)
 
 
+def add_away(pieces, away):
+    if not square():
+        return [(pieces[0].astype(f32) + away.astype(f32)).astype(bf16)]
+    size, half = pieces[1].shape
+    away = away.reshape(2, 2, size, 2 * half)
+    parts = [
+        away[0, 0, :, :half],
+        away[0, 1, :, :half],
+        away[1, :, :, :half].reshape(2 * size, half),
+        away[0, 0, :, half:],
+        away[1, 0, :, half:],
+        away[:, 1, :, half:].reshape(2 * size, half),
+    ]
+    return [
+        (piece.astype(f32) + part.astype(f32)).astype(piece.dtype) for piece, part in zip(pieces, parts)
+    ]
+
+
 def scatter_near(pieces):
     if not square():
         return ()
@@ -231,6 +249,68 @@
     return scatter_end(pieces, near, scatter_far(scatter_middle(pieces, near)))
 
 
+def rows_backward_kernel(added, *refs):
+    own, got, last = refs[0:2], refs[2:4], refs[4:6]
+    v_ref, base_ref, gain_ref = refs[6 + added : 9 + added]
+    g_ref, low_ref = refs[9 + added :]
+    half = own[0].shape[1]
+    width = 2 * half
+    v = v_ref[...].astype(f32)
+    r = lax.rsqrt(jnp.sum(v * v, axis=-1, keepdims=True) * (1.0 / width) + eps_norm)
+    n = v * r
+    parts = []
+    for i in range(2):
+        columns = slice(i * half, (i + 1) * half)
+        d = own[i][...] + got[i][...].astype(f32) + last[i][...].astype(f32)
+        if added:
+            d = d + refs[6][:, columns].astype(f32)
+        parts.append(d * gain_ref[:, columns])
+    e = jnp.concatenate(parts, axis=1)
+    inner = jnp.sum(e * n, axis=-1, keepdims=True) * (1.0 / width)
+    g = base_ref[...].astype(f32) + r * (e - n * inner)
+    g_ref[...] = g
+    low_ref[...] = g.astype(bf16)
+
+
+def rows_backward(pieces, near, far, away, v, base, gain):
+    if not square():
+        here = pieces[0].shape[0] // lax.axis_size("mp")
+        d = scatter_end(pieces, near, far)
+
+        def own(u):
+            if u.shape[0] == here:
+                return u
+            return lax.dynamic_slice_in_dim(u, lax.axis_index("mp") * here, here, 0)
+
+        v, base = own(v).astype(f32), own(base).astype(f32)
+        r = lax.rsqrt(jnp.mean(v * v, axis=-1, keepdims=True) + eps_norm)
+        n, e = v * r, d * gain
+        g = base + r * (e - n * jnp.mean(e * n, axis=-1, keepdims=True))
+        return g, g.astype(bf16)
+    here, half = pieces[0].shape
+    tm = tile(here, 64)
+    narrow = pl.BlockSpec((tm, half), lambda i: (i, 0))
+    wide = pl.BlockSpec((tm, 2 * half), lambda i: (i, 0))
+    adds = [] if away is None else [away]
+    return pl.pallas_call(
+        functools.partial(rows_backward_kernel, len(adds)),
+        name="rows_backward",
+        grid=(here // tm,),
+        in_specs=[narrow] * 6
+        + [wide] * (len(adds) + 2)
+        + [pl.BlockSpec((1, 2 * half), lambda i: (0, 0))],
+        out_specs=[wide, wide],
+        out_shape=[
+            jax.ShapeDtypeStruct((here, 2 * half), f32),
+            jax.ShapeDtypeStruct((here, 2 * half), bf16),
+        ],
+        cost_estimate=pl.CostEstimate(
+            flops=40 * here * half, transcendentals=here, bytes_accessed=40 * here * half
+        ),
+        compiler_params=pltpu.CompilerParams(vmem_limit_bytes=40 << 20),
+    )(pieces[0], pieces[3], *near, *far, *adds, v, base, gain.reshape(1, -1))
+
+
 def assemble_kernel(order_ref, own, over_x, over_y, diag_a, diag_b, out_ref):
     half = diag_a.shape[1]
     for i, ref in enumerate([own, over_y, over_x]):
@@ -262,6 +342,56 @@
     )(order, *pieces)
 
 
+def join_near_kernel(order_ref, own, over_x, over_y, out_ref):
+    for i, ref in enumerate([own, over_y, over_x]):
+
+        @pl.when(pl.program_id(0) == i)
+        def _(ref=ref):
+            out_ref[...] = ref[...].astype(out_ref.dtype)
+
+
+def join_far_kernel(order_ref, diag_a, diag_b, near_ref, out_ref):
+    half = diag_a.shape[1]
+    out_ref[:, :half] = diag_a[...].astype(out_ref.dtype)
+    out_ref[:, half:] = diag_b[...].astype(out_ref.dtype)
+
+
+def join_near(pieces, dtype):
+    here, width = pieces[0].shape
+    return pl.pallas_call(
+        join_near_kernel,
+        name="join_near",
+        grid_spec=pltpu.PrefetchScalarGridSpec(
+            num_scalar_prefetch=1,
+            grid=(3,),
+            in_specs=[pl.BlockSpec((here, width), lambda i, s: (0, 0))] * 3,
+            out_specs=pl.BlockSpec((here, width), lambda i, s: (s[i], 0)),
+        ),
+        out_shape=jax.ShapeDtypeStruct((4 * here, width), dtype),
+        cost_estimate=pl.CostEstimate(flops=0, transcendentals=0, bytes_accessed=18 * here * width),
+        compiler_params=pltpu.CompilerParams(vmem_limit_bytes=40 << 20),
+    )(block_orders()[0], *pieces)
+
+
+def join_far(pieces, near):
+    here, half = pieces[0].shape
+    return pl.pallas_call(
+        join_far_kernel,
+        name="join_far",
+        grid_spec=pltpu.PrefetchScalarGridSpec(
+            num_scalar_prefetch=1,
+            grid=(1,),
+            in_specs=[pl.BlockSpec((here, half), lambda i, s: (0, 0))] * 2
+            + [pl.BlockSpec(memory_space=pl.ANY)],
+            out_specs=pl.BlockSpec((here, 2 * half), lambda i, s: (s[3], 0)),
+        ),
+        out_shape=jax.ShapeDtypeStruct(near.shape, near.dtype),
+        input_output_aliases={3: 0},
+        cost_estimate=pl.CostEstimate(flops=0, transcendentals=0, bytes_accessed=12 * here * half),
+        compiler_params=pltpu.CompilerParams(vmem_limit_bytes=40 << 20),
+    )(block_orders()[0], *pieces, near)
+
+
 def exchange_near(block):
     if not square():
         return (lax.all_gather(block, "mp", axis=0, tiled=True),)
@@ -293,25 +423,20 @@
     return assemble(order, pieces, dtype)
 
 
-def sum_mp(v):
-    if not square():
-        return lax.psum(v, "mp")
-    v = v + send_x(v)
-    return v + send_y(v)
-
-
-def allowed_block(i, size, seq_len):
-    shape = (size, (i + 1) * size)
+SHORTEST = 512
+FACTOR = HEAD_SIZE ** (-0.5)
+
+
+def probabilities(queries, keys, i, size, seq_len):
+    scores = mm_t(queries, keys)
+    first = min(i * size, SHORTEST)
+    shape = (size, (i + 1) * size - first)
     q_pos = i * size + lax.broadcasted_iota(jnp.int32, shape, 0)
-    k_pos = lax.broadcasted_iota(jnp.int32, shape, 1)
-    return (k_pos <= q_pos) & (k_pos < seq_len)
-
-
-def probabilities(queries, keys, i, size, seq_len):
-    factor = HEAD_SIZE ** (-0.5)
-    scores = mm_t(queries, keys) * factor
-    scores = jnp.where(allowed_block(i, size, seq_len), scores, neg_large)
-    exps = jnp.exp(scores - jnp.max(scores, axis=-1, keepdims=True))
+    k_pos = first + lax.broadcasted_iota(jnp.int32, shape, 1)
+    seen = jnp.where((k_pos <= q_pos) & (k_pos < seq_len), scores[:, first:], neg_large)
+    if first:
+        seen = jnp.concatenate([scores[:, :first], seen], axis=1)
+    exps = jnp.exp(seen - jnp.max(seen, axis=-1, keepdims=True))
     return exps * (1.0 / jnp.sum(exps, axis=-1, keepdims=True))
 
 
@@ -342,7 +467,7 @@
         rows = block_rows(order_ref, i, size)
         here = pl.ds(i * size, size)
         upto = (i + 1) * size
-        queries = rotate(q_ref[rows], cos_ref[here], sin_ref[here]).astype(bf16)
+        queries = (FACTOR * rotate(q_ref[rows], cos_ref[here], sin_ref[here])).astype(bf16)
         probs = probabilities(queries, keys[:upto], i, size, seq_len).astype(bf16)
         out_ref[rows] = mm(probs, values[:upto]).astype(bf16)
 
@@ -355,7 +480,6 @@
     seq_len = len_ref[0]
     step = pl.program_id(0)
     heads = pl.num_programs(0) - 2
-    factor = HEAD_SIZE ** (-0.5)
 
     @pl.when(step == 0)
     def _():
@@ -370,15 +494,16 @@
             here = pl.ds(i * size, size)
             upto = (i + 1) * size
             cos_b, sin_b = cos_ref[here], sin_ref[here]
-            queries = rotate(q_ref[rows], cos_b, sin_b).astype(bf16)
+            queries = (FACTOR * rotate(q_ref[rows], cos_b, sin_b)).astype(bf16)
             grads = g_ref[rows]
             probs = probabilities(queries, keys[:upto], i, size, seq_len)
             d_values[:upto] += mm_rows(probs.astype(bf16), grads)
             d_probs = mm_t(grads, values[:upto])
             inner = jnp.sum(probs * d_probs, axis=-1, keepdims=True)
-            d_scores = (probs * (d_probs - inner) * factor).astype(bf16)
+            d_scores = (probs * (d_probs - inner)).astype(bf16)
             d_keys[:upto] += mm_rows(d_scores, queries)
-            out_ref[rows] = rotate_back(mm(d_scores, keys[:upto]), cos_b, sin_b).astype(bf16)
+            d_queries = FACTOR * mm(d_scores, keys[:upto])
+            out_ref[rows] = rotate_back(d_queries, cos_b, sin_b).astype(bf16)
 
     @pl.when(step == heads)
     def _():
@@ -519,12 +644,57 @@
     return got.reshape(rows, n * mp_size * part)
 
 
-def collect_heads(block, heads):
+def attention_end_kernel(heads, grads_ref, q_ref, kv_ref, gain_ref, sums_ref, out_ref, q_out_ref, send_ref):
+    cols = q_ref.shape[1]
+    size = kv_ref.shape[1] // 2
+    part = size // send_ref.shape[0]
+    out_ref[...] = grads_ref[:, :cols].astype(f32).T
+    q_grad = grads_ref[:, cols : 2 * cols].astype(f32)
+    q_out_ref[...] = q_grad
+    kv_grad = grads_ref[:, 2 * cols :]
+    products = jnp.sum(q_grad * q_ref[...].astype(f32), axis=1, keepdims=True) + jnp.sum(
+        kv_grad.astype(f32) * kv_ref[...].astype(f32), axis=1, keepdims=True
+    )
+    rows = products.shape[0]
+    lane = lax.broadcasted_iota(jnp.int32, (rows, 2 * part), 1)
+    extra = jnp.zeros((rows, 2 * part), f32)
+    for i, v in enumerate([products / gain_ref[...].astype(f32), sums_ref[...]]):
+        high = v.astype(bf16).astype(f32)
+        extra = jnp.where(lane == 2 * i, high, jnp.where(lane == 2 * i + 1, v - high, extra))
+    for m in range(send_ref.shape[0]):
+        for i in range(2):
+            first = i * size + m * part
+            send_ref[m, :, i * part : (i + 1) * part] = kv_grad[:, first : first + part]
+        send_ref[m, :, 2 * part :] = extra.astype(bf16)
+
+
+def attention_end(grads, query_weight, kv_block, gain, ffn_sums):
+    rows, cols = query_weight.shape
     mp_size = lax.axis_size("mp")
-    rows, n, size = block.shape
-    part = size // mp_size
-    got = lax.all_to_all(block.reshape(rows, n, mp_size, part), "mp", 2, 2, tiled=True)
-    return jnp.sum(got.reshape(rows, n, heads, mp_size // heads, part).astype(f32), axis=3)
+    part = kv_block.shape[1] // 2 // mp_size
+    return pl.pallas_call(
+        functools.partial(attention_end_kernel, KEY_VALUE_HEADS),
+        name="attention_end",
+        out_shape=[
+            jax.ShapeDtypeStruct((cols, rows), f32),
+            jax.ShapeDtypeStruct((rows, cols), f32),
+            jax.ShapeDtypeStruct((mp_size, rows, 4 * part), bf16),
+        ],
+        cost_estimate=pl.CostEstimate(
+            flops=8 * rows * cols, transcendentals=0, bytes_accessed=20 * rows * cols
+        ),
+        compiler_params=pltpu.CompilerParams(vmem_limit_bytes=40 << 20),
+    )(grads, query_weight, kv_block, gain.reshape(-1, 1), ffn_sums.reshape(-1, 1))
+
+
+def collect_heads(send, heads):
+    mp_size, rows, width = send.shape
+    part = width // 4
+    got = lax.all_to_all(send, "mp", 0, 0, tiled=True).astype(f32)
+    kept = jnp.sum(got[:, :, : 2 * part].reshape(heads, mp_size // heads, rows, 2 * part), axis=1)
+    extra = jnp.sum(got[:, :, 2 * part : 2 * part + 4], axis=0)
+    kept = jnp.transpose(kept, (1, 0, 2))
+    return kept[:, :, :part], kept[:, :, part:], extra[:, 0] + extra[:, 1], extra[:, 2] + extra[:, 3]
 
 
 def gather_dp(block):
@@ -643,30 +813,31 @@
         ).astype(bf16)
 
 
-def rows_product(mine, away, right, part, parts, into=None, earlier=()):
+def rows_product(mine, away, right, start, share, into=None, earlier=()):
     rows, width = mine.shape
     cols = 2 * right.shape[2]
-    tm = tile(width // parts, 256)
-    steps = width // parts // tm
+    tm = tile(width // 4, 256)
+    steps = share * width // 4 // tm
+    begin = start * width // 4 // tm
     more = ([] if into is None else [into]) + list(earlier)
     return pl.pallas_call(
         rows_product_kernel,
         name="rows_product",
         grid=(steps,),
         in_specs=[
-            pl.BlockSpec((rows, tm), lambda i: (0, part * steps + i)),
-            pl.BlockSpec((rows, tm), lambda i: (0, part * steps + i)),
+            pl.BlockSpec((rows, tm), lambda i: (0, begin + i)),
+            pl.BlockSpec((rows, tm), lambda i: (0, begin + i)),
             pl.BlockSpec((2, rows, cols // 2), lambda i: (0, 0, 0)),
             pl.BlockSpec((2, rows, cols // 2), lambda i: (0, 1, 0)),
         ]
         + [pl.BlockSpec(memory_space=pl.ANY)] * len(more),
-        out_specs=pl.BlockSpec((tm, cols), lambda i: (part * steps + i, 0)),
+        out_specs=pl.BlockSpec((tm, cols), lambda i: (begin + i, 0)),
         out_shape=jax.ShapeDtypeStruct((width, cols), bf16),
         input_output_aliases={} if into is None else {4: 0},
         cost_estimate=pl.CostEstimate(
-            flops=4 * rows * width * cols // parts,
+            flops=4 * rows * width * cols * share // 4,
             transcendentals=0,
-            bytes_accessed=(4 * rows * width + 2 * width * cols) // parts + 4 * rows * cols,
+            bytes_accessed=(4 * rows * width + 2 * width * cols) * share // 4 + 4 * rows * cols,
         ),
         compiler_params=pltpu.CompilerParams(vmem_limit_bytes=56 << 20),
     )(mine, away, right, right, *more)
@@ -760,22 +931,26 @@
     ffn_away = away_product(hidden, w_d, slots, (down_grad,))
     ffn_add = send_core(ffn_away)
     d_gu = ffn_backward(grad_all, w_d, factors, ffn_away)
-    gu_grad = rows_product(h_mine, h_away, d_gu, 0, 1, earlier=(d_gu,))
+    ffn_pieces = scatter_product(hidden, w_d, 0, slots, ffn_add, (d_gu,))
+    ffn_near = scatter_near(ffn_pieces)
+    gu_grad = rows_product(h_mine, h_away, d_gu, 0, 2, earlier=(ffn_pieces[-1],))
+    h2_away = away_product(d_gu, w_gu, slots, (gu_grad,))
+    ffn_middle = scatter_middle(ffn_pieces, ffn_near)
+    gu_grad = rows_product(h_mine, h_away, d_gu, 2, 2, gu_grad, (h2_away, *ffn_middle))
+    gu_grad, down_out = tie(gu_grad, down_out)
     gu_out = reduce_z(gu_grad)
-    ffn_pieces = scatter_product(hidden, w_d, 0, slots, ffn_add, (gu_grad,))
-    ffn_near = scatter_near(ffn_pieces)
-    h2_away = away_product(d_gu, w_gu, slots, (ffn_pieces[-1],))
     h2_add = send_core(h2_away)
-    ffn_middle = scatter_middle(ffn_pieces, ffn_near)
     ffn_far = scatter_far(ffn_middle)
-    h2_pieces = scatter_product(d_gu, w_gu, 0, slots, h2_add)
-    h2_pieces, ffn_far = tie(h2_pieces, ffn_far)
+    h2_pieces = list(scatter_product(d_gu, w_gu, 0, slots, earlier=(gu_grad,)))
+    h2_pieces[0], h2_add = tie(h2_pieces[0], h2_add)
+    h2_summed = add_away(h2_pieces, h2_add)
+    h2_summed[-1], ffn_far = tie(h2_summed[-1], ffn_far)
     ffn_rows = scatter_end(ffn_pieces, ffn_near, ffn_far)
-    d_h2 = scatter_rows(h2_pieces)
-
-    e2 = d_h2 * g_ffn
-    g1 = own_rows(grad_mine).astype(f32) + r2 * (e2 - n2 * jnp.mean(e2 * n2, axis=-1, keepdims=True))
-    g1_low = join_rows(exchange_rows(g1.astype(bf16)), True)
+    h2_near = scatter_near(h2_summed)
+    h2_far = scatter_far(scatter_middle(h2_summed, h2_near))
+    kept, h2_own = (h2_pieces, h2_add) if square() else (h2_summed, None)
+    g1, g1_block = rows_backward(kept, h2_near, h2_far, h2_own, mid, grad_mine, g_ffn)
+    g1_low = join_rows(exchange_rows(g1_block), True)
 
     layer_block, g1_low = tie((mid + ffn_rows).astype(bf16), g1_low)
     layer_near = exchange_near(layer_block)
@@ -788,46 +963,37 @@
     h1_pieces = scatter_product(d_qkv, w_attn, 0, slots, earlier=(attn_grads,))
     h1_pieces, layer_far = tie(h1_pieces, layer_far)
     layer_out = join_rows((layer_block, *layer_near, *layer_far), False)
-    d_h1 = scatter_rows(h1_pieces)
-    r1_here = own_rows(r1)
-    n1 = tok_here * r1_here
-    e1 = d_h1 * g_attn
-    grad_in = g1 + r1_here * (e1 - n1 * jnp.mean(e1 * n1, axis=-1, keepdims=True))
-    grad_pieces = exchange_rows(grad_in.astype(bf16))
-
-    rows_here = gain_attn.shape[0]
-
+    h1_near = scatter_near(h1_pieces)
     (down_out,) = from_core(down_out, 1, True)
     gate_out, up_out = from_core(gu_out, 2, earlier=(down_out,))
-    out_out, q_out = attn_out[:, :q_cols], attn_out[:, q_cols : 2 * q_cols].astype(f32)
-    kv_out = attn_out[:, 2 * q_cols :]
-    kv_grad = collect_heads(kv_out.reshape(rows_here, 2, HEAD_SIZE), KEY_VALUE_HEADS)
-
-    def row_sums(*pairs):
-        return sum(jnp.sum(w.astype(f32) * g.astype(f32), axis=1) for w, g in pairs)
-
-    gain_sums = sum_mp(
-        jnp.stack(
-            [
-                row_sums((query_weight, q_out), (kv_block, kv_out)),
-                row_sums((gate_weight, gate_out), (up_weight, up_out)),
-            ]
-        )
-    )
-    gain_attn_grad = gain_sums[0] / gain_attn.astype(f32)
-    gain_ffn_grad = gain_sums[1] / gain_ffn.astype(f32)
-    grad_pieces, kv_grad, down_out, gate_out, up_out = tie(
-        grad_pieces, kv_grad, down_out, gate_out, up_out
-    )
-    grad_input = join_rows(grad_pieces, False, f32)
+    h1_near, gate_out, up_out, layer_out = tie(h1_near, gate_out, up_out, layer_out)
+    h1_far = scatter_far(scatter_middle(h1_pieces, h1_near))
+    _, grad_block = rows_backward(h1_pieces, h1_near, h1_far, None, x_rel, g1, g_attn)
+    grad_pieces = list(exchange_rows(grad_block))
+    grad_pieces[0], attn_out = tie(grad_pieces[0], attn_out)
+
+    rows_here = gain_attn.shape[0]
+
+    ffn_sums = sum(
+        jnp.sum(w.astype(f32) * g, axis=1) for w, g in [(gate_weight, gate_out), (up_weight, up_out)]
+    ) / gain_ffn.astype(f32)
+    out_out, q_out, send = attention_end(attn_out, query_weight, kv_block, gain_attn, ffn_sums)
+    if square():
+        joined = join_near(grad_pieces[:3], f32)
+        *far_pieces, send, joined = tie(*grad_pieces[3:], send, joined)
+    key_grad, value_grad, gain_attn_grad, gain_ffn_grad = collect_heads(send, KEY_VALUE_HEADS)
+    if square():
+        grad_input = join_far(far_pieces, joined)
+    else:
+        grad_input = grad_pieces[1].astype(f32)
     return (
         layer_out[None],
         grad_input[None],
         gain_attn_grad,
         q_out,
-        kv_grad[:, 0],
-        kv_grad[:, 1],
-        out_out.T.astype(f32),
+        key_grad,
+        value_grad,
+        out_out,
         gain_ffn_grad,
         gate_out,
         up_out,

time: 675 us -> 664 us (0.984)
  other arithmetic: 45.3 us -> 29.5 us
  Pallas kernels: 204 us -> 219 us
    pallas_call x0 -> x5, Pallas kernels: none -> 15.9 us  [the longest x2 7.98 us: rows_backward(): pl.pallas_call(functools.partial(rows_backward_kernel, len(adds)), name='...]
    ppermute x17 -> x16, waiting for transfers between devices: 110 us -> 101 us  [send_x(): return lax.ppermute(v, 'mp', OVER_X)]
    pallas_call x1 -> x2, Pallas kernels: 23.9 us -> 28.6 us  [rows_product(): pl.pallas_call(rows_product_kernel, name='rows_product', grid=(steps,), i...]
    ppermute x17 -> x16, starting transfers between devices: 19.7 us -> 17.9 us  [send_y(): return lax.ppermute(v, 'mp', OVER_Y)]
    unnamed x115 -> x120, local copies, waits for them, and re-layouts: 23.3 us -> 24.8 us
    ppermute x17 -> x16, waiting for transfers between devices: 75.7 us -> 74.6 us  [send_y(): return lax.ppermute(v, 'mp', OVER_Y)]
    ppermute x17 -> x16, starting transfers between devices: 17.3 us -> 18 us  [send_x(): return lax.ppermute(v, 'mp', OVER_X)]
  transfers between devices with their start and end apart: 49 -> 47, of which waited for: 25 -> 28; matrix products, arithmetic and copies ran while one was open for 12% -> 9% of each run, Pallas kernels for 30% -> 33%
where the time goes in v4:
time: 664 us; the launch traced here: 659 us
  waiting for transfers between devices  282 us (42%)
  Pallas kernels  219 us (33%)
  starting transfers between devices  45.9 us (7%)
  local copies, waits for them, and re-layouts  39.9 us (6%)
  other arithmetic  29.5 us (4%)
  between operations  15.8 us (2%)
  matrix products  14 us (2%)
  blocking collectives  12.5 us (2%)
    ppermute x16, waiting for transfers between devices, send_x(): return lax.ppermute(v, 'mp', OVER_X)  101 us
    ppermute x16, waiting for transfers between devices, send_y(): return lax.ppermute(v, 'mp', OVER_Y)  74.6 us
    all_gather x2, waiting for transfers between devices, gather_z(): return lax.all_gather(block, 'z', axis=0, tiled=True)  71.3 us
    pallas_call x6, Pallas kernels, transposed_product(): pl.pallas_call(functools.partial(transposed_product_kernel, groups, add i...  64.5 us
    pallas_call x2, Pallas kernels, rows_product(): pl.pallas_call(rows_product_kernel, name='rows_product', grid=(steps,), i...  28.6 us
    pallas_call x1, Pallas kernels, ffn_forward(): pl.pallas_call(ffn_forward_kernel, name='ffn_forward', grid=(2, ff // tn)...  26.2 us
    unnamed x120, local copies, waits for them, and re-layouts  24.8 us
    all_gather x1, waiting for transfers between devices, gather_dp(): return lax.all_gather(block, DP, axis=0, tiled=True)  22.4 us
  transfers between devices with their start and end apart: 47, of which 28 were waited for; matrix products, arithmetic and copies ran while one was open for 9% of the time, Pallas kernels for 33%

profile of v4, /device:TPU:0, one launch (start us, length us, event | category | flops | bytes accessed | tf_op | source)
XLA Modules:
  0.0 658.9 jit_solution(10819938787583002391)
XLA Ops:
  38.4 5.6 prepare.1
  44.0 12.5 %all_gather.12 = bf16[2,2048]{1,0:T(2,128)(2,1)S(1)} all-gather(bf16[2,256]{1,0:T(2,128)(2,1)S(1)} %pad_maximum_fusion.4), channel_id=1, replica_groups=mesh['z'=4,'core'=2,'mp'=4] {'z','core'}, dimensions={1}, use_global_device_ids=true | all-gather | bytes 9216 | tf_op jit(solution)/shard_map/all_gather | solution.py:909
  64.3 22.4 %all-gather.4.cloned.1.call-done.right_ref = bf16[2048,1536]{1,0:T(8,128)(2,1)} async-done(((bf16[256,1536]{1,0:T(8,128)(2,1)}), bf16[2048,1536]{1,0:T(8,128)(2,1)}) %all-gather.4.cloned.1.call-update) | async-done | bytes 6291472 | tf_op jit(solution)/shard_map/all_gather | solution.py:701
  86.7 9.0 %column_product.2.q_ref.k_ref.v_ref = f32[1024,1024]{1,0:T(8,128)} custom-call(bf16[1024,2048]{1,0:T(8,128)(2,1)} %fusion.2.left_ref.h_ref, bf16[2048,1536]{1,0:T(8,128)(2,1)} %all-gather.4.cloned.1.call-done.right_ref), custom_call_target="tpu_custom_call" | custom-call | flops 4294967296 | bytes 12582912 | tf_op jit(solution)/shard_map/column_product/pallas_call | solution.py:100
  95.7 8.2 %attention_forward.1.left_ref.context_ref = bf16[1024,512]{1,0:T(8,128)(2,1)} custom-call(s32[4]{0:T(128)} %fusion.14.order_ref, s32[1]{0:T(128)S(6)} %copy.65.len_ref, f32[1024,1024]{1,0:T(8,128)} %column_product.2.q_ref.k_ref.v_ref, f32[1024,1024]{1,0:T(8,128)} %column_product.2.q_ref.k_ref.v_ref, f32[1024,1024]{1,0:T(8,128)} %column_product.2.q_ref.k_ref.v_ref, ...), custom_call_target="tpu_custom_call" | custom-call | flops 1610612736 | bytes 8388608 | tf_op jit(solution)/shard_map/attention_forward/pallas_call | solution.py:536
  103.9 7.1 %transposed_product.6 = (f32[256,1024]{1,0:T(8,128)}, bf16[256,1024]{1,0:T(8,128)(2,1)}, bf16[512,1024]{1,0:T(8,128)(2,1)}, f32[256,1024]{1,0:T(8,128)}, bf16[25...) custom-call(bf16[1024,512]{1,0:T(8,128)(2,1)} %attention_forward.1.left_ref.context_ref, ...), custom_call_target="tpu_custom_call" | custom-call | flops 2147483648 | bytes 7340032 | tf_op jit(solution)/shard_map/transposed_product/pallas_call | solution.py:151
  114.1 22.5 %collective-permute-done = bf16[512,1024]{1,0:T(8,128)(2,1)S(1)} collective-permute-done((bf16[512,1024]{1,0:T(8,128)(2,1)}, bf16[512,1024]{1,0:T(8,128)(2,1)S(1)}, u32[]{:S(2)}, u32[]{:S(2)}) %collective-permute-start) | collective-permute-done | bytes 1048608 | tf_op jit(solution)/shard_map/ppermute | solution.py:59
  142.3 9.0 %collective-permute-done.1 = bf16[256,1024]{1,0:T(8,128)(2,1)S(1)} collective-permute-done((bf16[256,1024]{1,0:T(8,128)(2,1)S(1)}, bf16[256,1024]{1,0:T(8,128)(2,1)S(1)}, u32[]{:S(2)}, u32[]{:S(2)}) %collective-permute-start.1) | collective-permute-done | bytes 524320 | tf_op jit(solution)/shard_map/ppermute | solution.py:63
  158.0 21.5 %collective-permute-done.5.over_y = bf16[256,2048]{1,0:T(8,128)(2,1)S(1)} collective-permute-done((bf16[256,2048]{1,0:T(8,128)(2,1)S(1)}, bf16[256,2048]{1,0:T(8,128)(2,1)S(1)}, u32[]{:S(2)}, u32[]{:S(2)}) %collective-permute-start.5) | collective-permute-done | bytes 1048608 | tf_op jit(solution)/shard_map/ppermute | solution.py:63
  182.1 8.9 %collective-permute-done.6.diag_a = bf16[256,1024]{1,0:T(8,128)(2,1)S(1)} collective-permute-done((bf16[256,1024]{1,0:T(8,128)(2,1)S(1)}, bf16[256,1024]{1,0:T(8,128)(2,1)S(1)}, u32[]{:S(2)}, u32[]{:S(2)}) %collective-permute-start.6) | collective-permute-done | bytes 524320 | tf_op jit(solution)/shard_map/ppermute | solution.py:59
  206.6 30.6 %all-gather.6.cloned.1.call-done.g_ref.u_ref.right_ref = bf16[2048,2048]{1,0:T(8,128)(2,1)} async-done(((bf16[512,2048]{1,0:T(8,128)(2,1)}), bf16[2048,2048]{1,0:T(8,128)(2,1)}) %all-gather.6.cloned.1.call-update) | async-done | bytes 8388624 | tf_op jit(solution)/shard_map/all_gather | solution.py:709
  237.2 26.2 %ffn_forward.1 = (bf16[2048,1024]{1,0:T(8,128)(2,1)}, bf16[2,2048,1024]{2,1,0:T(8,128)(2,1)}) custom-call(bf16[1024,2048]{1,0:T(8,128)(2,1)} %assemble.3.mine_ref, bf16[1024,2048]{1,0:T(8,128)(2,1)} %collective-permute-done.8.away_ref, bf16[2048,2048]{1,0:T(8,128)(2,1)} %all-gather.6.cloned.1.call-done.g_ref.u_ref.right_ref, ...), custom_call_target="tpu_custom_call" | custom-call | flops 17179869184 | bytes 29360128 | tf_op jit(solution)/shard_map/ffn_forward/pallas_call | solution.py:780
  263.4 14.0 %convolution_convert_fusion.refs_0_ = bf16[2048,1024]{1,0:T(8,128)(2,1)} fusion(bf16[2048,2048]{1,0:T(8,128)(2,1)} %constant_dynamic-update-slice_fusion.grad_ref, bf16[2048,1024]{1,0:T(8,128)(2,1)} %get-tuple-element.80.left_ref), kind=kOutput, calls=%fused_computation.5 | convolution fusion | flops 8592031744 | bytes 16777216 | tf_op jit(solution)/shard_map/dot_general | solution.py:49
  277.6 40.8 %all-gather.8.cloned.1.call-done.right_ref.d_ref = bf16[2048,1024]{1,0:T(8,128)(2,1)} async-done(((bf16[512,1024]{1,0:T(8,128)(2,1)}), bf16[2048,1024]{1,0:T(8,128)(2,1)}) %all-gather.8.cloned.1.call-update) | async-done | bytes 4194320 | tf_op jit(solution)/shard_map/all_gather | solution.py:709
  318.4 8.8 %transposed_product.7.earlier_ref = bf16[1024,2048]{1,0:T(8,128)(2,1)} custom-call(bf16[2048,1024]{1,0:T(8,128)(2,1)} %get-tuple-element.80.left_ref, bf16[2048,1024]{1,0:T(8,128)(2,1)} %all-gather.8.cloned.1.call-done.right_ref.d_ref, bf16[2048,1024]{1,0:T(8,128)(2,1)} %convolution_convert_fusion.refs_0_), custom_call_target="tpu_custom_call" | custom-call | flops 4294967296 | bytes 10485760 | tf_op jit(solution)/shard_map/transposed_product/pallas_call | solution.py:151
  327.2 18.0 %ffn_backward.1.refs_1_.right_mine_ref.right_away_ref.left_ref = bf16[2,2048,1024]{2,1,0:T(8,128)(2,1)} custom-call(bf16[2048,2048]{1,0:T(8,128)(2,1)} %constant_dynamic-update-slice_fusion.grad_ref, bf16[2048,1024]{1,0:T(8,128)(2,1)} %all-gather.8.cloned.1.call-done.right_ref.d_ref, bf16[2,2048,1024]{2,1,0:T(8,128)(2,1)} %get-tuple-element.82.factor_ref, ...), custom_call_target="tpu_custom_call" | custom-call | flops 8589934592 | bytes 29360128 | tf_op jit(solution)/shard_map/ffn_backward/pallas_call | solution.py:856
  347.2 10.1 %transposed_product.8 = (f32[256,1024]{1,0:T(8,128)}, bf16[256,1024]{1,0:T(8,128)(2,1)}, bf16[512,1024]{1,0:T(8,128)(2,1)}, f32[256,1024]{1,0:T(8,128)}, bf16[25...) custom-call(bf16[2048,1024]{1,0:T(8,128)(2,1)} %get-tuple-element.80.left_ref, ...), custom_call_target="tpu_custom_call" | custom-call | flops 4294967296 | bytes 10485760 | tf_op jit(solution)/shard_map/transposed_product/pallas_call | solution.py:151
  360.3 14.3 %rows_product.2.refs_0_ = bf16[2048,2048]{1,0:T(8,128)(2,1)} custom-call(bf16[1024,2048]{1,0:T(8,128)(2,1)} %assemble.3.mine_ref, bf16[1024,2048]{1,0:T(8,128)(2,1)} %collective-permute-done.8.away_ref, bf16[2,2048,1024]{2,1,0:T(8,128)(2,1)} %ffn_backward.1.refs_1_.right_mine_ref.right_away_ref.left_ref, ...), custom_call_target="tpu_custom_call" | custom-call | flops 8589934592 | bytes 16777216 | tf_op jit(solution)/shard_map/rows_product/pallas_call | solution.py:823
  374.5 13.9 %transposed_product.9.refs_1_ = bf16[1024,2048]{1,0:T(8,128)(2,1)} custom-call(bf16[2,2048,1024]{2,1,0:T(8,128)(2,1)} %ffn_backward.1.refs_1_.right_mine_ref.right_away_ref.left_ref, bf16[2048,2048]{1,0:T(8,128)(2,1)} %all-gather.6.cloned.1.call-done.g_ref.u_ref.right_ref, bf16[2048,2048]{1,0:T(8,128)(2,1)} %rows_product.2.refs_0_), custom_call_target="tpu_custom_call" | custom-call | flops 8589934592 | bytes 16777216 | tf_op jit(solution)/shard_map/transposed_product/pallas_call | solution.py:151
  392.5 14.4 %rows_product.3.refs_0_ = bf16[2048,2048]{1,0:T(8,128)(2,1)} custom-call(bf16[1024,2048]{1,0:T(8,128)(2,1)} %assemble.3.mine_ref, bf16[1024,2048]{1,0:T(8,128)(2,1)} %collective-permute-done.8.away_ref, bf16[2,2048,1024]{2,1,0:T(8,128)(2,1)} %ffn_backward.1.refs_1_.right_mine_ref.right_away_ref.left_ref, ...), custom_call_target="tpu_custom_call", output_to_operand_aliasing={{}: (4, {})} | custom-call | flops 8589934592 | bytes 16777216 | tf_op jit(solution)/shard_map/rows_product/pallas_call | solution.py:823
  409.0 15.2 %transposed_product.10 = (f32[256,1024]{1,0:T(8,128)}, bf16[256,1024]{1,0:T(8,128)(2,1)}, bf16[512,1024]{1,0:T(8,128)(2,1)}, f32[256,1024]{1,0:T(8,128)}, bf16[2...) custom-call(bf16[2,2048,1024]{2,1,0:T(8,128)(2,1)} %ffn_backward.1.refs_1_.right_mine_ref.right_away_ref.left_ref, ...), custom_call_target="tpu_custom_call" | custom-call | flops 8589934592 | bytes 16777216 | tf_op jit(solution)/shard_map/transposed_product/pallas_call | solution.py:151
  430.3 20.7 %collective-permute-done.18.refs_3_ = bf16[512,1024]{1,0:T(8,128)(2,1)S(1)} collective-permute-done((bf16[512,1024]{1,0:T(8,128)(2,1)S(1)}, bf16[512,1024]{1,0:T(8,128)(2,1)S(1)}, u32[]{:S(2)}, u32[]{:S(2)}) %collective-permute-start.18) | collective-permute-done | bytes 1048608 | tf_op jit(solution)/shard_map/ppermute | solution.py:63
  455.6 9.3 %collective-permute-done.20.refs_5_ = bf16[256,1024]{1,0:T(8,128)(2,1)S(1)} collective-permute-done((bf16[256,1024]{1,0:T(8,128)(2,1)S(1)}, bf16[256,1024]{1,0:T(8,128)(2,1)S(1)}, u32[]{:S(2)}, u32[]{:S(2)}) %collective-permute-start.20) | collective-permute-done | bytes 524320 | tf_op jit(solution)/shard_map/ppermute | solution.py:59
  473.0 18.9 %collective-permute-done.22.over_y = bf16[256,2048]{1,0:T(8,128)(2,1)S(1)} collective-permute-done((bf16[256,2048]{1,0:T(8,128)(2,1)S(1)}, bf16[256,2048]{1,0:T(8,128)(2,1)S(1)}, u32[]{:S(2)}, u32[]{:S(2)}) %collective-permute-start.22) | collective-permute-done | bytes 1048608 | tf_op jit(solution)/shard_map/ppermute | solution.py:63
  495.4 8.7 %collective-permute-done.23.diag_a = bf16[256,1024]{1,0:T(8,128)(2,1)S(1)} collective-permute-done((bf16[256,1024]{1,0:T(8,128)(2,1)S(1)}, bf16[256,1024]{1,0:T(8,128)(2,1)S(1)}, u32[]{:S(2)}, u32[]{:S(2)}) %collective-permute-start.23) | collective-permute-done | bytes 524320 | tf_op jit(solution)/shard_map/ppermute | solution.py:59
  508.2 5.8 column_product.3.g_ref
  514.1 12.8 %attention_backward.1.d_qkv_ref.left_ref = bf16[1024,1024]{1,0:T(8,128)(2,1)} custom-call(s32[4]{0:T(128)} %fusion.14.order_ref, s32[1]{0:T(128)S(6)} %copy.65.len_ref, f32[1024,1024]{1,0:T(8,128)} %column_product.2.q_ref.k_ref.v_ref, f32[1024,1024]{1,0:T(8,128)} %column_product.2.q_ref.k_ref.v_ref, f32[1024,1024]{1,0:T(8,128)} %column_product.2.q_ref.k_ref.v_ref, ...), custom_call_target="tpu_custom_call" | custom-call | flops 3758096384 | bytes 8388608 | tf_op jit(solution)/shard_map/attention_backward/pallas_call | solution.py:559
  531.1 11.7 %attention_products.1.refs_0_ = bf16[2048,1536]{1,0:T(8,128)(2,1)} custom-call(bf16[1024,2048]{1,0:T(8,128)(2,1)} %copy-done.2, bf16[1024,512]{1,0:T(8,128)(2,1)} %attention_forward.1.left_ref.context_ref, bf16[1024,2048]{1,0:T(8,128)(2,1)} %fusion.2.left_ref.h_ref, bf16[1024,1024]{1,0:T(8,128)(2,1)} %attention_backward.1.d_qkv_ref.left_ref, ...), custom_call_target="tpu_custom_call" | custom-call | flops 6442450944 | bytes 17825792 | tf_op jit(solution)/shard_map/attention_products/pallas_call | solution.py:592
  544.1 9.4 %transposed_product.11 = (f32[256,1024]{1,0:T(8,128)}, bf16[256,1024]{1,0:T(8,128)(2,1)}, bf16[512,1024]{1,0:T(8,128)(2,1)}, f32[256,1024]{1,0:T(8,128)}, bf16[2...) custom-call(bf16[1024,1024]{1,0:T(8,128)(2,1)} %attention_backward.1.d_qkv_ref.left_ref, ...), custom_call_target="tpu_custom_call" | custom-call | flops 4294967296 | bytes 10485760 | tf_op jit(solution)/shard_map/transposed_product/pallas_call | solution.py:151
  570.1 10.6 %collective-permute-done.29.refs_2_ = bf16[512,1024]{1,0:T(8,128)(2,1)S(1)} collective-permute-done((bf16[512,1024]{1,0:T(8,128)(2,1)}, bf16[512,1024]{1,0:T(8,128)(2,1)S(1)}, u32[]{:S(2)}, u32[]{:S(2)}) %collective-permute-start.29) | collective-permute-done | bytes 1048608 | tf_op jit(solution)/shard_map/ppermute | solution.py:59
  584.9 10.6 %collective-permute-done.34.refs_5_ = bf16[256,1024]{1,0:T(8,128)(2,1)S(1)} collective-permute-done((bf16[256,1024]{1,0:T(8,128)(2,1)S(1)}, bf16[256,1024]{1,0:T(8,128)(2,1)S(1)}, u32[]{:S(2)}, u32[]{:S(2)}) %collective-permute-start.34) | collective-permute-done | bytes 524320 | tf_op jit(solution)/shard_map/ppermute | solution.py:59
  604.1 20.0 %collective-permute-done.37.over_x = bf16[256,2048]{1,0:T(8,128)(2,1)S(1)} collective-permute-done((bf16[256,2048]{1,0:T(8,128)(2,1)S(1)}, bf16[256,2048]{1,0:T(8,128)(2,1)S(1)}, u32[]{:S(2)}, u32[]{:S(2)}) %collective-permute-start.37) | collective-permute-done | bytes 1048608 | tf_op jit(solution)/shard_map/ppermute | solution.py:59
  (280 shorter events, 171.9 us)
Async XLA Ops:
  14.1 72.5 %all-gather.4.cloned.1.call-start = ((), (), s32[]{:S(2)}) async-start(), calls=%async_computation.5 | async-start | bytes 7077888 | tf_op jit(solution)/shard_map/all_gather | solution.py:701
  21.7 215.5 %all-gather.6.cloned.1.call-start = ((), (), s32[]{:S(2)}) async-start(), calls=%async_computation.6 | async-start | bytes 10485760 | tf_op jit(solution)/shard_map/all_gather | solution.py:709
  35.4 283.0 %all-gather.8.cloned.1.call-start = ((), (), s32[]{:S(2)}) async-start(), calls=%async_computation.7 | async-start | bytes 5242880 | tf_op jit(solution)/shard_map/all_gather | solution.py:709
  111.0 25.6 %collective-permute-start = (bf16[512,1024]{1,0:T(8,128)(2,1)}, bf16[512,1024]{1,0:T(8,128)(2,1)S(1)}, u32[]{:S(2)}, u32[]{:S(2)}) collective-permute-start(bf16[512,1024]{1,0:T(8,128)(2,1)} %get-tuple-element.75), channel_id=1, source_target_pairs={{0,1},{1,0},{2,3},{3,2},{4,5},{5,4},{6,7},{7,6},{8,9},{9,8},{10,11... | collective-permute-start | bytes 3145736 | tf_op jit(solution)/shard_map/ppermute | solution.py:59
  112.5 26.9 %collective-permute-start.2 = (bf16[512,1024]{1,0:T(8,128)(2,1)}, bf16[512,1024]{1,0:T(8,128)(2,1)S(1)}, u32[]{:S(2)}, u32[]{:S(2)}) collective-permute-start(bf16[512,1024]{1,0:T(8,128)(2,1)} %get-tuple-element.78), channel_id=1, source_target_pairs={{0,2},{2,0},{1,3},{3,1},{4,6},{6,4},{5,7},{7,5},{8,10},{10,8},{9,1... | collective-permute-start | bytes 3145736 | tf_op jit(solution)/shard_map/ppermute | solution.py:63
  137.8 13.5 %collective-permute-start.1 = (bf16[256,1024]{1,0:T(8,128)(2,1)S(1)}, bf16[256,1024]{1,0:T(8,128)(2,1)S(1)}, u32[]{:S(2)}, u32[]{:S(2)}) collective-permute-start(bf16[256,1024]{1,0:T(8,128)(2,1)S(1)} %add_convert_fusion.7), channel_id=1, source_target_pairs={{0,2},{2,0},{1,3},{3,1},{4,6},{6,4},{5,7},{7,5},{8,10},{10,8},{9,1... | collective-permute-start | bytes 1572872 | tf_op jit(solution)/shard_map/ppermute | solution.py:63
  140.7 13.1 %collective-permute-start.3 = (bf16[256,1024]{1,0:T(8,128)(2,1)S(1)}, bf16[256,1024]{1,0:T(8,128)(2,1)S(1)}, u32[]{:S(2)}, u32[]{:S(2)}) collective-permute-start(bf16[256,1024]{1,0:T(8,128)(2,1)S(1)} %add_convert_fusion.6), channel_id=1, source_target_pairs={{0,1},{1,0},{2,3},{3,2},{4,5},{5,4},{6,7},{7,6},{8,9},{9,8},{10,11... | collective-permute-start | bytes 1572872 | tf_op jit(solution)/shard_map/ppermute | solution.py:59
  155.9 23.6 %collective-permute-start.5 = (bf16[256,2048]{1,0:T(8,128)(2,1)S(1)}, bf16[256,2048]{1,0:T(8,128)(2,1)S(1)}, u32[]{:S(2)}, u32[]{:S(2)}) collective-permute-start(bf16[256,2048]{1,0:T(8,128)(2,1)S(1)} %multiply_convert_fusion.own), channel_id=1, source_target_pairs={{0,2},{2,0},{1,3},{3,1},{4,6},{6,4},{5,7},{7,5},{8,10},{10,8},{9,1... | collective-permute-start | bytes 3145736 | tf_op jit(solution)/shard_map/ppermute | solution.py:63
  156.5 24.6 %collective-permute-start.4 = (bf16[256,2048]{1,0:T(8,128)(2,1)S(1)}, bf16[256,2048]{1,0:T(8,128)(2,1)S(1)}, u32[]{:S(2)}, u32[]{:S(2)}) collective-permute-start(bf16[256,2048]{1,0:T(8,128)(2,1)S(1)} %multiply_convert_fusion.own), channel_id=1, source_target_pairs={{0,1},{1,0},{2,3},{3,2},{4,5},{5,4},{6,7},{7,6},{8,9},{9,8},{10,11... | collective-permute-start | bytes 3145736 | tf_op jit(solution)/shard_map/ppermute | solution.py:59
  182.1 19.7 %collective-permute-start.10 = (bf16[1024,2048]{1,0:T(8,128)(2,1)}, bf16[1024,2048]{1,0:T(8,128)(2,1)}, u32[]{:S(2)}, u32[]{:S(2)}) collective-permute-start(bf16[1024,2048]{1,0:T(8,128)(2,1)} %get-tuple-element.81.refs_8_), channel_id=1, source_target_pairs={{0,4},{4,0},{1,5},{5,1},{2,6},{6,2},{3,7},{7,3},{8,12},{12,8},{9,1... | collective-permute-start | bytes 12582920 | tf_op jit(solution)/shard_map/ppermute | solution.py:67
  195.4 41.8 %collective-permute-start.8 = (bf16[1024,2048]{1,0:T(8,128)(2,1)}, bf16[1024,2048]{1,0:T(8,128)(2,1)}, u32[]{:S(2)}, u32[]{:S(2)}) collective-permute-start(bf16[1024,2048]{1,0:T(8,128)(2,1)} %assemble.3.mine_ref), channel_id=1, source_target_pairs={{0,4},{4,0},{1,5},{5,1},{2,6},{6,2},{3,7},{7,3},{8,12},{12,8},{9,1... | collective-permute-start | bytes 12582920 | tf_op jit(solution)/shard_map/ppermute | solution.py:67
  196.5 210.4 %reduce-scatter.4.cloned.1.call-start = ((), (), s32[]{:S(2)}) async-start(), calls=%async_computation.8 | async-start | bytes 5242880 | tf_op jit(solution)/shard_map/reduce_scatter | solution.py:713
  277.4 276.1 %reduce-scatter.6.cloned.1.call-start = ((), (), s32[]{:S(2)}) async-start(), calls=%async_computation.9 | async-start | bytes 10485760 | tf_op jit(solution)/shard_map/reduce_scatter | solution.py:713
  327.2 18.0 %collective-permute-start.11 = (bf16[1024,2048]{1,0:T(8,128)(2,1)}, bf16[1024,2048]{1,0:T(8,128)(2,1)S(1)}, u32[]{:S(2)}, u32[]{:S(2)}) collective-permute-start(bf16[1024,2048]{1,0:T(8,128)(2,1)} %transposed_product.7.earlier_ref), channel_id=1, source_target_pairs={{0,4},{4,0},{1,5},{5,1},{2,6},{6,2},{3,7},{7,3},{8,12},{12,8},{9,1... | collective-permute-start | bytes 12582920 | tf_op jit(solution)/shard_map/ppermute | solution.py:67
  357.3 31.2 %collective-permute-start.12 = (bf16[512,1024]{1,0:T(8,128)(2,1)}, bf16[512,1024]{1,0:T(8,128)(2,1)S(1)}, u32[]{:S(2)}, u32[]{:S(2)}) collective-permute-start(bf16[512,1024]{1,0:T(8,128)(2,1)} %get-tuple-element.84), channel_id=1, source_target_pairs={{0,1},{1,0},{2,3},{3,2},{4,5},{5,4},{6,7},{7,6},{8,9},{9,8},{10,11... | collective-permute-start | bytes 3145736 | tf_op jit(solution)/shard_map/ppermute | solution.py:59
  358.8 31.8 %collective-permute-start.13 = (bf16[512,1024]{1,0:T(8,128)(2,1)}, bf16[512,1024]{1,0:T(8,128)(2,1)S(1)}, u32[]{:S(2)}, u32[]{:S(2)}) collective-permute-start(bf16[512,1024]{1,0:T(8,128)(2,1)} %get-tuple-element.85.refs_0_), channel_id=1, source_target_pairs={{0,2},{2,0},{1,3},{3,1},{4,6},{6,4},{5,7},{7,5},{8,10},{10,8},{9,1... | collective-permute-start | bytes 3145736 | tf_op jit(solution)/shard_map/ppermute | solution.py:63
  407.0 222.4 %reduce-scatter.8.cloned.1.call-start = ((), (), s32[]{:S(2)}) async-start(), calls=%async_computation.10 | async-start | bytes 7077888 | tf_op jit(solution)/shard_map/reduce_scatter | solution.py:705
  407.2 17.0 %collective-permute-start.14 = (bf16[1024,2048]{1,0:T(8,128)(2,1)}, bf16[1024,2048]{1,0:T(8,128)(2,1)S(1)}, u32[]{:S(2)}, u32[]{:S(2)}) collective-permute-start(bf16[1024,2048]{1,0:T(8,128)(2,1)} %transposed_product.9.refs_1_), channel_id=1, source_target_pairs={{0,4},{4,0},{1,5},{5,1},{2,6},{6,2},{3,7},{7,3},{8,12},{12,8},{9,1... | collective-permute-start | bytes 12582920 | tf_op jit(solution)/shard_map/ppermute | solution.py:67
  407.9 18.8 %collective-permute-start.15 = (bf16[256,1024]{1,0:T(8,128)(2,1)S(1)}, bf16[256,1024]{1,0:T(8,128)(2,1)S(1)}, u32[]{:S(2)}, u32[]{:S(2)}) collective-permute-start(bf16[256,1024]{1,0:T(8,128)(2,1)S(1)} %copy-done.34), channel_id=1, source_target_pairs={{0,2},{2,0},{1,3},{3,1},{4,6},{6,4},{5,7},{7,5},{8,10},{10,8},{9,1... | collective-permute-start | bytes 1572872 | tf_op jit(solution)/shard_map/ppermute | solution.py:63
  408.5 18.2 %collective-permute-start.16 = (bf16[256,1024]{1,0:T(8,128)(2,1)S(1)}, bf16[256,1024]{1,0:T(8,128)(2,1)}, u32[]{:S(2)}, u32[]{:S(2)}) collective-permute-start(bf16[256,1024]{1,0:T(8,128)(2,1)S(1)} %copy-done.35), channel_id=1, source_target_pairs={{0,1},{1,0},{2,3},{3,2},{4,5},{5,4},{6,7},{7,6},{8,9},{9,8},{10,11... | collective-permute-start | bytes 1572872 | tf_op jit(solution)/shard_map/ppermute | solution.py:59
  426.7 24.3 %collective-permute-start.18 = (bf16[512,1024]{1,0:T(8,128)(2,1)S(1)}, bf16[512,1024]{1,0:T(8,128)(2,1)S(1)}, u32[]{:S(2)}, u32[]{:S(2)}) collective-permute-start(bf16[512,1024]{1,0:T(8,128)(2,1)S(1)} %fusion.6), channel_id=1, source_target_pairs={{0,2},{2,0},{1,3},{3,1},{4,6},{6,4},{5,7},{7,5},{8,10},{10,8},{9,1... | collective-permute-start | bytes 3145736 | tf_op jit(solution)/shard_map/ppermute | solution.py:63
  428.8 23.7 %collective-permute-start.17 = (bf16[512,1024]{1,0:T(8,128)(2,1)S(1)}, bf16[512,1024]{1,0:T(8,128)(2,1)S(1)}, u32[]{:S(2)}, u32[]{:S(2)}) collective-permute-start(bf16[512,1024]{1,0:T(8,128)(2,1)S(1)} %fusion.5), channel_id=1, source_target_pairs={{0,1},{1,0},{2,3},{3,2},{4,5},{5,4},{6,7},{7,6},{8,9},{9,8},{10,11... | collective-permute-start | bytes 3145736 | tf_op jit(solution)/shard_map/ppermute | solution.py:59
  469.8 22.2 %collective-permute-start.22 = (bf16[256,2048]{1,0:T(8,128)(2,1)S(1)}, bf16[256,2048]{1,0:T(8,128)(2,1)S(1)}, u32[]{:S(2)}, u32[]{:S(2)}) collective-permute-start(bf16[256,2048]{1,0:T(8,128)(2,1)S(1)} %get-tuple-element.101.own), channel_id=1, source_target_pairs={{0,2},{2,0},{1,3},{3,1},{4,6},{6,4},{5,7},{7,5},{8,10},{10,8},{9,1... | collective-permute-start | bytes 3145736 | tf_op jit(solution)/shard_map/ppermute | solution.py:63
  470.9 24.1 %collective-permute-start.21 = (bf16[256,2048]{1,0:T(8,128)(2,1)S(1)}, bf16[256,2048]{1,0:T(8,128)(2,1)S(1)}, u32[]{:S(2)}, u32[]{:S(2)}) collective-permute-start(bf16[256,2048]{1,0:T(8,128)(2,1)S(1)} %get-tuple-element.101.own), channel_id=1, source_target_pairs={{0,1},{1,0},{2,3},{3,2},{4,5},{5,4},{6,7},{7,6},{8,9},{9,8},{10,11... | collective-permute-start | bytes 3145736 | tf_op jit(solution)/shard_map/ppermute | solution.py:59
  507.2 22.2 %collective-permute-start.26 = (bf16[256,2048]{1,0:T(8,128)(2,1)S(1)}, bf16[256,2048]{1,0:T(8,128)(2,1)S(1)}, u32[]{:S(2)}, u32[]{:S(2)}) collective-permute-start(bf16[256,2048]{1,0:T(8,128)(2,1)S(1)} %fusion.4.own), channel_id=1, source_target_pairs={{0,1},{1,0},{2,3},{3,2},{4,5},{5,4},{6,7},{7,6},{8,9},{9,8},{10,11... | collective-permute-start | bytes 3145736 | tf_op jit(solution)/shard_map/ppermute | solution.py:59
  507.7 22.6 %collective-permute-start.25 = (bf16[256,2048]{1,0:T(8,128)(2,1)S(1)}, bf16[256,2048]{1,0:T(8,128)(2,1)S(1)}, u32[]{:S(2)}, u32[]{:S(2)}) collective-permute-start(bf16[256,2048]{1,0:T(8,128)(2,1)S(1)} %fusion.4.own), channel_id=1, source_target_pairs={{0,2},{2,0},{1,3},{3,1},{4,6},{6,4},{5,7},{7,5},{8,10},{10,8},{9,1... | collective-permute-start | bytes 3145736 | tf_op jit(solution)/shard_map/ppermute | solution.py:63
  555.0 25.8 %collective-permute-start.29 = (bf16[512,1024]{1,0:T(8,128)(2,1)}, bf16[512,1024]{1,0:T(8,128)(2,1)S(1)}, u32[]{:S(2)}, u32[]{:S(2)}) collective-permute-start(bf16[512,1024]{1,0:T(8,128)(2,1)} %get-tuple-element.110), channel_id=1, source_target_pairs={{0,1},{1,0},{2,3},{3,2},{4,5},{5,4},{6,7},{7,6},{8,9},{9,8},{10,11... | collective-permute-start | bytes 3145736 | tf_op jit(solution)/shard_map/ppermute | solution.py:59
  556.0 25.7 %collective-permute-start.30 = (bf16[512,1024]{1,0:T(8,128)(2,1)}, bf16[512,1024]{1,0:T(8,128)(2,1)S(1)}, u32[]{:S(2)}, u32[]{:S(2)}) collective-permute-start(bf16[512,1024]{1,0:T(8,128)(2,1)} %get-tuple-element.111), channel_id=1, source_target_pairs={{0,2},{2,0},{1,3},{3,1},{4,6},{6,4},{5,7},{7,5},{8,10},{10,8},{9,1... | collective-permute-start | bytes 3145736 | tf_op jit(solution)/shard_map/ppermute | solution.py:63
  581.8 13.6 %collective-permute-start.34 = (bf16[256,1024]{1,0:T(8,128)(2,1)S(1)}, bf16[256,1024]{1,0:T(8,128)(2,1)S(1)}, u32[]{:S(2)}, u32[]{:S(2)}) collective-permute-start(bf16[256,1024]{1,0:T(8,128)(2,1)S(1)} %add_convert_fusion), channel_id=1, source_target_pairs={{0,1},{1,0},{2,3},{3,2},{4,5},{5,4},{6,7},{7,6},{8,9},{9,8},{10,11... | collective-permute-start | bytes 1572872 | tf_op jit(solution)/shard_map/ppermute | solution.py:59
  583.1 13.1 %collective-permute-start.33 = (bf16[256,1024]{1,0:T(8,128)(2,1)S(1)}, bf16[256,1024]{1,0:T(8,128)(2,1)S(1)}, u32[]{:S(2)}, u32[]{:S(2)}) collective-permute-start(bf16[256,1024]{1,0:T(8,128)(2,1)S(1)} %add_convert_fusion.1), channel_id=1, source_target_pairs={{0,2},{2,0},{1,3},{3,1},{4,6},{6,4},{5,7},{7,5},{8,10},{10,8},{9,1... | collective-permute-start | bytes 1572872 | tf_op jit(solution)/shard_map/ppermute | solution.py:63
  600.7 23.5 %collective-permute-start.37 = (bf16[256,2048]{1,0:T(8,128)(2,1)S(1)}, bf16[256,2048]{1,0:T(8,128)(2,1)S(1)}, u32[]{:S(2)}, u32[]{:S(2)}) collective-permute-start(bf16[256,2048]{1,0:T(8,128)(2,1)S(1)} %get-tuple-element.128.own), channel_id=1, source_target_pairs={{0,1},{1,0},{2,3},{3,2},{4,5},{5,4},{6,7},{7,6},{8,9},{9,8},{10,11... | collective-permute-start | bytes 3145736 | tf_op jit(solution)/shard_map/ppermute | solution.py:59
  601.9 24.7 %collective-permute-start.35 = (bf16[256,2048]{1,0:T(8,128)(2,1)S(1)}, bf16[256,2048]{1,0:T(8,128)(2,1)S(1)}, u32[]{:S(2)}, u32[]{:S(2)}) collective-permute-start(bf16[256,2048]{1,0:T(8,128)(2,1)S(1)} %get-tuple-element.128.own), channel_id=1, source_target_pairs={{0,2},{2,0},{1,3},{3,1},{4,6},{6,4},{5,7},{7,5},{8,10},{10,8},{9,1... | collective-permute-start | bytes 3145736 | tf_op jit(solution)/shard_map/ppermute | solution.py:63
  (72 other events, 802.5 us)
Sparse Core Ops, SparseCore 0:
  21.8 64.8 all-gather.3
  88.8 148.3 all-gather.5
  239.4 78.9 all-gather.7
  320.5 75.2 reduce-scatter.3
  407.1 141.7 reduce-scatter.5
  551.1 70.5 reduce-scatter.7

commit v5 on v4

--- a/solution.py
+++ b/solution.py
@@ -956,31 +956,32 @@
     layer_near = exchange_near(layer_block)
     d_context = column_product(g1_low, w_attn, o_first, q_cols, bf16)
     d_qkv = attention_backward(relative_place, lengths, qkv, tables, d_context)
+    d_qkv, layer_near = tie(d_qkv, layer_near)
     layer_middle = exchange_middle(layer_near)
-    attn_grads = attention_products(g1_low, context, h_attn, d_qkv, *layer_middle)
-    attn_out = reduce_dp(attn_grads)
     layer_far = exchange_far(layer_middle)
-    h1_pieces = scatter_product(d_qkv, w_attn, 0, slots, earlier=(attn_grads,))
-    h1_pieces, layer_far = tie(h1_pieces, layer_far)
+    h1_pieces = list(scatter_product(d_qkv, w_attn, 0, slots))
+    attn_grads = attention_products(g1_low, context, h_attn, d_qkv, h1_pieces[0])
+    h1_pieces[-1], layer_far = tie(h1_pieces[-1], layer_far)
     layer_out = join_rows((layer_block, *layer_near, *layer_far), False)
     h1_near = scatter_near(h1_pieces)
-    (down_out,) = from_core(down_out, 1, True)
-    gate_out, up_out = from_core(gu_out, 2, earlier=(down_out,))
-    h1_near, gate_out, up_out, layer_out = tie(h1_near, gate_out, up_out, layer_out)
+    h1_near, layer_out, attn_grads = tie(h1_near, layer_out, attn_grads)
+    attn_out = reduce_dp(attn_grads)
     h1_far = scatter_far(scatter_middle(h1_pieces, h1_near))
     _, grad_block = rows_backward(h1_pieces, h1_near, h1_far, None, x_rel, g1, g_attn)
     grad_pieces = list(exchange_rows(grad_block))
-    grad_pieces[0], attn_out = tie(grad_pieces[0], attn_out)
+    grad_pieces[0], gu_out, down_out = tie(grad_pieces[0], gu_out, down_out)
+    (down_out,) = from_core(down_out, 1, True)
+    gate_out, up_out = from_core(gu_out, 2, earlier=(down_out,))
 
     rows_here = gain_attn.shape[0]
 
     ffn_sums = sum(
         jnp.sum(w.astype(f32) * g, axis=1) for w, g in [(gate_weight, gate_out), (up_weight, up_out)]
     ) / gain_ffn.astype(f32)
-    out_out, q_out, send = attention_end(attn_out, query_weight, kv_block, gain_attn, ffn_sums)
     if square():
         joined = join_near(grad_pieces[:3], f32)
-        *far_pieces, send, joined = tie(*grad_pieces[3:], send, joined)
+        *far_pieces, attn_out, joined, ffn_sums = tie(*grad_pieces[3:], attn_out, joined, ffn_sums)
+    out_out, q_out, send = attention_end(attn_out, query_weight, kv_block, gain_attn, ffn_sums)
     key_grad, value_grad, gain_attn_grad, gain_ffn_grad = collect_heads(send, KEY_VALUE_HEADS)
     if square():
         grad_input = join_far(far_pieces, joined)

time: 664 us -> 662 us (level)
  waiting for transfers between devices: 282 us -> 260 us
  local copies, waits for them, and re-layouts: 39.9 us -> 54.2 us
    ppermute x16, waiting for transfers between devices: 101 us -> 78.7 us  [send_x(): return lax.ppermute(v, 'mp', OVER_X)]
    unnamed x120 -> x144, local copies, waits for them, and re-layouts: 24.8 us -> 44.1 us
  transfers between devices with their start and end apart: 47 -> 47, of which waited for: 28 -> 25; matrix products, arithmetic and copies ran while one was open for 9% -> 9% of each run, Pallas kernels for 33% -> 33%
where the time goes in v5:
time: 662 us; the launch traced here: 656 us
  waiting for transfers between devices  260 us (39%)
  Pallas kernels  218 us (33%)
  local copies, waits for them, and re-layouts  54.2 us (8%)
  starting transfers between devices  47.4 us (7%)
  other arithmetic  34.1 us (5%)
  between operations  15.8 us (2%)
  matrix products  14 us (2%)
  blocking collectives  12.5 us (2%)
    ppermute x16, waiting for transfers between devices, send_x(): return lax.ppermute(v, 'mp', OVER_X)  78.7 us
    ppermute x16, waiting for transfers between devices, send_y(): return lax.ppermute(v, 'mp', OVER_Y)  77.4 us
    all_gather x2, waiting for transfers between devices, gather_z(): return lax.all_gather(block, 'z', axis=0, tiled=True)  71.3 us
    pallas_call x6, Pallas kernels, transposed_product(): pl.pallas_call(functools.partial(transposed_product_kernel, groups, add i...  64.7 us
    unnamed x144, local copies, waits for them, and re-layouts  44.1 us
    pallas_call x2, Pallas kernels, rows_product(): pl.pallas_call(rows_product_kernel, name='rows_product', grid=(steps,), i...  28.6 us
    pallas_call x1, Pallas kernels, ffn_forward(): pl.pallas_call(ffn_forward_kernel, name='ffn_forward', grid=(2, ff // tn)...  26.2 us
    all_gather x1, waiting for transfers between devices, gather_dp(): return lax.all_gather(block, DP, axis=0, tiled=True)  22.5 us
  transfers between devices with their start and end apart: 47, of which 25 were waited for; matrix products, arithmetic and copies ran while one was open for 9% of the time, Pallas kernels for 33%

profile of v5, /device:TPU:0, one launch (start us, length us, event | category | flops | bytes accessed | tf_op | source)
XLA Modules:
  0.0 656.4 jit_solution(1682420416825778338)
XLA Ops:
  9.0 5.2 all-to-all-start
  38.8 5.6 prepare.1
  44.4 12.5 %all_gather.12 = bf16[2,2048]{1,0:T(2,128)(2,1)S(1)} all-gather(bf16[2,256]{1,0:T(2,128)(2,1)S(1)} %pad_maximum_fusion.4), channel_id=1, replica_groups=mesh['z'=4,'core'=2,'mp'=4] {'z','core'}, dimensions={1}, use_global_device_ids=true | all-gather | bytes 9216 | tf_op jit(solution)/shard_map/all_gather | solution.py:909
  64.2 22.5 %all-gather.4.cloned.1.call-done.right_ref = bf16[2048,1536]{1,0:T(8,128)(2,1)} async-done(((bf16[256,1536]{1,0:T(8,128)(2,1)}), bf16[2048,1536]{1,0:T(8,128)(2,1)}) %all-gather.4.cloned.1.call-update) | async-done | bytes 6291472 | tf_op jit(solution)/shard_map/all_gather | solution.py:701
  86.7 9.0 %column_product.2.q_ref.k_ref.v_ref = f32[1024,1024]{1,0:T(8,128)} custom-call(bf16[1024,2048]{1,0:T(8,128)(2,1)} %fusion.2.left_ref.h_ref, bf16[2048,1536]{1,0:T(8,128)(2,1)} %all-gather.4.cloned.1.call-done.right_ref), custom_call_target="tpu_custom_call" | custom-call | flops 4294967296 | bytes 12582912 | tf_op jit(solution)/shard_map/column_product/pallas_call | solution.py:100
  95.8 8.2 %attention_forward.1.left_ref.context_ref = bf16[1024,512]{1,0:T(8,128)(2,1)} custom-call(s32[4]{0:T(128)} %get-tuple-element.182.order_ref, s32[1]{0:T(128)S(6)} %copy.65.len_ref, f32[1024,1024]{1,0:T(8,128)} %column_product.2.q_ref.k_ref.v_ref, f32[1024,1024]{1,0:T(8,128)} %column_product.2.q_ref.k_ref.v_ref, ...), custom_call_target="tpu_custom_call" | custom-call | flops 1610612736 | bytes 8388608 | tf_op jit(solution)/shard_map/attention_forward/pallas_call | solution.py:536
  103.9 7.1 %transposed_product.6 = (f32[256,1024]{1,0:T(8,128)}, bf16[256,1024]{1,0:T(8,128)(2,1)}, bf16[512,1024]{1,0:T(8,128)(2,1)}, f32[256,1024]{1,0:T(8,128)}, bf16[25...) custom-call(bf16[1024,512]{1,0:T(8,128)(2,1)} %attention_forward.1.left_ref.context_ref, ...), custom_call_target="tpu_custom_call" | custom-call | flops 2147483648 | bytes 7340032 | tf_op jit(solution)/shard_map/transposed_product/pallas_call | solution.py:151
  114.1 22.5 %collective-permute-done = bf16[512,1024]{1,0:T(8,128)(2,1)S(1)} collective-permute-done((bf16[512,1024]{1,0:T(8,128)(2,1)}, bf16[512,1024]{1,0:T(8,128)(2,1)S(1)}, u32[]{:S(2)}, u32[]{:S(2)}) %collective-permute-start) | collective-permute-done | bytes 1048608 | tf_op jit(solution)/shard_map/ppermute | solution.py:59
  142.3 9.1 %collective-permute-done.1 = bf16[256,1024]{1,0:T(8,128)(2,1)S(1)} collective-permute-done((bf16[256,1024]{1,0:T(8,128)(2,1)S(1)}, bf16[256,1024]{1,0:T(8,128)(2,1)S(1)}, u32[]{:S(2)}, u32[]{:S(2)}) %collective-permute-start.1) | collective-permute-done | bytes 524320 | tf_op jit(solution)/shard_map/ppermute | solution.py:63
  158.1 21.4 %collective-permute-done.5.over_y = bf16[256,2048]{1,0:T(8,128)(2,1)S(1)} collective-permute-done((bf16[256,2048]{1,0:T(8,128)(2,1)S(1)}, bf16[256,2048]{1,0:T(8,128)(2,1)S(1)}, u32[]{:S(2)}, u32[]{:S(2)}) %collective-permute-start.5) | collective-permute-done | bytes 1048608 | tf_op jit(solution)/shard_map/ppermute | solution.py:63
  182.1 9.0 %collective-permute-done.6.diag_a = bf16[256,1024]{1,0:T(8,128)(2,1)S(1)} collective-permute-done((bf16[256,1024]{1,0:T(8,128)(2,1)S(1)}, bf16[256,1024]{1,0:T(8,128)(2,1)S(1)}, u32[]{:S(2)}, u32[]{:S(2)}) %collective-permute-start.6) | collective-permute-done | bytes 524320 | tf_op jit(solution)/shard_map/ppermute | solution.py:59
  206.7 30.5 %all-gather.6.cloned.1.call-done.g_ref.u_ref.right_ref = bf16[2048,2048]{1,0:T(8,128)(2,1)} async-done(((bf16[512,2048]{1,0:T(8,128)(2,1)}), bf16[2048,2048]{1,0:T(8,128)(2,1)}) %all-gather.6.cloned.1.call-update) | async-done | bytes 8388624 | tf_op jit(solution)/shard_map/all_gather | solution.py:709
  237.2 26.2 %ffn_forward.1 = (bf16[2048,1024]{1,0:T(8,128)(2,1)}, bf16[2,2048,1024]{2,1,0:T(8,128)(2,1)}) custom-call(bf16[1024,2048]{1,0:T(8,128)(2,1)} %assemble.3.mine_ref, bf16[1024,2048]{1,0:T(8,128)(2,1)} %collective-permute-done.8.away_ref, bf16[2048,2048]{1,0:T(8,128)(2,1)} %all-gather.6.cloned.1.call-done.g_ref.u_ref.right_ref, ...), custom_call_target="tpu_custom_call" | custom-call | flops 17179869184 | bytes 29360128 | tf_op jit(solution)/shard_map/ffn_forward/pallas_call | solution.py:780
  263.4 14.0 %convolution_convert_fusion.refs_0_ = bf16[2048,1024]{1,0:T(8,128)(2,1)} fusion(bf16[2048,2048]{1,0:T(8,128)(2,1)} %constant_dynamic-update-slice_fusion.grad_ref, bf16[2048,1024]{1,0:T(8,128)(2,1)} %get-tuple-element.79.left_ref), kind=kOutput, calls=%fused_computation.5 | convolution fusion | flops 8592031744 | bytes 16777216 | tf_op jit(solution)/shard_map/dot_general | solution.py:49
  277.6 40.8 %all-gather.8.cloned.1.call-done.right_ref.d_ref = bf16[2048,1024]{1,0:T(8,128)(2,1)} async-done(((bf16[512,1024]{1,0:T(8,128)(2,1)}), bf16[2048,1024]{1,0:T(8,128)(2,1)}) %all-gather.8.cloned.1.call-update) | async-done | bytes 4194320 | tf_op jit(solution)/shard_map/all_gather | solution.py:709
  318.4 8.8 %transposed_product.7.earlier_ref = bf16[1024,2048]{1,0:T(8,128)(2,1)} custom-call(bf16[2048,1024]{1,0:T(8,128)(2,1)} %get-tuple-element.79.left_ref, bf16[2048,1024]{1,0:T(8,128)(2,1)} %all-gather.8.cloned.1.call-done.right_ref.d_ref, bf16[2048,1024]{1,0:T(8,128)(2,1)} %convolution_convert_fusion.refs_0_), custom_call_target="tpu_custom_call" | custom-call | flops 4294967296 | bytes 10485760 | tf_op jit(solution)/shard_map/transposed_product/pallas_call | solution.py:151
  327.2 18.0 %ffn_backward.1.refs_1_.right_mine_ref.right_away_ref.left_ref = bf16[2,2048,1024]{2,1,0:T(8,128)(2,1)} custom-call(bf16[2048,2048]{1,0:T(8,128)(2,1)} %constant_dynamic-update-slice_fusion.grad_ref, bf16[2048,1024]{1,0:T(8,128)(2,1)} %all-gather.8.cloned.1.call-done.right_ref.d_ref, bf16[2,2048,1024]{2,1,0:T(8,128)(2,1)} %get-tuple-element.81.factor_ref, ...), custom_call_target="tpu_custom_call" | custom-call | flops 8589934592 | bytes 29360128 | tf_op jit(solution)/shard_map/ffn_backward/pallas_call | solution.py:856
  347.2 10.1 %transposed_product.8 = (f32[256,1024]{1,0:T(8,128)}, bf16[256,1024]{1,0:T(8,128)(2,1)}, bf16[512,1024]{1,0:T(8,128)(2,1)}, f32[256,1024]{1,0:T(8,128)}, bf16[25...) custom-call(bf16[2048,1024]{1,0:T(8,128)(2,1)} %get-tuple-element.79.left_ref, ...), custom_call_target="tpu_custom_call" | custom-call | flops 4294967296 | bytes 10485760 | tf_op jit(solution)/shard_map/transposed_product/pallas_call | solution.py:151
  360.2 14.3 %rows_product.2.refs_0_ = bf16[2048,2048]{1,0:T(8,128)(2,1)} custom-call(bf16[1024,2048]{1,0:T(8,128)(2,1)} %assemble.3.mine_ref, bf16[1024,2048]{1,0:T(8,128)(2,1)} %collective-permute-done.8.away_ref, bf16[2,2048,1024]{2,1,0:T(8,128)(2,1)} %ffn_backward.1.refs_1_.right_mine_ref.right_away_ref.left_ref, ...), custom_call_target="tpu_custom_call" | custom-call | flops 8589934592 | bytes 16777216 | tf_op jit(solution)/shard_map/rows_product/pallas_call | solution.py:823
  374.5 13.9 %transposed_product.9.refs_1_ = bf16[1024,2048]{1,0:T(8,128)(2,1)} custom-call(bf16[2,2048,1024]{2,1,0:T(8,128)(2,1)} %ffn_backward.1.refs_1_.right_mine_ref.right_away_ref.left_ref, bf16[2048,2048]{1,0:T(8,128)(2,1)} %all-gather.6.cloned.1.call-done.g_ref.u_ref.right_ref, bf16[2048,2048]{1,0:T(8,128)(2,1)} %rows_product.2.refs_0_), custom_call_target="tpu_custom_call" | custom-call | flops 8589934592 | bytes 16777216 | tf_op jit(solution)/shard_map/transposed_product/pallas_call | solution.py:151
  392.4 14.4 %rows_product.3.refs_0_ = bf16[2048,2048]{1,0:T(8,128)(2,1)} custom-call(bf16[1024,2048]{1,0:T(8,128)(2,1)} %assemble.3.mine_ref, bf16[1024,2048]{1,0:T(8,128)(2,1)} %collective-permute-done.8.away_ref, bf16[2,2048,1024]{2,1,0:T(8,128)(2,1)} %ffn_backward.1.refs_1_.right_mine_ref.right_away_ref.left_ref, ...), custom_call_target="tpu_custom_call", output_to_operand_aliasing={{}: (4, {})} | custom-call | flops 8589934592 | bytes 16777216 | tf_op jit(solution)/shard_map/rows_product/pallas_call | solution.py:823
  408.9 15.2 %transposed_product.10 = (f32[256,1024]{1,0:T(8,128)}, bf16[256,1024]{1,0:T(8,128)(2,1)}, bf16[512,1024]{1,0:T(8,128)(2,1)}, f32[256,1024]{1,0:T(8,128)}, bf16[2...) custom-call(bf16[2,2048,1024]{2,1,0:T(8,128)(2,1)} %ffn_backward.1.refs_1_.right_mine_ref.right_away_ref.left_ref, ...), custom_call_target="tpu_custom_call" | custom-call | flops 8589934592 | bytes 16777216 | tf_op jit(solution)/shard_map/transposed_product/pallas_call | solution.py:151
  430.2 20.7 %collective-permute-done.18.refs_3_ = bf16[512,1024]{1,0:T(8,128)(2,1)S(1)} collective-permute-done((bf16[512,1024]{1,0:T(8,128)(2,1)S(1)}, bf16[512,1024]{1,0:T(8,128)(2,1)S(1)}, u32[]{:S(2)}, u32[]{:S(2)}) %collective-permute-start.18) | collective-permute-done | bytes 1048608 | tf_op jit(solution)/shard_map/ppermute | solution.py:63
  455.4 9.3 %collective-permute-done.20.refs_5_ = bf16[256,1024]{1,0:T(8,128)(2,1)S(1)} collective-permute-done((bf16[256,1024]{1,0:T(8,128)(2,1)S(1)}, bf16[256,1024]{1,0:T(8,128)(2,1)S(1)}, u32[]{:S(2)}, u32[]{:S(2)}) %collective-permute-start.20) | collective-permute-done | bytes 524320 | tf_op jit(solution)/shard_map/ppermute | solution.py:59
  472.9 19.0 %collective-permute-done.22.over_y = bf16[256,2048]{1,0:T(8,128)(2,1)S(1)} collective-permute-done((bf16[256,2048]{1,0:T(8,128)(2,1)S(1)}, bf16[256,2048]{1,0:T(8,128)(2,1)S(1)}, u32[]{:S(2)}, u32[]{:S(2)}) %collective-permute-start.22) | collective-permute-done | bytes 1048608 | tf_op jit(solution)/shard_map/ppermute | solution.py:63
  495.2 8.5 %collective-permute-done.23.diag_a = bf16[256,1024]{1,0:T(8,128)(2,1)S(1)} collective-permute-done((bf16[256,1024]{1,0:T(8,128)(2,1)S(1)}, bf16[256,1024]{1,0:T(8,128)(2,1)S(1)}, u32[]{:S(2)}, u32[]{:S(2)}) %collective-permute-start.23) | collective-permute-done | bytes 524320 | tf_op jit(solution)/shard_map/ppermute | solution.py:59
  508.0 5.8 column_product.3.g_ref
  513.9 12.8 %attention_backward.1.left_ref.d_qkv_ref = bf16[1024,1024]{1,0:T(8,128)(2,1)} custom-call(s32[4]{0:T(128)} %get-tuple-element.182.order_ref, s32[1]{0:T(128)S(6)} %copy.65.len_ref, f32[1024,1024]{1,0:T(8,128)} %column_product.2.q_ref.k_ref.v_ref, f32[1024,1024]{1,0:T(8,128)} %column_product.2.q_ref.k_ref.v_ref, ...), custom_call_target="tpu_custom_call" | custom-call | flops 3758096384 | bytes 8388608 | tf_op jit(solution)/shard_map/attention_backward/pallas_call | solution.py:559
  532.6 9.7 %transposed_product.11 = (f32[256,1024]{1,0:T(8,128)}, bf16[256,1024]{1,0:T(8,128)(2,1)}, bf16[512,1024]{1,0:T(8,128)(2,1)}, f32[256,1024]{1,0:T(8,128)}, bf16[2...) custom-call(bf16[1024,1024]{1,0:T(8,128)(2,1)} %attention_backward.1.left_ref.d_qkv_ref, ...), custom_call_target="tpu_custom_call" | custom-call | flops 4294967296 | bytes 10485760 | tf_op jit(solution)/shard_map/transposed_product/pallas_call | solution.py:151
  545.6 11.4 %attention_products.1 = bf16[2048,1536]{1,0:T(8,128)(2,1)} custom-call(bf16[1024,2048]{1,0:T(8,128)(2,1)} %copy-done.2, bf16[1024,512]{1,0:T(8,128)(2,1)} %attention_forward.1.left_ref.context_ref, bf16[1024,2048]{1,0:T(8,128)(2,1)} %fusion.2.left_ref.h_ref, bf16[1024,1024]{1,0:T(8,128)(2,1)} %attention_backward.1.left_ref.d_qkv_ref, ...), custom_call_target="tpu_custom_call" | custom-call | flops 6442450944 | bytes 17825792 | tf_op jit(solution)/shard_map/attention_products/pallas_call | solution.py:592
  570.0 6.0 collective-permute-done.32.refs_5_
  594.3 17.1 %collective-permute-done.35.over_x = bf16[256,2048]{1,0:T(8,128)(2,1)S(1)} collective-permute-done((bf16[256,2048]{1,0:T(8,128)(2,1)}, bf16[256,2048]{1,0:T(8,128)(2,1)S(1)}, u32[]{:S(2)}, u32[]{:S(2)}) %collective-permute-start.35) | collective-permute-done | bytes 1048608 | tf_op jit(solution)/shard_map/ppermute | solution.py:59
  (304 shorter events, 182.3 us)
Async XLA Ops:
  14.1 72.6 %all-gather.4.cloned.1.call-start = ((), (), s32[]{:S(2)}) async-start(), calls=%async_computation.5 | async-start | bytes 7077888 | tf_op jit(solution)/shard_map/all_gather | solution.py:701
  21.7 215.5 %all-gather.6.cloned.1.call-start = ((), (), s32[]{:S(2)}) async-start(), calls=%async_computation.6 | async-start | bytes 10485760 | tf_op jit(solution)/shard_map/all_gather | solution.py:709
  35.4 283.0 %all-gather.8.cloned.1.call-start = ((), (), s32[]{:S(2)}) async-start(), calls=%async_computation.7 | async-start | bytes 5242880 | tf_op jit(solution)/shard_map/all_gather | solution.py:709
  111.0 25.6 %collective-permute-start = (bf16[512,1024]{1,0:T(8,128)(2,1)}, bf16[512,1024]{1,0:T(8,128)(2,1)S(1)}, u32[]{:S(2)}, u32[]{:S(2)}) collective-permute-start(bf16[512,1024]{1,0:T(8,128)(2,1)} %get-tuple-element.74), channel_id=1, source_target_pairs={{0,1},{1,0},{2,3},{3,2},{4,5},{5,4},{6,7},{7,6},{8,9},{9,8},{10,11... | collective-permute-start | bytes 3145736 | tf_op jit(solution)/shard_map/ppermute | solution.py:59
  112.6 26.9 %collective-permute-start.2 = (bf16[512,1024]{1,0:T(8,128)(2,1)}, bf16[512,1024]{1,0:T(8,128)(2,1)S(1)}, u32[]{:S(2)}, u32[]{:S(2)}) collective-permute-start(bf16[512,1024]{1,0:T(8,128)(2,1)} %get-tuple-element.77), channel_id=1, source_target_pairs={{0,2},{2,0},{1,3},{3,1},{4,6},{6,4},{5,7},{7,5},{8,10},{10,8},{9,1... | collective-permute-start | bytes 3145736 | tf_op jit(solution)/shard_map/ppermute | solution.py:63
  156.0 23.5 %collective-permute-start.5 = (bf16[256,2048]{1,0:T(8,128)(2,1)S(1)}, bf16[256,2048]{1,0:T(8,128)(2,1)S(1)}, u32[]{:S(2)}, u32[]{:S(2)}) collective-permute-start(bf16[256,2048]{1,0:T(8,128)(2,1)S(1)} %multiply_convert_fusion.own), channel_id=1, source_target_pairs={{0,2},{2,0},{1,3},{3,1},{4,6},{6,4},{5,7},{7,5},{8,10},{10,8},{9,1... | collective-permute-start | bytes 3145736 | tf_op jit(solution)/shard_map/ppermute | solution.py:63
  156.6 24.5 %collective-permute-start.4 = (bf16[256,2048]{1,0:T(8,128)(2,1)S(1)}, bf16[256,2048]{1,0:T(8,128)(2,1)S(1)}, u32[]{:S(2)}, u32[]{:S(2)}) collective-permute-start(bf16[256,2048]{1,0:T(8,128)(2,1)S(1)} %multiply_convert_fusion.own), channel_id=1, source_target_pairs={{0,1},{1,0},{2,3},{3,2},{4,5},{5,4},{6,7},{7,6},{8,9},{9,8},{10,11... | collective-permute-start | bytes 3145736 | tf_op jit(solution)/shard_map/ppermute | solution.py:59
  182.1 19.8 %collective-permute-start.10 = (bf16[1024,2048]{1,0:T(8,128)(2,1)}, bf16[1024,2048]{1,0:T(8,128)(2,1)}, u32[]{:S(2)}, u32[]{:S(2)}) collective-permute-start(bf16[1024,2048]{1,0:T(8,128)(2,1)} %get-tuple-element.80.refs_8_), channel_id=1, source_target_pairs={{0,4},{4,0},{1,5},{5,1},{2,6},{6,2},{3,7},{7,3},{8,12},{12,8},{9,1... | collective-permute-start | bytes 12582920 | tf_op jit(solution)/shard_map/ppermute | solution.py:67
  195.5 41.7 %collective-permute-start.8 = (bf16[1024,2048]{1,0:T(8,128)(2,1)}, bf16[1024,2048]{1,0:T(8,128)(2,1)}, u32[]{:S(2)}, u32[]{:S(2)}) collective-permute-start(bf16[1024,2048]{1,0:T(8,128)(2,1)} %assemble.3.mine_ref), channel_id=1, source_target_pairs={{0,4},{4,0},{1,5},{5,1},{2,6},{6,2},{3,7},{7,3},{8,12},{12,8},{9,1... | collective-permute-start | bytes 12582920 | tf_op jit(solution)/shard_map/ppermute | solution.py:67
  196.5 210.3 %reduce-scatter.4.cloned.1.call-start = ((), (), s32[]{:S(2)}) async-start(), calls=%async_computation.8 | async-start | bytes 5242880 | tf_op jit(solution)/shard_map/reduce_scatter | solution.py:713
  277.4 314.7 %reduce-scatter.8.cloned.1.call-start = ((), (), s32[]{:S(2)}) async-start(), calls=%async_computation.10 | async-start | bytes 10485760 | tf_op jit(solution)/shard_map/reduce_scatter | solution.py:713
  327.2 18.0 %collective-permute-start.11 = (bf16[1024,2048]{1,0:T(8,128)(2,1)}, bf16[1024,2048]{1,0:T(8,128)(2,1)S(1)}, u32[]{:S(2)}, u32[]{:S(2)}) collective-permute-start(bf16[1024,2048]{1,0:T(8,128)(2,1)} %transposed_product.7.earlier_ref), channel_id=1, source_target_pairs={{0,4},{4,0},{1,5},{5,1},{2,6},{6,2},{3,7},{7,3},{8,12},{12,8},{9,1... | collective-permute-start | bytes 12582920 | tf_op jit(solution)/shard_map/ppermute | solution.py:67
  357.2 31.2 %collective-permute-start.12 = (bf16[512,1024]{1,0:T(8,128)(2,1)}, bf16[512,1024]{1,0:T(8,128)(2,1)S(1)}, u32[]{:S(2)}, u32[]{:S(2)}) collective-permute-start(bf16[512,1024]{1,0:T(8,128)(2,1)} %get-tuple-element.83), channel_id=1, source_target_pairs={{0,1},{1,0},{2,3},{3,2},{4,5},{5,4},{6,7},{7,6},{8,9},{9,8},{10,11... | collective-permute-start | bytes 3145736 | tf_op jit(solution)/shard_map/ppermute | solution.py:59
  358.7 31.7 %collective-permute-start.13 = (bf16[512,1024]{1,0:T(8,128)(2,1)}, bf16[512,1024]{1,0:T(8,128)(2,1)S(1)}, u32[]{:S(2)}, u32[]{:S(2)}) collective-permute-start(bf16[512,1024]{1,0:T(8,128)(2,1)} %get-tuple-element.84.refs_0_), channel_id=1, source_target_pairs={{0,2},{2,0},{1,3},{3,1},{4,6},{6,4},{5,7},{7,5},{8,10},{10,8},{9,1... | collective-permute-start | bytes 3145736 | tf_op jit(solution)/shard_map/ppermute | solution.py:63
  406.9 226.3 %reduce-scatter.6.cloned.1.call-start = ((), (), s32[]{:S(2)}) async-start(), calls=%async_computation.9 | async-start | bytes 7077888 | tf_op jit(solution)/shard_map/reduce_scatter | solution.py:705
  407.1 17.1 %collective-permute-start.14 = (bf16[1024,2048]{1,0:T(8,128)(2,1)}, bf16[1024,2048]{1,0:T(8,128)(2,1)S(1)}, u32[]{:S(2)}, u32[]{:S(2)}) collective-permute-start(bf16[1024,2048]{1,0:T(8,128)(2,1)} %transposed_product.9.refs_1_), channel_id=1, source_target_pairs={{0,4},{4,0},{1,5},{5,1},{2,6},{6,2},{3,7},{7,3},{8,12},{12,8},{9,1... | collective-permute-start | bytes 12582920 | tf_op jit(solution)/shard_map/ppermute | solution.py:67
  407.8 18.8 %collective-permute-start.15 = (bf16[256,1024]{1,0:T(8,128)(2,1)S(1)}, bf16[256,1024]{1,0:T(8,128)(2,1)S(1)}, u32[]{:S(2)}, u32[]{:S(2)}) collective-permute-start(bf16[256,1024]{1,0:T(8,128)(2,1)S(1)} %copy-done.46), channel_id=1, source_target_pairs={{0,2},{2,0},{1,3},{3,1},{4,6},{6,4},{5,7},{7,5},{8,10},{10,8},{9,1... | collective-permute-start | bytes 1572872 | tf_op jit(solution)/shard_map/ppermute | solution.py:63
  408.4 18.2 %collective-permute-start.16 = (bf16[256,1024]{1,0:T(8,128)(2,1)S(1)}, bf16[256,1024]{1,0:T(8,128)(2,1)}, u32[]{:S(2)}, u32[]{:S(2)}) collective-permute-start(bf16[256,1024]{1,0:T(8,128)(2,1)S(1)} %copy-done.47), channel_id=1, source_target_pairs={{0,1},{1,0},{2,3},{3,2},{4,5},{5,4},{6,7},{7,6},{8,9},{9,8},{10,11... | collective-permute-start | bytes 1572872 | tf_op jit(solution)/shard_map/ppermute | solution.py:59
  426.6 24.3 %collective-permute-start.18 = (bf16[512,1024]{1,0:T(8,128)(2,1)S(1)}, bf16[512,1024]{1,0:T(8,128)(2,1)S(1)}, u32[]{:S(2)}, u32[]{:S(2)}) collective-permute-start(bf16[512,1024]{1,0:T(8,128)(2,1)S(1)} %fusion.6), channel_id=1, source_target_pairs={{0,2},{2,0},{1,3},{3,1},{4,6},{6,4},{5,7},{7,5},{8,10},{10,8},{9,1... | collective-permute-start | bytes 3145736 | tf_op jit(solution)/shard_map/ppermute | solution.py:63
  428.7 23.7 %collective-permute-start.17 = (bf16[512,1024]{1,0:T(8,128)(2,1)S(1)}, bf16[512,1024]{1,0:T(8,128)(2,1)S(1)}, u32[]{:S(2)}, u32[]{:S(2)}) collective-permute-start(bf16[512,1024]{1,0:T(8,128)(2,1)S(1)} %fusion.5), channel_id=1, source_target_pairs={{0,1},{1,0},{2,3},{3,2},{4,5},{5,4},{6,7},{7,6},{8,9},{9,8},{10,11... | collective-permute-start | bytes 3145736 | tf_op jit(solution)/shard_map/ppermute | solution.py:59
  469.6 22.2 %collective-permute-start.22 = (bf16[256,2048]{1,0:T(8,128)(2,1)S(1)}, bf16[256,2048]{1,0:T(8,128)(2,1)S(1)}, u32[]{:S(2)}, u32[]{:S(2)}) collective-permute-start(bf16[256,2048]{1,0:T(8,128)(2,1)S(1)} %get-tuple-element.100.own), channel_id=1, source_target_pairs={{0,2},{2,0},{1,3},{3,1},{4,6},{6,4},{5,7},{7,5},{8,10},{10,8},{9,1... | collective-permute-start | bytes 3145736 | tf_op jit(solution)/shard_map/ppermute | solution.py:63
  470.7 24.0 %collective-permute-start.21 = (bf16[256,2048]{1,0:T(8,128)(2,1)S(1)}, bf16[256,2048]{1,0:T(8,128)(2,1)S(1)}, u32[]{:S(2)}, u32[]{:S(2)}) collective-permute-start(bf16[256,2048]{1,0:T(8,128)(2,1)S(1)} %get-tuple-element.100.own), channel_id=1, source_target_pairs={{0,1},{1,0},{2,3},{3,2},{4,5},{5,4},{6,7},{7,6},{8,9},{9,8},{10,11... | collective-permute-start | bytes 3145736 | tf_op jit(solution)/shard_map/ppermute | solution.py:59
  507.0 23.1 %collective-permute-start.26 = (bf16[256,2048]{1,0:T(8,128)(2,1)S(1)}, bf16[256,2048]{1,0:T(8,128)(2,1)S(1)}, u32[]{:S(2)}, u32[]{:S(2)}) collective-permute-start(bf16[256,2048]{1,0:T(8,128)(2,1)S(1)} %fusion.4.own), channel_id=1, source_target_pairs={{0,2},{2,0},{1,3},{3,1},{4,6},{6,4},{5,7},{7,5},{8,10},{10,8},{9,1... | collective-permute-start | bytes 3145736 | tf_op jit(solution)/shard_map/ppermute | solution.py:63
  507.4 22.6 %collective-permute-start.25 = (bf16[256,2048]{1,0:T(8,128)(2,1)S(1)}, bf16[256,2048]{1,0:T(8,128)(2,1)S(1)}, u32[]{:S(2)}, u32[]{:S(2)}) collective-permute-start(bf16[256,2048]{1,0:T(8,128)(2,1)S(1)} %fusion.4.own), channel_id=1, source_target_pairs={{0,1},{1,0},{2,3},{3,2},{4,5},{5,4},{6,7},{7,6},{8,9},{9,8},{10,11... | collective-permute-start | bytes 3145736 | tf_op jit(solution)/shard_map/ppermute | solution.py:59
  542.3 22.2 %collective-permute-start.27 = (bf16[512,1024]{1,0:T(8,128)(2,1)}, bf16[512,1024]{1,0:T(8,128)(2,1)S(1)}, u32[]{:S(2)}, u32[]{:S(2)}) collective-permute-start(bf16[512,1024]{1,0:T(8,128)(2,1)} %get-tuple-element.104), channel_id=1, source_target_pairs={{0,1},{1,0},{2,3},{3,2},{4,5},{5,4},{6,7},{7,6},{8,9},{9,8},{10,11... | collective-permute-start | bytes 3145736 | tf_op jit(solution)/shard_map/ppermute | solution.py:59
  545.3 19.2 %collective-permute-start.30 = (bf16[512,1024]{1,0:T(8,128)(2,1)}, bf16[512,1024]{1,0:T(8,128)(2,1)S(1)}, u32[]{:S(2)}, u32[]{:S(2)}) collective-permute-start(bf16[512,1024]{1,0:T(8,128)(2,1)} %get-tuple-element.108), channel_id=1, source_target_pairs={{0,2},{2,0},{1,3},{3,1},{4,6},{6,4},{5,7},{7,5},{8,10},{10,8},{9,1... | collective-permute-start | bytes 3145736 | tf_op jit(solution)/shard_map/ppermute | solution.py:63
  589.1 22.3 %collective-permute-start.35 = (bf16[256,2048]{1,0:T(8,128)(2,1)}, bf16[256,2048]{1,0:T(8,128)(2,1)S(1)}, u32[]{:S(2)}, u32[]{:S(2)}) collective-permute-start(bf16[256,2048]{1,0:T(8,128)(2,1)} %get-tuple-element.122.own), channel_id=1, source_target_pairs={{0,1},{1,0},{2,3},{3,2},{4,5},{5,4},{6,7},{7,6},{8,9},{9,8},{10,11... | collective-permute-start | bytes 3145736 | tf_op jit(solution)/shard_map/ppermute | solution.py:59
  590.4 23.1 %collective-permute-start.33 = (bf16[256,2048]{1,0:T(8,128)(2,1)}, bf16[256,2048]{1,0:T(8,128)(2,1)S(1)}, u32[]{:S(2)}, u32[]{:S(2)}) collective-permute-start(bf16[256,2048]{1,0:T(8,128)(2,1)} %get-tuple-element.122.own), channel_id=1, source_target_pairs={{0,2},{2,0},{1,3},{3,1},{4,6},{6,4},{5,7},{7,5},{8,10},{10,8},{9,1... | collective-permute-start | bytes 3145736 | tf_op jit(solution)/shard_map/ppermute | solution.py:63
  593.5 27.8 %collective-permute-start.37 = (bf16[256,2048]{1,0:T(8,128)(2,1)S(1)}, bf16[256,2048]{1,0:T(8,128)(2,1)S(1)}, u32[]{:S(2)}, u32[]{:S(2)}) collective-permute-start(bf16[256,2048]{1,0:T(8,128)(2,1)S(1)} %constant_dynamic-slice_fusion.1), channel_id=1, source_target_pairs={{0,4},{4,0},{1,5},{5,1},{2,6},{6,2},{3,7},{7,3},{8,12},{12,8},{9,1... | collective-permute-start | bytes 3145736 | tf_op jit(solution)/shard_map/ppermute | solution.py:67
  593.6 26.2 %collective-permute-start.38 = (bf16[256,1024]{1,0:T(8,128)(2,1)S(1)}, bf16[256,1024]{1,0:T(8,128)(2,1)S(1)}, u32[]{:S(2)}, u32[]{:S(2)}) collective-permute-start(bf16[256,1024]{1,0:T(8,128)(2,1)S(1)} %constant_dynamic-slice_fusion), channel_id=1, source_target_pairs={{0,4},{4,0},{1,5},{5,1},{2,6},{6,2},{3,7},{7,3},{8,12},{12,8},{9,1... | collective-permute-start | bytes 1572872 | tf_op jit(solution)/shard_map/ppermute | solution.py:67
  611.4 19.3 %collective-permute-start.36 = (bf16[256,1024]{1,0:T(8,128)(2,1)S(1)}, bf16[256,1024]{1,0:T(8,128)(2,1)S(1)}, u32[]{:S(2)}, u32[]{:S(2)}) collective-permute-start(bf16[256,1024]{1,0:T(8,128)(2,1)S(1)} %slice.171), channel_id=1, source_target_pairs={{0,2},{2,0},{1,3},{3,1},{4,6},{6,4},{5,7},{7,5},{8,10},{10,8},{9,1... | collective-permute-start | bytes 1572872 | tf_op jit(solution)/shard_map/ppermute | solution.py:63
  613.6 18.0 %collective-permute-start.34 = (bf16[256,1024]{1,0:T(8,128)(2,1)S(1)}, bf16[256,1024]{1,0:T(8,128)(2,1)S(1)}, u32[]{:S(2)}, u32[]{:S(2)}) collective-permute-start(bf16[256,1024]{1,0:T(8,128)(2,1)S(1)} %slice.170), channel_id=1, source_target_pairs={{0,1},{1,0},{2,3},{3,2},{4,5},{5,4},{6,7},{7,6},{8,9},{9,8},{10,11... | collective-permute-start | bytes 1572872 | tf_op jit(solution)/shard_map/ppermute | solution.py:59
  (84 other events, 616.4 us)
Sparse Core Ops, SparseCore 0:
  21.8 64.8 all-gather.3
  88.9 148.2 all-gather.5
  239.4 78.9 all-gather.7
  320.5 75.2 reduce-scatter.3
  407.0 141.7 reduce-scatter.7
  564.7 68.3 reduce-scatter.5

commit v6 on v5

--- a/solution.py
+++ b/solution.py
@@ -964,7 +964,9 @@
     h1_pieces[-1], layer_far = tie(h1_pieces[-1], layer_far)
     layer_out = join_rows((layer_block, *layer_near, *layer_far), False)
     h1_near = scatter_near(h1_pieces)
-    h1_near, layer_out, attn_grads = tie(h1_near, layer_out, attn_grads)
+    if square():
+        first, attn_grads = tie(h1_near[0], attn_grads)
+        *h1_near, layer_out = tie(first, h1_near[1], layer_out)
     attn_out = reduce_dp(attn_grads)
     h1_far = scatter_far(scatter_middle(h1_pieces, h1_near))
     _, grad_block = rows_backward(h1_pieces, h1_near, h1_far, None, x_rel, g1, g_attn)

time: 662 us -> 690 us (1.042)
  waiting for transfers between devices: 260 us -> 295 us
    ppermute x16, waiting for transfers between devices: 77.4 us -> 101 us  [send_y(): return lax.ppermute(v, 'mp', OVER_Y)]
    ppermute x16, waiting for transfers between devices: 78.7 us -> 90.5 us  [send_x(): return lax.ppermute(v, 'mp', OVER_X)]
    unnamed x144 -> x136, local copies, waits for them, and re-layouts: 44.1 us -> 39.4 us
  transfers between devices with their start and end apart: 47 -> 47, of which waited for: 25 -> 28; matrix products, arithmetic and copies ran while one was open for 9% -> 9% of each run, Pallas kernels for 33% -> 32%
where the time goes in v6:
time: 690 us; the launch traced here: 684 us
  waiting for transfers between devices  295 us (43%)
  Pallas kernels  219 us (32%)
  local copies, waits for them, and re-layouts  50.5 us (7%)
  starting transfers between devices  44 us (6%)
  other arithmetic  34.2 us (5%)
  between operations  15.8 us (2%)
  matrix products  14 us (2%)
  blocking collectives  12.4 us (2%)
    ppermute x16, waiting for transfers between devices, send_y(): return lax.ppermute(v, 'mp', OVER_Y)  101 us
    ppermute x16, waiting for transfers between devices, send_x(): return lax.ppermute(v, 'mp', OVER_X)  90.5 us
    all_gather x2, waiting for transfers between devices, gather_z(): return lax.all_gather(block, 'z', axis=0, tiled=True)  71.2 us
    pallas_call x6, Pallas kernels, transposed_product(): pl.pallas_call(functools.partial(transposed_product_kernel, groups, add i...  65.2 us
    unnamed x136, local copies, waits for them, and re-layouts  39.4 us
    pallas_call x2, Pallas kernels, rows_product(): pl.pallas_call(rows_product_kernel, name='rows_product', grid=(steps,), i...  28.7 us
    pallas_call x1, Pallas kernels, ffn_forward(): pl.pallas_call(ffn_forward_kernel, name='ffn_forward', grid=(2, ff // tn)...  26.2 us
    all_gather x1, waiting for transfers between devices, gather_dp(): return lax.all_gather(block, DP, axis=0, tiled=True)  22.5 us
  transfers between devices with their start and end apart: 47, of which 28 were waited for; matrix products, arithmetic and copies ran while one was open for 9% of the time, Pallas kernels for 32%

profile of v6, /device:TPU:0, one launch (start us, length us, event | category | flops | bytes accessed | tf_op | source)
XLA Modules:
  0.0 684.3 jit_solution(16229453509437572794)
XLA Ops:
  44.0 12.4 %all_gather.12 = bf16[2,2048]{1,0:T(2,128)(2,1)S(1)} all-gather(bf16[2,256]{1,0:T(2,128)(2,1)S(1)} %pad_maximum_fusion.4), channel_id=1, replica_groups=mesh['z'=4,'core'=2,'mp'=4] {'z','core'}, dimensions={1}, use_global_device_ids=true | all-gather | bytes 9216 | tf_op jit(solution)/shard_map/all_gather | solution.py:909
  64.1 22.5 %all-gather.4.cloned.1.call-done.right_ref = bf16[2048,1536]{1,0:T(8,128)(2,1)} async-done(((bf16[256,1536]{1,0:T(8,128)(2,1)}), bf16[2048,1536]{1,0:T(8,128)(2,1)}) %all-gather.4.cloned.1.call-update) | async-done | bytes 6291472 | tf_op jit(solution)/shard_map/all_gather | solution.py:701
  86.7 9.0 %column_product.2.q_ref.k_ref.v_ref = f32[1024,1024]{1,0:T(8,128)} custom-call(bf16[1024,2048]{1,0:T(8,128)(2,1)} %fusion.2.left_ref.h_ref, bf16[2048,1536]{1,0:T(8,128)(2,1)} %all-gather.4.cloned.1.call-done.right_ref), custom_call_target="tpu_custom_call" | custom-call | flops 4294967296 | bytes 12582912 | tf_op jit(solution)/shard_map/column_product/pallas_call | solution.py:100
  95.7 8.2 %attention_forward.1.left_ref.context_ref = bf16[1024,512]{1,0:T(8,128)(2,1)} custom-call(s32[4]{0:T(128)} %fusion.14.order_ref, s32[1]{0:T(128)S(6)} %copy.65.len_ref, f32[1024,1024]{1,0:T(8,128)} %column_product.2.q_ref.k_ref.v_ref, f32[1024,1024]{1,0:T(8,128)} %column_product.2.q_ref.k_ref.v_ref, f32[1024,1024]{1,0:T(8,128)} %column_product.2.q_ref.k_ref.v_ref, ...), custom_call_target="tpu_custom_call" | custom-call | flops 1610612736 | bytes 8388608 | tf_op jit(solution)/shard_map/attention_forward/pallas_call | solution.py:536
  103.9 7.1 %transposed_product.6 = (f32[256,1024]{1,0:T(8,128)}, bf16[256,1024]{1,0:T(8,128)(2,1)}, bf16[512,1024]{1,0:T(8,128)(2,1)}, f32[256,1024]{1,0:T(8,128)}, bf16[25...) custom-call(bf16[1024,512]{1,0:T(8,128)(2,1)} %attention_forward.1.left_ref.context_ref, ...), custom_call_target="tpu_custom_call" | custom-call | flops 2147483648 | bytes 7340032 | tf_op jit(solution)/shard_map/transposed_product/pallas_call | solution.py:151
  114.1 22.5 %collective-permute-done = bf16[512,1024]{1,0:T(8,128)(2,1)S(1)} collective-permute-done((bf16[512,1024]{1,0:T(8,128)(2,1)}, bf16[512,1024]{1,0:T(8,128)(2,1)S(1)}, u32[]{:S(2)}, u32[]{:S(2)}) %collective-permute-start) | collective-permute-done | bytes 1048608 | tf_op jit(solution)/shard_map/ppermute | solution.py:59
  142.3 9.0 %collective-permute-done.1 = bf16[256,1024]{1,0:T(8,128)(2,1)S(1)} collective-permute-done((bf16[256,1024]{1,0:T(8,128)(2,1)S(1)}, bf16[256,1024]{1,0:T(8,128)(2,1)S(1)}, u32[]{:S(2)}, u32[]{:S(2)}) %collective-permute-start.1) | collective-permute-done | bytes 524320 | tf_op jit(solution)/shard_map/ppermute | solution.py:63
  158.1 21.5 %collective-permute-done.5.over_y = bf16[256,2048]{1,0:T(8,128)(2,1)S(1)} collective-permute-done((bf16[256,2048]{1,0:T(8,128)(2,1)S(1)}, bf16[256,2048]{1,0:T(8,128)(2,1)S(1)}, u32[]{:S(2)}, u32[]{:S(2)}) %collective-permute-start.5) | collective-permute-done | bytes 1048608 | tf_op jit(solution)/shard_map/ppermute | solution.py:63
  182.1 9.0 %collective-permute-done.6.diag_a = bf16[256,1024]{1,0:T(8,128)(2,1)S(1)} collective-permute-done((bf16[256,1024]{1,0:T(8,128)(2,1)S(1)}, bf16[256,1024]{1,0:T(8,128)(2,1)S(1)}, u32[]{:S(2)}, u32[]{:S(2)}) %collective-permute-start.6) | collective-permute-done | bytes 524320 | tf_op jit(solution)/shard_map/ppermute | solution.py:59
  206.8 30.4 %all-gather.6.cloned.1.call-done.g_ref.u_ref.right_ref = bf16[2048,2048]{1,0:T(8,128)(2,1)} async-done(((bf16[512,2048]{1,0:T(8,128)(2,1)}), bf16[2048,2048]{1,0:T(8,128)(2,1)}) %all-gather.6.cloned.1.call-update) | async-done | bytes 8388624 | tf_op jit(solution)/shard_map/all_gather | solution.py:709
  237.2 26.2 %ffn_forward.1 = (bf16[2048,1024]{1,0:T(8,128)(2,1)}, bf16[2,2048,1024]{2,1,0:T(8,128)(2,1)}) custom-call(bf16[1024,2048]{1,0:T(8,128)(2,1)} %assemble.3.mine_ref, bf16[1024,2048]{1,0:T(8,128)(2,1)} %collective-permute-done.8.away_ref, bf16[2048,2048]{1,0:T(8,128)(2,1)} %all-gather.6.cloned.1.call-done.g_ref.u_ref.right_ref, ...), custom_call_target="tpu_custom_call" | custom-call | flops 17179869184 | bytes 29360128 | tf_op jit(solution)/shard_map/ffn_forward/pallas_call | solution.py:780
  263.4 14.0 %convolution_convert_fusion.refs_0_ = bf16[2048,1024]{1,0:T(8,128)(2,1)} fusion(bf16[2048,2048]{1,0:T(8,128)(2,1)} %constant_dynamic-update-slice_fusion.grad_ref, bf16[2048,1024]{1,0:T(8,128)(2,1)} %get-tuple-element.80.left_ref), kind=kOutput, calls=%fused_computation.5 | convolution fusion | flops 8592031744 | bytes 16777216 | tf_op jit(solution)/shard_map/dot_general | solution.py:49
  277.6 40.8 %all-gather.8.cloned.1.call-done.right_ref.d_ref = bf16[2048,1024]{1,0:T(8,128)(2,1)} async-done(((bf16[512,1024]{1,0:T(8,128)(2,1)}), bf16[2048,1024]{1,0:T(8,128)(2,1)}) %all-gather.8.cloned.1.call-update) | async-done | bytes 4194320 | tf_op jit(solution)/shard_map/all_gather | solution.py:709
  318.4 8.8 %transposed_product.7.earlier_ref = bf16[1024,2048]{1,0:T(8,128)(2,1)} custom-call(bf16[2048,1024]{1,0:T(8,128)(2,1)} %get-tuple-element.80.left_ref, bf16[2048,1024]{1,0:T(8,128)(2,1)} %all-gather.8.cloned.1.call-done.right_ref.d_ref, bf16[2048,1024]{1,0:T(8,128)(2,1)} %convolution_convert_fusion.refs_0_), custom_call_target="tpu_custom_call" | custom-call | flops 4294967296 | bytes 10485760 | tf_op jit(solution)/shard_map/transposed_product/pallas_call | solution.py:151
  327.2 18.0 %ffn_backward.1.refs_1_.right_mine_ref.right_away_ref.left_ref = bf16[2,2048,1024]{2,1,0:T(8,128)(2,1)} custom-call(bf16[2048,2048]{1,0:T(8,128)(2,1)} %constant_dynamic-update-slice_fusion.grad_ref, bf16[2048,1024]{1,0:T(8,128)(2,1)} %all-gather.8.cloned.1.call-done.right_ref.d_ref, bf16[2,2048,1024]{2,1,0:T(8,128)(2,1)} %get-tuple-element.82.factor_ref, ...), custom_call_target="tpu_custom_call" | custom-call | flops 8589934592 | bytes 29360128 | tf_op jit(solution)/shard_map/ffn_backward/pallas_call | solution.py:856
  347.2 10.1 %transposed_product.8 = (f32[256,1024]{1,0:T(8,128)}, bf16[256,1024]{1,0:T(8,128)(2,1)}, bf16[512,1024]{1,0:T(8,128)(2,1)}, f32[256,1024]{1,0:T(8,128)}, bf16[25...) custom-call(bf16[2048,1024]{1,0:T(8,128)(2,1)} %get-tuple-element.80.left_ref, ...), custom_call_target="tpu_custom_call" | custom-call | flops 4294967296 | bytes 10485760 | tf_op jit(solution)/shard_map/transposed_product/pallas_call | solution.py:151
  360.2 14.3 %rows_product.2.refs_0_ = bf16[2048,2048]{1,0:T(8,128)(2,1)} custom-call(bf16[1024,2048]{1,0:T(8,128)(2,1)} %assemble.3.mine_ref, bf16[1024,2048]{1,0:T(8,128)(2,1)} %collective-permute-done.8.away_ref, bf16[2,2048,1024]{2,1,0:T(8,128)(2,1)} %ffn_backward.1.refs_1_.right_mine_ref.right_away_ref.left_ref, ...), custom_call_target="tpu_custom_call" | custom-call | flops 8589934592 | bytes 16777216 | tf_op jit(solution)/shard_map/rows_product/pallas_call | solution.py:823
  374.5 13.9 %transposed_product.9.refs_1_ = bf16[1024,2048]{1,0:T(8,128)(2,1)} custom-call(bf16[2,2048,1024]{2,1,0:T(8,128)(2,1)} %ffn_backward.1.refs_1_.right_mine_ref.right_away_ref.left_ref, bf16[2048,2048]{1,0:T(8,128)(2,1)} %all-gather.6.cloned.1.call-done.g_ref.u_ref.right_ref, bf16[2048,2048]{1,0:T(8,128)(2,1)} %rows_product.2.refs_0_), custom_call_target="tpu_custom_call" | custom-call | flops 8589934592 | bytes 16777216 | tf_op jit(solution)/shard_map/transposed_product/pallas_call | solution.py:151
  392.5 14.4 %rows_product.3.refs_0_ = bf16[2048,2048]{1,0:T(8,128)(2,1)} custom-call(bf16[1024,2048]{1,0:T(8,128)(2,1)} %assemble.3.mine_ref, bf16[1024,2048]{1,0:T(8,128)(2,1)} %collective-permute-done.8.away_ref, bf16[2,2048,1024]{2,1,0:T(8,128)(2,1)} %ffn_backward.1.refs_1_.right_mine_ref.right_away_ref.left_ref, ...), custom_call_target="tpu_custom_call", output_to_operand_aliasing={{}: (4, {})} | custom-call | flops 8589934592 | bytes 16777216 | tf_op jit(solution)/shard_map/rows_product/pallas_call | solution.py:823
  409.0 15.2 %transposed_product.10 = (f32[256,1024]{1,0:T(8,128)}, bf16[256,1024]{1,0:T(8,128)(2,1)}, bf16[512,1024]{1,0:T(8,128)(2,1)}, f32[256,1024]{1,0:T(8,128)}, bf16[2...) custom-call(bf16[2,2048,1024]{2,1,0:T(8,128)(2,1)} %ffn_backward.1.refs_1_.right_mine_ref.right_away_ref.left_ref, ...), custom_call_target="tpu_custom_call" | custom-call | flops 8589934592 | bytes 16777216 | tf_op jit(solution)/shard_map/transposed_product/pallas_call | solution.py:151
  430.2 20.7 %collective-permute-done.18.refs_3_ = bf16[512,1024]{1,0:T(8,128)(2,1)S(1)} collective-permute-done((bf16[512,1024]{1,0:T(8,128)(2,1)S(1)}, bf16[512,1024]{1,0:T(8,128)(2,1)S(1)}, u32[]{:S(2)}, u32[]{:S(2)}) %collective-permute-start.18) | collective-permute-done | bytes 1048608 | tf_op jit(solution)/shard_map/ppermute | solution.py:63
  455.4 9.3 %collective-permute-done.20.refs_5_ = bf16[256,1024]{1,0:T(8,128)(2,1)S(1)} collective-permute-done((bf16[256,1024]{1,0:T(8,128)(2,1)S(1)}, bf16[256,1024]{1,0:T(8,128)(2,1)S(1)}, u32[]{:S(2)}, u32[]{:S(2)}) %collective-permute-start.20) | collective-permute-done | bytes 524320 | tf_op jit(solution)/shard_map/ppermute | solution.py:59
  472.8 18.9 %collective-permute-done.22.over_y = bf16[256,2048]{1,0:T(8,128)(2,1)S(1)} collective-permute-done((bf16[256,2048]{1,0:T(8,128)(2,1)S(1)}, bf16[256,2048]{1,0:T(8,128)(2,1)S(1)}, u32[]{:S(2)}, u32[]{:S(2)}) %collective-permute-start.22) | collective-permute-done | bytes 1048608 | tf_op jit(solution)/shard_map/ppermute | solution.py:63
  495.2 8.6 %collective-permute-done.23.diag_a = bf16[256,1024]{1,0:T(8,128)(2,1)S(1)} collective-permute-done((bf16[256,1024]{1,0:T(8,128)(2,1)S(1)}, bf16[256,1024]{1,0:T(8,128)(2,1)S(1)}, u32[]{:S(2)}, u32[]{:S(2)}) %collective-permute-start.23) | collective-permute-done | bytes 524320 | tf_op jit(solution)/shard_map/ppermute | solution.py:59
  513.8 12.8 %attention_backward.1.left_ref.d_qkv_ref = bf16[1024,1024]{1,0:T(8,128)(2,1)} custom-call(s32[4]{0:T(128)} %fusion.14.order_ref, s32[1]{0:T(128)S(6)} %copy.65.len_ref, f32[1024,1024]{1,0:T(8,128)} %column_product.2.q_ref.k_ref.v_ref, f32[1024,1024]{1,0:T(8,128)} %column_product.2.q_ref.k_ref.v_ref, f32[1024,1024]{1,0:T(8,128)} %column_product.2.q_ref.k_ref.v_ref, ...), custom_call_target="tpu_custom_call" | custom-call | flops 3758096384 | bytes 8388608 | tf_op jit(solution)/shard_map/attention_backward/pallas_call | solution.py:559
  529.1 10.1 %transposed_product.11 = (f32[256,1024]{1,0:T(8,128)}, bf16[256,1024]{1,0:T(8,128)(2,1)}, bf16[512,1024]{1,0:T(8,128)(2,1)}, f32[256,1024]{1,0:T(8,128)}, bf16[2...) custom-call(bf16[1024,1024]{1,0:T(8,128)(2,1)} %attention_backward.1.left_ref.d_qkv_ref, ...), custom_call_target="tpu_custom_call" | custom-call | flops 4294967296 | bytes 10485760 | tf_op jit(solution)/shard_map/transposed_product/pallas_call | solution.py:151
  540.0 11.3 %attention_products.1 = bf16[2048,1536]{1,0:T(8,128)(2,1)} custom-call(bf16[1024,2048]{1,0:T(8,128)(2,1)} %copy-done.2, bf16[1024,512]{1,0:T(8,128)(2,1)} %attention_forward.1.left_ref.context_ref, bf16[1024,2048]{1,0:T(8,128)(2,1)} %fusion.2.left_ref.h_ref, bf16[1024,1024]{1,0:T(8,128)(2,1)} %attention_backward.1.left_ref.d_qkv_ref, ...), custom_call_target="tpu_custom_call" | custom-call | flops 6442450944 | bytes 17825792 | tf_op jit(solution)/shard_map/attention_products/pallas_call | solution.py:592
  551.4 9.7 %collective-permute-done.27.refs_2_ = bf16[512,1024]{1,0:T(8,128)(2,1)S(1)} collective-permute-done((bf16[512,1024]{1,0:T(8,128)(2,1)}, bf16[512,1024]{1,0:T(8,128)(2,1)S(1)}, u32[]{:S(2)}, u32[]{:S(2)}) %collective-permute-start.27) | collective-permute-done | bytes 1048608 | tf_op jit(solution)/shard_map/ppermute | solution.py:59
  564.0 9.6 %collective-permute-done.29.diag_b = bf16[256,1024]{1,0:T(8,128)(2,1)S(1)} collective-permute-done((bf16[256,1024]{1,0:T(8,128)(2,1)S(1)}, bf16[256,1024]{1,0:T(8,128)(2,1)S(1)}, u32[]{:S(2)}, u32[]{:S(2)}) %collective-permute-start.29) | collective-permute-done | bytes 524320 | tf_op jit(solution)/shard_map/ppermute | solution.py:63
  579.9 14.3 %collective-permute-done.30.refs_3_ = bf16[512,1024]{1,0:T(8,128)(2,1)S(1)} collective-permute-done((bf16[512,1024]{1,0:T(8,128)(2,1)}, bf16[512,1024]{1,0:T(8,128)(2,1)S(1)}, u32[]{:S(2)}, u32[]{:S(2)}) %collective-permute-start.30) | collective-permute-done | bytes 1048608 | tf_op jit(solution)/shard_map/ppermute | solution.py:63
  597.6 7.0 %collective-permute-done.32.refs_5_ = bf16[256,1024]{1,0:T(8,128)(2,1)S(1)} collective-permute-done((bf16[256,1024]{1,0:T(8,128)(2,1)}, bf16[256,1024]{1,0:T(8,128)(2,1)S(1)}, u32[]{:S(2)}, u32[]{:S(2)}) %collective-permute-start.32) | collective-permute-done | bytes 524320 | tf_op jit(solution)/shard_map/ppermute | solution.py:59
  622.0 18.1 %collective-permute-done.35.over_x = bf16[256,2048]{1,0:T(8,128)(2,1)S(1)} collective-permute-done((bf16[256,2048]{1,0:T(8,128)(2,1)}, bf16[256,2048]{1,0:T(8,128)(2,1)S(1)}, u32[]{:S(2)}, u32[]{:S(2)}) %collective-permute-start.35) | collective-permute-done | bytes 1048608 | tf_op jit(solution)/shard_map/ppermute | solution.py:59
  (296 shorter events, 191.1 us)
Async XLA Ops:
  14.1 72.5 %all-gather.4.cloned.1.call-start = ((), (), s32[]{:S(2)}) async-start(), calls=%async_computation.5 | async-start | bytes 7077888 | tf_op jit(solution)/shard_map/all_gather | solution.py:701
  21.7 215.5 %all-gather.6.cloned.1.call-start = ((), (), s32[]{:S(2)}) async-start(), calls=%async_computation.6 | async-start | bytes 10485760 | tf_op jit(solution)/shard_map/all_gather | solution.py:709
  35.4 283.0 %all-gather.8.cloned.1.call-start = ((), (), s32[]{:S(2)}) async-start(), calls=%async_computation.7 | async-start | bytes 5242880 | tf_op jit(solution)/shard_map/all_gather | solution.py:709
  111.0 25.6 %collective-permute-start = (bf16[512,1024]{1,0:T(8,128)(2,1)}, bf16[512,1024]{1,0:T(8,128)(2,1)S(1)}, u32[]{:S(2)}, u32[]{:S(2)}) collective-permute-start(bf16[512,1024]{1,0:T(8,128)(2,1)} %get-tuple-element.75), channel_id=1, source_target_pairs={{0,1},{1,0},{2,3},{3,2},{4,5},{5,4},{6,7},{7,6},{8,9},{9,8},{10,11... | collective-permute-start | bytes 3145736 | tf_op jit(solution)/shard_map/ppermute | solution.py:59
  112.6 26.9 %collective-permute-start.2 = (bf16[512,1024]{1,0:T(8,128)(2,1)}, bf16[512,1024]{1,0:T(8,128)(2,1)S(1)}, u32[]{:S(2)}, u32[]{:S(2)}) collective-permute-start(bf16[512,1024]{1,0:T(8,128)(2,1)} %get-tuple-element.78), channel_id=1, source_target_pairs={{0,2},{2,0},{1,3},{3,1},{4,6},{6,4},{5,7},{7,5},{8,10},{10,8},{9,1... | collective-permute-start | bytes 3145736 | tf_op jit(solution)/shard_map/ppermute | solution.py:63
  155.9 23.6 %collective-permute-start.5 = (bf16[256,2048]{1,0:T(8,128)(2,1)S(1)}, bf16[256,2048]{1,0:T(8,128)(2,1)S(1)}, u32[]{:S(2)}, u32[]{:S(2)}) collective-permute-start(bf16[256,2048]{1,0:T(8,128)(2,1)S(1)} %multiply_convert_fusion.own), channel_id=1, source_target_pairs={{0,2},{2,0},{1,3},{3,1},{4,6},{6,4},{5,7},{7,5},{8,10},{10,8},{9,1... | collective-permute-start | bytes 3145736 | tf_op jit(solution)/shard_map/ppermute | solution.py:63
  156.6 24.6 %collective-permute-start.4 = (bf16[256,2048]{1,0:T(8,128)(2,1)S(1)}, bf16[256,2048]{1,0:T(8,128)(2,1)S(1)}, u32[]{:S(2)}, u32[]{:S(2)}) collective-permute-start(bf16[256,2048]{1,0:T(8,128)(2,1)S(1)} %multiply_convert_fusion.own), channel_id=1, source_target_pairs={{0,1},{1,0},{2,3},{3,2},{4,5},{5,4},{6,7},{7,6},{8,9},{9,8},{10,11... | collective-permute-start | bytes 3145736 | tf_op jit(solution)/shard_map/ppermute | solution.py:59
  182.1 19.9 %collective-permute-start.10 = (bf16[1024,2048]{1,0:T(8,128)(2,1)}, bf16[1024,2048]{1,0:T(8,128)(2,1)}, u32[]{:S(2)}, u32[]{:S(2)}) collective-permute-start(bf16[1024,2048]{1,0:T(8,128)(2,1)} %get-tuple-element.81.refs_8_), channel_id=1, source_target_pairs={{0,4},{4,0},{1,5},{5,1},{2,6},{6,2},{3,7},{7,3},{8,12},{12,8},{9,1... | collective-permute-start | bytes 12582920 | tf_op jit(solution)/shard_map/ppermute | solution.py:67
  195.5 41.7 %collective-permute-start.8 = (bf16[1024,2048]{1,0:T(8,128)(2,1)}, bf16[1024,2048]{1,0:T(8,128)(2,1)}, u32[]{:S(2)}, u32[]{:S(2)}) collective-permute-start(bf16[1024,2048]{1,0:T(8,128)(2,1)} %assemble.3.mine_ref), channel_id=1, source_target_pairs={{0,4},{4,0},{1,5},{5,1},{2,6},{6,2},{3,7},{7,3},{8,12},{12,8},{9,1... | collective-permute-start | bytes 12582920 | tf_op jit(solution)/shard_map/ppermute | solution.py:67
  196.6 210.2 %reduce-scatter.4.cloned.1.call-start = ((), (), s32[]{:S(2)}) async-start(), calls=%async_computation.8 | async-start | bytes 5242880 | tf_op jit(solution)/shard_map/reduce_scatter | solution.py:713
  277.4 342.5 %reduce-scatter.8.cloned.1.call-start = ((), (), s32[]{:S(2)}) async-start(), calls=%async_computation.10 | async-start | bytes 10485760 | tf_op jit(solution)/shard_map/reduce_scatter | solution.py:713
  327.2 18.0 %collective-permute-start.11 = (bf16[1024,2048]{1,0:T(8,128)(2,1)}, bf16[1024,2048]{1,0:T(8,128)(2,1)S(1)}, u32[]{:S(2)}, u32[]{:S(2)}) collective-permute-start(bf16[1024,2048]{1,0:T(8,128)(2,1)} %transposed_product.7.earlier_ref), channel_id=1, source_target_pairs={{0,4},{4,0},{1,5},{5,1},{2,6},{6,2},{3,7},{7,3},{8,12},{12,8},{9,1... | collective-permute-start | bytes 12582920 | tf_op jit(solution)/shard_map/ppermute | solution.py:67
  357.3 31.2 %collective-permute-start.12 = (bf16[512,1024]{1,0:T(8,128)(2,1)}, bf16[512,1024]{1,0:T(8,128)(2,1)S(1)}, u32[]{:S(2)}, u32[]{:S(2)}) collective-permute-start(bf16[512,1024]{1,0:T(8,128)(2,1)} %get-tuple-element.84), channel_id=1, source_target_pairs={{0,1},{1,0},{2,3},{3,2},{4,5},{5,4},{6,7},{7,6},{8,9},{9,8},{10,11... | collective-permute-start | bytes 3145736 | tf_op jit(solution)/shard_map/ppermute | solution.py:59
  358.8 31.7 %collective-permute-start.13 = (bf16[512,1024]{1,0:T(8,128)(2,1)}, bf16[512,1024]{1,0:T(8,128)(2,1)S(1)}, u32[]{:S(2)}, u32[]{:S(2)}) collective-permute-start(bf16[512,1024]{1,0:T(8,128)(2,1)} %get-tuple-element.85.refs_0_), channel_id=1, source_target_pairs={{0,2},{2,0},{1,3},{3,1},{4,6},{6,4},{5,7},{7,5},{8,10},{10,8},{9,1... | collective-permute-start | bytes 3145736 | tf_op jit(solution)/shard_map/ppermute | solution.py:63
  406.9 254.4 %reduce-scatter.6.cloned.1.call-start = ((), (), s32[]{:S(2)}) async-start(), calls=%async_computation.9 | async-start | bytes 7077888 | tf_op jit(solution)/shard_map/reduce_scatter | solution.py:705
  407.1 17.1 %collective-permute-start.14 = (bf16[1024,2048]{1,0:T(8,128)(2,1)}, bf16[1024,2048]{1,0:T(8,128)(2,1)S(1)}, u32[]{:S(2)}, u32[]{:S(2)}) collective-permute-start(bf16[1024,2048]{1,0:T(8,128)(2,1)} %transposed_product.9.refs_1_), channel_id=1, source_target_pairs={{0,4},{4,0},{1,5},{5,1},{2,6},{6,2},{3,7},{7,3},{8,12},{12,8},{9,1... | collective-permute-start | bytes 12582920 | tf_op jit(solution)/shard_map/ppermute | solution.py:67
  407.9 18.8 %collective-permute-start.15 = (bf16[256,1024]{1,0:T(8,128)(2,1)S(1)}, bf16[256,1024]{1,0:T(8,128)(2,1)S(1)}, u32[]{:S(2)}, u32[]{:S(2)}) collective-permute-start(bf16[256,1024]{1,0:T(8,128)(2,1)S(1)} %copy-done.42), channel_id=1, source_target_pairs={{0,2},{2,0},{1,3},{3,1},{4,6},{6,4},{5,7},{7,5},{8,10},{10,8},{9,1... | collective-permute-start | bytes 1572872 | tf_op jit(solution)/shard_map/ppermute | solution.py:63
  408.4 18.2 %collective-permute-start.16 = (bf16[256,1024]{1,0:T(8,128)(2,1)S(1)}, bf16[256,1024]{1,0:T(8,128)(2,1)}, u32[]{:S(2)}, u32[]{:S(2)}) collective-permute-start(bf16[256,1024]{1,0:T(8,128)(2,1)S(1)} %copy-done.43), channel_id=1, source_target_pairs={{0,1},{1,0},{2,3},{3,2},{4,5},{5,4},{6,7},{7,6},{8,9},{9,8},{10,11... | collective-permute-start | bytes 1572872 | tf_op jit(solution)/shard_map/ppermute | solution.py:59
  426.7 24.2 %collective-permute-start.18 = (bf16[512,1024]{1,0:T(8,128)(2,1)S(1)}, bf16[512,1024]{1,0:T(8,128)(2,1)S(1)}, u32[]{:S(2)}, u32[]{:S(2)}) collective-permute-start(bf16[512,1024]{1,0:T(8,128)(2,1)S(1)} %fusion.6), channel_id=1, source_target_pairs={{0,2},{2,0},{1,3},{3,1},{4,6},{6,4},{5,7},{7,5},{8,10},{10,8},{9,1... | collective-permute-start | bytes 3145736 | tf_op jit(solution)/shard_map/ppermute | solution.py:63
  428.7 23.7 %collective-permute-start.17 = (bf16[512,1024]{1,0:T(8,128)(2,1)S(1)}, bf16[512,1024]{1,0:T(8,128)(2,1)S(1)}, u32[]{:S(2)}, u32[]{:S(2)}) collective-permute-start(bf16[512,1024]{1,0:T(8,128)(2,1)S(1)} %fusion.5), channel_id=1, source_target_pairs={{0,1},{1,0},{2,3},{3,2},{4,5},{5,4},{6,7},{7,6},{8,9},{9,8},{10,11... | collective-permute-start | bytes 3145736 | tf_op jit(solution)/shard_map/ppermute | solution.py:59
  469.5 22.2 %collective-permute-start.22 = (bf16[256,2048]{1,0:T(8,128)(2,1)S(1)}, bf16[256,2048]{1,0:T(8,128)(2,1)S(1)}, u32[]{:S(2)}, u32[]{:S(2)}) collective-permute-start(bf16[256,2048]{1,0:T(8,128)(2,1)S(1)} %get-tuple-element.101.own), channel_id=1, source_target_pairs={{0,2},{2,0},{1,3},{3,1},{4,6},{6,4},{5,7},{7,5},{8,10},{10,8},{9,1... | collective-permute-start | bytes 3145736 | tf_op jit(solution)/shard_map/ppermute | solution.py:63
  470.7 24.1 %collective-permute-start.21 = (bf16[256,2048]{1,0:T(8,128)(2,1)S(1)}, bf16[256,2048]{1,0:T(8,128)(2,1)S(1)}, u32[]{:S(2)}, u32[]{:S(2)}) collective-permute-start(bf16[256,2048]{1,0:T(8,128)(2,1)S(1)} %get-tuple-element.101.own), channel_id=1, source_target_pairs={{0,1},{1,0},{2,3},{3,2},{4,5},{5,4},{6,7},{7,6},{8,9},{9,8},{10,11... | collective-permute-start | bytes 3145736 | tf_op jit(solution)/shard_map/ppermute | solution.py:59
  507.0 22.1 %collective-permute-start.26 = (bf16[256,2048]{1,0:T(8,128)(2,1)S(1)}, bf16[256,2048]{1,0:T(8,128)(2,1)S(1)}, u32[]{:S(2)}, u32[]{:S(2)}) collective-permute-start(bf16[256,2048]{1,0:T(8,128)(2,1)S(1)} %fusion.4.own), channel_id=1, source_target_pairs={{0,2},{2,0},{1,3},{3,1},{4,6},{6,4},{5,7},{7,5},{8,10},{10,8},{9,1... | collective-permute-start | bytes 3145736 | tf_op jit(solution)/shard_map/ppermute | solution.py:63
  507.5 21.6 %collective-permute-start.25 = (bf16[256,2048]{1,0:T(8,128)(2,1)S(1)}, bf16[256,2048]{1,0:T(8,128)(2,1)S(1)}, u32[]{:S(2)}, u32[]{:S(2)}) collective-permute-start(bf16[256,2048]{1,0:T(8,128)(2,1)S(1)} %fusion.4.own), channel_id=1, source_target_pairs={{0,1},{1,0},{2,3},{3,2},{4,5},{5,4},{6,7},{7,6},{8,9},{9,8},{10,11... | collective-permute-start | bytes 3145736 | tf_op jit(solution)/shard_map/ppermute | solution.py:59
  539.2 21.8 %collective-permute-start.27 = (bf16[512,1024]{1,0:T(8,128)(2,1)}, bf16[512,1024]{1,0:T(8,128)(2,1)S(1)}, u32[]{:S(2)}, u32[]{:S(2)}) collective-permute-start(bf16[512,1024]{1,0:T(8,128)(2,1)} %get-tuple-element.105), channel_id=1, source_target_pairs={{0,1},{1,0},{2,3},{3,2},{4,5},{5,4},{6,7},{7,6},{8,9},{9,8},{10,11... | collective-permute-start | bytes 3145736 | tf_op jit(solution)/shard_map/ppermute | solution.py:59
  573.6 20.6 %collective-permute-start.30 = (bf16[512,1024]{1,0:T(8,128)(2,1)}, bf16[512,1024]{1,0:T(8,128)(2,1)S(1)}, u32[]{:S(2)}, u32[]{:S(2)}) collective-permute-start(bf16[512,1024]{1,0:T(8,128)(2,1)} %get-tuple-element.111), channel_id=1, source_target_pairs={{0,2},{2,0},{1,3},{3,1},{4,6},{6,4},{5,7},{7,5},{8,10},{10,8},{9,1... | collective-permute-start | bytes 3145736 | tf_op jit(solution)/shard_map/ppermute | solution.py:63
  617.5 22.6 %collective-permute-start.35 = (bf16[256,2048]{1,0:T(8,128)(2,1)}, bf16[256,2048]{1,0:T(8,128)(2,1)S(1)}, u32[]{:S(2)}, u32[]{:S(2)}) collective-permute-start(bf16[256,2048]{1,0:T(8,128)(2,1)} %get-tuple-element.124.own), channel_id=1, source_target_pairs={{0,1},{1,0},{2,3},{3,2},{4,5},{5,4},{6,7},{7,6},{8,9},{9,8},{10,11... | collective-permute-start | bytes 3145736 | tf_op jit(solution)/shard_map/ppermute | solution.py:59
  619.0 23.0 %collective-permute-start.33 = (bf16[256,2048]{1,0:T(8,128)(2,1)}, bf16[256,2048]{1,0:T(8,128)(2,1)S(1)}, u32[]{:S(2)}, u32[]{:S(2)}) collective-permute-start(bf16[256,2048]{1,0:T(8,128)(2,1)} %get-tuple-element.124.own), channel_id=1, source_target_pairs={{0,2},{2,0},{1,3},{3,1},{4,6},{6,4},{5,7},{7,5},{8,10},{10,8},{9,1... | collective-permute-start | bytes 3145736 | tf_op jit(solution)/shard_map/ppermute | solution.py:63
  621.2 29.0 %collective-permute-start.37 = (bf16[256,2048]{1,0:T(8,128)(2,1)S(1)}, bf16[256,2048]{1,0:T(8,128)(2,1)S(1)}, u32[]{:S(2)}, u32[]{:S(2)}) collective-permute-start(bf16[256,2048]{1,0:T(8,128)(2,1)S(1)} %constant_dynamic-slice_fusion.1), channel_id=1, source_target_pairs={{0,4},{4,0},{1,5},{5,1},{2,6},{6,2},{3,7},{7,3},{8,12},{12,8},{9,1... | collective-permute-start | bytes 3145736 | tf_op jit(solution)/shard_map/ppermute | solution.py:67
  621.3 27.3 %collective-permute-start.38 = (bf16[256,1024]{1,0:T(8,128)(2,1)S(1)}, bf16[256,1024]{1,0:T(8,128)(2,1)S(1)}, u32[]{:S(2)}, u32[]{:S(2)}) collective-permute-start(bf16[256,1024]{1,0:T(8,128)(2,1)S(1)} %constant_dynamic-slice_fusion), channel_id=1, source_target_pairs={{0,4},{4,0},{1,5},{5,1},{2,6},{6,2},{3,7},{7,3},{8,12},{12,8},{9,1... | collective-permute-start | bytes 1572872 | tf_op jit(solution)/shard_map/ppermute | solution.py:67
  640.1 19.4 %collective-permute-start.36 = (bf16[256,1024]{1,0:T(8,128)(2,1)S(1)}, bf16[256,1024]{1,0:T(8,128)(2,1)S(1)}, u32[]{:S(2)}, u32[]{:S(2)}) collective-permute-start(bf16[256,1024]{1,0:T(8,128)(2,1)S(1)} %slice.171), channel_id=1, source_target_pairs={{0,2},{2,0},{1,3},{3,1},{4,6},{6,4},{5,7},{7,5},{8,10},{10,8},{9,1... | collective-permute-start | bytes 1572872 | tf_op jit(solution)/shard_map/ppermute | solution.py:63
  642.0 18.3 %collective-permute-start.34 = (bf16[256,1024]{1,0:T(8,128)(2,1)S(1)}, bf16[256,1024]{1,0:T(8,128)(2,1)S(1)}, u32[]{:S(2)}, u32[]{:S(2)}) collective-permute-start(bf16[256,1024]{1,0:T(8,128)(2,1)S(1)} %slice.170), channel_id=1, source_target_pairs={{0,1},{1,0},{2,3},{3,2},{4,5},{5,4},{6,7},{7,6},{8,9},{9,8},{10,11... | collective-permute-start | bytes 1572872 | tf_op jit(solution)/shard_map/ppermute | solution.py:59
  (80 other events, 684.7 us)
Sparse Core Ops, SparseCore 0:
  21.8 64.8 all-gather.3
  88.8 148.3 all-gather.5
  239.4 78.9 all-gather.7
  320.5 75.2 reduce-scatter.3
  407.0 141.7 reduce-scatter.7
  561.2 68.3 reduce-scatter.5
